TPU v7x, 32 devices: a whole 2x2x4 slice. The times are simulated.
32 devices in a mesh: section: 4 (over x, core), bulk: 8 (over z, y).
Axes of the slice: x: 2, y: 2, z: 4, core: 2. Of those that a mesh axis runs over, the one named last changes fastest.
Arguments:
- activations: bfloat16 [4, 4, 2048, 256], P('section', None, 'bulk'), may hold values from -6 to 6
- weights: bfloat16 [4, 3, 256, 256], P('section'), may hold values from -0.109375 to 0.109375
- film_gain: float32 [4, 36, 256], P('section'), may hold values from 0.25 to 1.75
- film_shift: float32 [4, 36, 256], P('section'), may hold values from -3 to 3
- doa_bins: int32 [4], replicated, may hold values from 0 to 35
- cotangent: bfloat16 [4, 2048, 256], P(None, 'bulk'), may hold values from -6 to 6
Outputs:
- d_inputs: bfloat16 [4, 4, 2048, 256], P('section', None, 'bulk')
- d_weights: float32 [4, 3, 256, 256], P('section')
- d_gain: float32 [4, 36, 256], P('section')
- d_shift: float32 [4, 36, 256], P('section')
All inputs are finite; a program needn't handle non-finite values.
Results may differ from a plain program's by a relative error of at most 0.014.
Values may be sent and summed in bfloat16 or wider, within the bound.
No kernel may reach another device: no remote copies, remote signals or barrier semaphores. Data moves between devices by JAX's collectives and lax.ppermute only.
A program may use at most 64 MiB of HBM per device.

v0:
```python
import functools

import jax
import jax.numpy as jnp
from jax import lax
from jax.experimental import pallas as pl
from jax.experimental.pallas import tpu as pltpu
from jax.sharding import PartitionSpec as P


F32 = jnp.float32
BF16 = jnp.bfloat16
PARTS = 2


def cost(flops, moved, trans=0):
    return pl.CostEstimate(flops=flops, bytes_accessed=moved, transcendentals=trans)


def shifted(value, amount):
    rows = value.shape[0]
    return pltpu.roll(value, amount % rows, 0)


def copies(pairs, sems):
    started = []
    for index, (source, target) in enumerate(pairs):
        copy = pltpu.make_async_copy(source, target, sems.at[index])
        copy.start()
        started.append(copy)
    return started


def edge_kernel(x_ref, cot_ref, near_ref, far_ref, sems):
    rows = x_ref.shape[1]
    pad = near_ref.shape[2]
    odd = lax.axis_index("bulk") % 2
    last = rows - pad
    near = pl.multiple_of((1 - odd) * last, pad)
    far = pl.multiple_of(odd * last, pad)
    pairs = []
    for index, ref in enumerate((x_ref, cot_ref)):
        pairs.append((ref.at[:, pl.ds(near, pad), :], near_ref.at[index]))
        pairs.append((ref.at[:, pl.ds(far, pad), :], far_ref.at[index]))
    for copy in copies(pairs, sems):
        copy.wait()


def slopes(filmed):
    sig = 0.5 * jnp.tanh(0.5 * filmed) + 0.5
    return sig * (1.0 + filmed * (1.0 - sig))


def taps(value, w_ref):
    wide = value.astype(F32)
    pre = jnp.dot(shifted(wide, 1).astype(BF16), w_ref[0], preferred_element_type=F32)
    pre = pre + jnp.dot(value, w_ref[1], preferred_element_type=F32)
    return pre + jnp.dot(shifted(wide, -1).astype(BF16), w_ref[2], preferred_element_type=F32)


def forward_kernel(bins, x_in, cot_in, w_in, gain_in, shift_in, *refs):
    x_ref, cot_ref, w_ref, gain_ref, shift_ref, slope_ref, pre_ref, sems = refs
    micro = x_ref.shape[0]
    pairs = [(w_in, w_ref), (x_in, x_ref)]
    for m in range(micro):
        pairs.append((gain_in.at[bins[m]], gain_ref.at[m]))
        pairs.append((shift_in.at[bins[m]], shift_ref.at[m]))
    started = copies(pairs + [(cot_in, cot_ref)], sems)
    for copy in started[:-1]:
        copy.wait()
    for m in range(micro):
        pre = taps(x_ref[m], w_ref)
        slope_ref[m] = slopes(pre * gain_ref[m] + shift_ref[m])
        pre_ref[m] = pre
    started[-1].wait()


def rim_kernel(near_ref, far_ref, x_ref, w_ref, gain_ref, shift_ref, *refs):
    slope_ref, pre_ref, g_ref, halo = refs
    micro, rows = x_ref.shape[:2]
    pad = near_ref.shape[2]
    odd = lax.axis_index("bulk") % 2

    @pl.when(odd == 1)
    def _():
        halo[0] = near_ref[...]
        halo[1] = far_ref[...]

    @pl.when(odd == 0)
    def _():
        halo[0] = far_ref[...]
        halo[1] = near_ref[...]

    parts = []
    for m in range(micro):
        parts += [halo[0, 0, m], x_ref[m, :pad], x_ref[m, rows - pad :], halo[1, 0, m]]
        g_ref[m, 0] = halo[0, 1, m]
        g_ref[m, 1] = halo[1, 1, m]
    pre = taps(jnp.concatenate(parts, axis=0), w_ref)
    for m in range(micro):
        for side in range(2):
            start = (2 * m + side) * 2 * pad
            here = pre[start : start + 2 * pad]
            pre_ref[m, side] = here
            slope_ref[m, side] = slopes(here * gain_ref[m] + shift_ref[m])


def with_rim(main, rim, m):
    pad = rim.shape[2] // 2
    rows = main.shape[1]
    parts = [rim[m, 0, : pad + 8], main[m, 8 : rows - 8], rim[m, 1, pad - 8 :]]
    return jnp.concatenate(parts, axis=0)


def times_trans(left, right):
    return lax.dot_general(left, right, (((1,), (1,)), ((), ())), preferred_element_type=F32)


def trans_times(left, right):
    return lax.dot_general(left, right, (((0,), (0,)), ((), ())), preferred_element_type=F32)


def backward(g, slope, gain_row, w_ref):
    grad_film = g * slope
    grad_pre = (grad_film * gain_row).astype(BF16)
    wide = grad_pre.astype(F32)
    later = shifted(wide, -1).astype(BF16)
    earlier = shifted(wide, 1).astype(BF16)
    d_in = g + times_trans(later, w_ref[0]) + times_trans(grad_pre, w_ref[1])
    d_in = d_in + times_trans(earlier, w_ref[2])
    return grad_film, later, grad_pre, earlier, d_in.astype(BF16)


def top_gradient(cot_ref, rim_ref, m):
    return jnp.concatenate([rim_ref[m, 0], cot_ref[m], rim_ref[m, 1]], axis=0)


def relay_kernel(upper, slope_ref, slope_rim, w_ref, gain_ref, *refs):
    g_refs, d_ref = refs[:-1], refs[-1]

    @pl.when(lax.axis_index("section") == upper)
    def _():
        for m in range(slope_ref.shape[0]):
            g = top_gradient(*g_refs, m) if len(g_refs) == 2 else g_refs[0][m]
            slope = with_rim(slope_ref, slope_rim, m)
            d_ref[m] = backward(g.astype(F32), slope, gain_ref[m], w_ref)[-1]


def split_rows(rows):
    high = rows.astype(BF16).astype(F32)
    low = (rows - high).astype(BF16).astype(F32)
    return jnp.concatenate([high, low], axis=0).astype(BF16)


def joined_rows(pair):
    wide = pair.astype(F32)
    half = wide.shape[0] // 2
    return wide[:half] + wide[half:]


def last_kernel(hops, outer, *refs):
    slope_ref, slope_rim, pre_ref, pre_rim, x_ref, w_ref, gain_ref = refs[:7]
    cot_ref, g_rim = refs[7:9]
    got_refs = refs[9 : 9 + hops]
    d_ref = refs[9 + hops]
    own_refs = refs[10 + hops : 10 + hops + PARTS]
    send_refs = refs[10 + hops + PARTS : -3]
    g_now, total, sums = refs[-3:]
    micro, rows, channels = x_ref.shape
    pad = g_rim.shape[2]
    inner = slice(pad, pad + rows)
    section_id = lax.axis_index("section")
    mine = lax.axis_index("bulk") // 2

    @pl.when(section_id == hops)
    def _():
        for m in range(micro):
            g_now[m] = top_gradient(cot_ref, g_rim, m)

    for index in range(hops):

        @pl.when(section_id == hops - 1 - index)
        def _(index=index):
            g_now[...] = got_refs[index][...]

    for m in range(micro):
        g = g_now[m].astype(F32)
        slope = with_rim(slope_ref, slope_rim, m)
        parts = backward(g, slope, gain_ref[m], w_ref)
        d_ref[m] = parts[4][inner]
        for tap in range(3):
            where = slice(tap * channels, (tap + 1) * channels)
            term = trans_times(x_ref[m], parts[1 + tap][inner])
            total[where] = term if m == 0 else total[where] + term
        film_main = parts[0][inner]
        pre = with_rim(pre_ref, pre_rim, m)[inner]
        sums[m : m + 1] = jnp.sum(film_main * pre, axis=0, keepdims=True)
        sums[micro + m : micro + m + 1] = jnp.sum(film_main, axis=0, keepdims=True)
    rows_out = split_rows(sums[...])
    extra = rows_out.shape[0]
    chunk = own_refs[0].shape[0]
    parts_count = len(own_refs)
    for part in range(parts_count):
        for k in range(outer):
            start = pl.multiple_of(((mine ^ k) * parts_count + part) * chunk, 8)
            term = total[pl.ds(start, chunk), :]
            if k == 0:
                own_refs[part][...] = term
            else:
                ref = send_refs[part * (outer - 1) + k - 1]
                ref[ref.shape[0] - chunk :] = term.astype(BF16)
                if part == 0:
                    ref[:extra] = rows_out


def gather_kernel(outer, own_ref, mine_ref, *refs):
    got_refs = refs[: outer - 1]
    out_ref, held = refs[outer - 1 :]
    mine = lax.axis_index("bulk") // 2
    chunk = own_ref.shape[0]
    extra = out_ref.shape[0] - chunk
    acc = own_ref[...]
    for k in range(1, outer):
        acc = acc + got_refs[k - 1][extra:].astype(F32)
    out_ref[extra:] = acc.astype(BF16)
    if extra:
        held[mine] = joined_rows(mine_ref[:extra])
        for k in range(1, outer):
            held[mine ^ k] = joined_rows(got_refs[k - 1][:extra])
        rows = held[0]
        for index in range(1, outer):
            rows = rows + held[index]
        out_ref[:extra] = split_rows(rows)


def pair_kernel(a_ref, b_ref, *refs):
    out_ref = refs[-1]
    extra = a_ref.shape[0] - out_ref.shape[0]
    out_ref[...] = (a_ref[extra:].astype(F32) + b_ref[extra:].astype(F32)).astype(BF16)


def spread_kernel(micro, outer, bins, a_ref, b_ref, *refs):
    chunk_refs = refs[:-3]
    out_ref, gain_ref, shift_ref = refs[-3:]
    chunk = chunk_refs[0].shape[0]
    parts_count = len(chunk_refs) // outer
    mine = lax.axis_index("bulk") // 2
    for part in range(parts_count):
        for k in range(outer):
            start = pl.multiple_of(((mine ^ k) * parts_count + part) * chunk, 8)
            out_ref[pl.ds(start, chunk), :] = chunk_refs[part * outer + k][...].astype(F32)
    extra = 4 * micro
    rows = joined_rows(a_ref[:extra]) + joined_rows(b_ref[:extra])
    gain_ref[...] = jnp.zeros_like(gain_ref)
    shift_ref[...] = jnp.zeros_like(shift_ref)
    for m in range(micro):
        gain_ref[bins[m]] += rows[m : m + 1]
        shift_ref[bins[m]] += rows[micro + m : micro + m + 1]


def shape_of(shape, dtype):
    return jax.ShapeDtypeStruct(shape, dtype)


def call(kernel, outs, args, scalars=(), remote=(), scratch=(), flops=1, limit=4):
    vmem = pl.BlockSpec(memory_space=pltpu.VMEM)
    smem = pl.BlockSpec(memory_space=pltpu.SMEM)
    kept = pl.BlockSpec(memory_space=pltpu.HBM)
    several = isinstance(outs, (list, tuple))
    return pl.pallas_call(
        kernel,
        in_specs=[smem] * len(scalars) + [kept] * len(remote) + [vmem] * len(args),
        out_specs=[vmem] * len(outs) if several else vmem,
        out_shape=outs,
        scratch_shapes=scratch,
        compiler_params=pltpu.CompilerParams(vmem_limit_bytes=limit << 20),
        cost_estimate=cost(flops, 1 << 20),
    )(*scalars, *[pltpu.with_memory_space_constraint(v, pltpu.HBM) for v in remote], *args)


def step(activations, weights, film_gain, film_shift, doa_bins, cotangent):
    sections = lax.axis_size("section")
    bulk_count = lax.axis_size("bulk")
    outer = bulk_count // 2
    x = activations[0]
    w_set = weights[0]
    micro, rows, channels = x.shape
    bins_count = film_gain.shape[1]
    gain_table = film_gain.reshape(bins_count, 1, channels)
    shift_table = film_shift.reshape(bins_count, 1, channels)
    pad = 16 * -(-(sections + 1) // 16)
    wide = rows + 2 * pad

    edges = shape_of((2, micro, pad, channels), BF16)
    near, far = call(
        edge_kernel,
        [edges, edges],
        [],
        remote=[x, cotangent],
        scratch=[pltpu.SemaphoreType.DMA((4,))],
    )
    opposite = [(i, (i + 1 if i % 2 else i - 1) % bulk_count) for i in range(bulk_count)]
    far = lax.ppermute(far, "bulk", opposite)
    near = lax.ppermute(near, "bulk", [(i, i ^ 1) for i in range(bulk_count)])

    matmul = 2 * 3 * micro * wide * channels * channels
    wide_shape = (micro, wide, channels)
    rim_shape = (micro, 2, 2 * pad, channels)
    picked = shape_of((micro, 1, channels), F32)
    x, cot, w_set, gain_rows, shift_rows, slope, pre = call(
        forward_kernel,
        [shape_of(v.shape, v.dtype) for v in (x, cotangent, w_set)]
        + [picked, picked, shape_of(x.shape, F32), shape_of(x.shape, F32)],
        [],
        scalars=[doa_bins],
        remote=[x, cotangent, w_set, gain_table, shift_table],
        scratch=[pltpu.SemaphoreType.DMA((3 + 2 * micro,))],
        flops=matmul,
        limit=12,
    )
    slope_rim, pre_rim, g_rim = call(
        rim_kernel,
        [
            shape_of(rim_shape, F32),
            shape_of(rim_shape, F32),
            shape_of((micro, 2, pad, channels), BF16),
        ],
        [near, far, x, w_set, gain_rows, shift_rows],
        scratch=[pltpu.VMEM((2, 2, micro, pad, channels), BF16)],
        flops=matmul // 4,
        limit=8,
    )

    sources = []
    for hop in range(sections - 1):
        upper = sections - 1 - hop
        d_wide = call(
            functools.partial(relay_kernel, upper),
            shape_of(wide_shape, BF16),
            [slope, slope_rim, w_set, gain_rows] + (sources[-1:] if hop else [cot, g_rim]),
            flops=matmul,
            limit=8,
        )
        if upper % 2 and sections % 2 == 0:
            pairs = [(i, i ^ 1) for i in range(sections)]
        else:
            pairs = [(upper, upper - 1)]
        sources.append(lax.ppermute(d_wide, "section", pairs))

    chunk = 3 * channels // outer // PARTS
    extra = 4 * micro
    messages = [shape_of((chunk + (0 if part else extra), channels), BF16) for part in range(PARTS)]
    made = call(
        functools.partial(last_kernel, sections - 1, outer),
        [shape_of(x.shape, BF16)]
        + [shape_of((chunk, channels), F32)] * PARTS
        + [messages[part] for part in range(PARTS) for _ in range(outer - 1)],
        [slope, slope_rim, pre, pre_rim, x, w_set, gain_rows, cot, g_rim, *sources],
        scratch=[
            pltpu.VMEM(wide_shape, BF16),
            pltpu.VMEM((3 * channels, channels), F32),
            pltpu.VMEM((2 * micro, channels), F32),
        ],
        flops=2 * matmul,
        limit=16,
    )
    d_local = made[0]
    owns = made[1 : 1 + PARTS]

    def across(value, k):
        pairs = [(i, i ^ (2 * k)) for i in range(bulk_count)]
        return lax.ppermute(value, "bulk", pairs)

    swap = [(i, i ^ 1) for i in range(bulk_count)]
    order = [k for k in range(2, outer)] + [1]
    scattered = []
    for part in range(PARTS):
        sends = made[1 + PARTS + part * (outer - 1) :][: outer - 1]
        got = {k: across(sends[k - 1], k) for k in order}
        scattered.append((sends[0], got))
    summed = []
    for part in range(PARTS):
        first, got = scattered[part]
        partial_sum = call(
            functools.partial(gather_kernel, outer),
            messages[part],
            [owns[part], first] + [got[k] for k in range(1, outer)],
            scratch=[pltpu.VMEM((outer, 2 * micro, channels), F32)],
        )
        summed.append((partial_sum, lax.ppermute(partial_sum, "bulk", swap)))
    spread = []
    for part in range(PARTS):
        done = call(
            pair_kernel, shape_of((chunk, channels), BF16), list(summed[part]) + spread[-outer:][:1]
        )
        got = {k: across(done, k) for k in order}
        spread += [done] + [got[k] for k in range(1, outer)]
    table = shape_of((bins_count, 1, channels), F32)
    d_weights, d_gain, d_shift = call(
        functools.partial(spread_kernel, micro, outer),
        [shape_of((3 * channels, channels), F32), table, table],
        [*summed[0], *spread],
        scalars=[doa_bins],
    )
    return (
        d_local[None],
        d_weights.reshape(1, 3, channels, channels),
        d_gain.reshape(1, bins_count, channels),
        d_shift.reshape(1, bins_count, channels),
    )


def solution(mesh):
    return jax.shard_map(
        step,
        mesh=mesh,
        in_specs=(
            P("section", None, "bulk", None),
            P("section", None, None, None),
            P("section", None, None),
            P("section", None, None),
            P(),
            P(None, "bulk", None),
        ),
        out_specs=(
            P("section", None, "bulk", None),
            P("section", None, None, None),
            P("section", None, None),
            P("section", None, None),
        ),
        check_vma=False,
    )
```

profile of v0, /device:TPU:0, one launch (start us, length us, event | category | flops | bytes accessed | tf_op | source)
XLA Modules:
  0.0 59.5 jit_solution(1514176169545518580)
XLA Ops:
  0.6 0.9 %shard_map.94 = (bf16[2,4,16,256]{3,2,1,0:T(8,128)(2,1)S(1)}, bf16[2,4,16,256]{3,2,1,0:T(8,128)(2,1)S(1)}) custom-call(bf16[4,256,256]{2,1,0:T(8,128)(2,1)} %bitcast.8, bf16[4,256,256]{2,1,0:T(8,128)(2,1)} %cot_ref.1), custom_call_target="tpu_custom_call" | custom-call | flops 1 | bytes 1048576 | tf_op jit(solution)/shard_map/pallas_call | solution.py:270
  1.5 3.1 %collective-permute-start = (bf16[2,4,16,256]{3,2,1,0:T(8,128)(2,1)S(1)}, bf16[2,4,16,256]{3,2,1,0:T(8,128)(2,1)S(1)}, u32[]{:S(2)}, u32[]{:S(2)}) collective-permute-start(bf16[2,4,16,256]{3,2,1,0:T(8,128)(2,1)S(1)} %get-tuple-element.29), channel_id=1, source_target_pairs={{0,1},{1,0},{2,3},{3,2},{4,5},{5,4},{6,7},{7,6},{8,9},{9,8},{10,11... | collective-permute-start | bytes 196616 | tf_op jit(solution)/shard_map/ppermute | solution.py:304
  4.6 3.5 %collective-permute-start.1 = (bf16[2,4,16,256]{3,2,1,0:T(8,128)(2,1)S(1)}, bf16[2,4,16,256]{3,2,1,0:T(8,128)(2,1)S(1)}, u32[]{:S(2)}, u32[]{:S(2)}) collective-permute-start(bf16[2,4,16,256]{3,2,1,0:T(8,128)(2,1)S(1)} %get-tuple-element.30), channel_id=1, source_target_pairs={{0,7},{1,2},{2,1},{3,4},{4,3},{5,6},{6,5},{7,0},{8,15},{9,10},{10,... | collective-permute-start | bytes 196616 | tf_op jit(solution)/shard_map/ppermute | solution.py:303
  8.1 0.0 copy-start
  8.1 0.7 %copy-done = s32[4]{0:T(128)S(1)} copy-done((s32[4]{0:T(128)S(1)}, s32[4]{0:T(128)}, u32[]{:S(2)}) %copy-start) | copy-done | bytes 40
  8.8 2.7 %shard_map.93 = (bf16[4,256,256]{2,1,0:T(8,128)(2,1)S(1)}, bf16[4,256,256]{2,1,0:T(8,128)(2,1)S(1)}, bf16[3,256,256]{2,1,0:T(8,128)(2,1)S(1)}, f32[4,1,256]{2,1,...) custom-call(s32[4]{0:T(128)S(1)} %copy-done, ...), custom_call_target="tpu_custom_call" | custom-call | flops 452984832 | bytes 1048576 | tf_op jit(solution)/shard_map/pallas_call | solution.py:270
  11.4 0.0 collective-permute-done.near_ref
  11.4 0.1 collective-permute-done.1.far_ref
  11.5 0.3 shard_map.95
  11.9 0.1 collective-permute-start.2
  12.0 2.0 %collective-permute-done.2.refs_0_.refs_9_ = bf16[4,288,256]{2,1,0:T(8,128)(2,1)S(1)} collective-permute-done((bf16[4,288,256]{2,1,0:T(8,128)(2,1)S(1)}, bf16[4,288,256]{2,1,0:T(8,128)(2,1)S(1)}, u32[]{:S(2)}, u32[]{:S(2)}) %collective-permute-start.2) | collective-permute-done | bytes 589856 | tf_op jit(solution)/shard_map/ppermute | solution.py:348
  13.9 0.7 %collective-permute-start.3 = (bf16[4,288,256]{2,1,0:T(8,128)(2,1)S(1)}, bf16[4,288,256]{2,1,0:T(8,128)(2,1)S(1)}, u32[]{:S(2)}, u32[]{:S(2)}) collective-permute-start(bf16[4,288,256]{2,1,0:T(8,128)(2,1)S(1)} %shard_map.97), channel_id=1, source_target_pairs={{16,8},{17,9},{18,10},{19,11},{20,12},{21,13},{22,14},{23,15}} | collective-permute-start | bytes 1769480 | tf_op jit(solution)/shard_map/ppermute | solution.py:348
  14.6 0.0 collective-permute-done.3.refs_0_.refs_10_
  14.7 11.4 %collective-permute-start.4 = (bf16[4,288,256]{2,1,0:T(8,128)(2,1)S(1)}, bf16[4,288,256]{2,1,0:T(8,128)(2,1)S(1)}, u32[]{:S(2)}, u32[]{:S(2)}) collective-permute-start(bf16[4,288,256]{2,1,0:T(8,128)(2,1)S(1)} %shard_map.98), channel_id=1, source_target_pairs={{0,8},{8,0},{16,24},{24,16},{1,9},{9,1},{17,25},{25,17},{2,10},{10... | collective-permute-start | bytes 1769480 | tf_op jit(solution)/shard_map/ppermute | solution.py:348
  26.1 1.6 %collective-permute-done.4.refs_11_ = bf16[4,288,256]{2,1,0:T(8,128)(2,1)S(1)} collective-permute-done((bf16[4,288,256]{2,1,0:T(8,128)(2,1)S(1)}, bf16[4,288,256]{2,1,0:T(8,128)(2,1)S(1)}, u32[]{:S(2)}, u32[]{:S(2)}) %collective-permute-start.4) | collective-permute-done | bytes 589856 | tf_op jit(solution)/shard_map/ppermute | solution.py:348
  27.7 2.0 %shard_map.99 = (bf16[4,256,256]{2,1,0:T(8,128)(2,1)}, f32[96,256]{1,0:T(8,128)S(1)}, f32[96,256]{1,0:T(8,128)S(1)}, bf16[112,256]{1,0:T(8,128)(2,1)S(1)}, bf16[...) custom-call(f32[4,256,256]{2,1,0:T(8,128)S(1)} %get-tuple-element.28, ...), custom_call_target="tpu_custom_call" | custom-call | flops 905969664 | bytes 1048576 | tf_op jit(solution)/shard_map/pallas_call | solution.py:270
  29.8 0.8 %collective-permute-start.6 = (bf16[112,256]{1,0:T(8,128)(2,1)S(1)}, bf16[112,256]{1,0:T(8,128)(2,1)S(1)}, u32[]{:S(2)}, u32[]{:S(2)}) collective-permute-start(bf16[112,256]{1,0:T(8,128)(2,1)S(1)} %get-tuple-element.43), channel_id=1, source_target_pairs={{0,4},{1,5},{2,6},{3,7},{4,0},{5,1},{6,2},{7,3},{8,12},{9,13},{10,... | collective-permute-start | bytes 172040 | tf_op jit(solution)/shard_map/ppermute | solution.py:372
  30.6 1.3 %collective-permute-start.7 = (bf16[112,256]{1,0:T(8,128)(2,1)S(1)}, bf16[112,256]{1,0:T(8,128)(2,1)S(1)}, u32[]{:S(2)}, u32[]{:S(2)}) collective-permute-start(bf16[112,256]{1,0:T(8,128)(2,1)S(1)} %get-tuple-element.44), channel_id=1, source_target_pairs={{0,6},{1,7},{2,4},{3,5},{4,2},{5,3},{6,0},{7,1},{8,14},{9,15},{10,... | collective-permute-start | bytes 172040 | tf_op jit(solution)/shard_map/ppermute | solution.py:372
  31.9 1.4 %collective-permute-start.5 = (bf16[112,256]{1,0:T(8,128)(2,1)S(1)}, bf16[112,256]{1,0:T(8,128)(2,1)S(1)}, u32[]{:S(2)}, u32[]{:S(2)}) collective-permute-start(bf16[112,256]{1,0:T(8,128)(2,1)S(1)} %get-tuple-element.42.mine_ref), channel_id=1, source_target_pairs={{0,2},{1,3},{2,0},{3,1},{4,6},{5,7},{6,4},{7,5},{8,10},{9,11},{10,... | collective-permute-start | bytes 172040 | tf_op jit(solution)/shard_map/ppermute | solution.py:372
  33.3 1.7 %collective-permute-start.13 = (bf16[96,256]{1,0:T(8,128)(2,1)S(1)}, bf16[96,256]{1,0:T(8,128)(2,1)S(1)}, u32[]{:S(2)}, u32[]{:S(2)}) collective-permute-start(bf16[96,256]{1,0:T(8,128)(2,1)S(1)} %get-tuple-element.47), channel_id=1, source_target_pairs={{0,4},{1,5},{2,6},{3,7},{4,0},{5,1},{6,2},{7,3},{8,12},{9,13},{10,... | collective-permute-start | bytes 147464 | tf_op jit(solution)/shard_map/ppermute | solution.py:372
  35.0 1.3 %collective-permute-start.14 = (bf16[96,256]{1,0:T(8,128)(2,1)S(1)}, bf16[96,256]{1,0:T(8,128)(2,1)S(1)}, u32[]{:S(2)}, u32[]{:S(2)}) collective-permute-start(bf16[96,256]{1,0:T(8,128)(2,1)S(1)} %get-tuple-element.48), channel_id=1, source_target_pairs={{0,6},{1,7},{2,4},{3,5},{4,2},{5,3},{6,0},{7,1},{8,14},{9,15},{10,... | collective-permute-start | bytes 147464 | tf_op jit(solution)/shard_map/ppermute | solution.py:372
  36.3 0.0 collective-permute-done.6.refs_1_
  36.3 0.5 collective-permute-start.12
  36.8 0.4 collective-permute-done.7.refs_2_
  37.2 0.6 %collective-permute-done.5.refs_0_ = bf16[112,256]{1,0:T(8,128)(2,1)S(1)} collective-permute-done((bf16[112,256]{1,0:T(8,128)(2,1)S(1)}, bf16[112,256]{1,0:T(8,128)(2,1)S(1)}, u32[]{:S(2)}, u32[]{:S(2)}) %collective-permute-start.5) | collective-permute-done | bytes 57376 | tf_op jit(solution)/shard_map/ppermute | solution.py:372
  37.8 1.2 %collective-permute-start.8 = (bf16[112,256]{1,0:T(8,128)(2,1)S(1)}, bf16[112,256]{1,0:T(8,128)(2,1)S(1)}, u32[]{:S(2)}, u32[]{:S(2)}) collective-permute-start(bf16[112,256]{1,0:T(8,128)(2,1)S(1)} %shard_map.100.a_ref), channel_id=1, source_target_pairs={{0,1},{1,0},{2,3},{3,2},{4,5},{5,4},{6,7},{7,6},{8,9},{9,8},{10,11... | collective-permute-start | bytes 172040 | tf_op jit(solution)/shard_map/ppermute | solution.py:390
  39.0 1.8 %collective-permute-done.13.refs_1_ = bf16[96,256]{1,0:T(8,128)(2,1)S(1)} collective-permute-done((bf16[96,256]{1,0:T(8,128)(2,1)S(1)}, bf16[96,256]{1,0:T(8,128)(2,1)S(1)}, u32[]{:S(2)}, u32[]{:S(2)}) %collective-permute-start.13) | collective-permute-done | bytes 49184 | tf_op jit(solution)/shard_map/ppermute | solution.py:372
  40.8 0.5 collective-permute-done.14.refs_2_
  41.3 0.2 collective-permute-done.12.refs_0_
  41.5 1.3 %collective-permute-start.15 = (bf16[96,256]{1,0:T(8,128)(2,1)S(1)}, bf16[96,256]{1,0:T(8,128)(2,1)S(1)}, u32[]{:S(2)}, u32[]{:S(2)}) collective-permute-start(bf16[96,256]{1,0:T(8,128)(2,1)S(1)} %shard_map.102.a_ref), channel_id=1, source_target_pairs={{0,1},{1,0},{2,3},{3,2},{4,5},{5,4},{6,7},{7,6},{8,9},{9,8},{10,11... | collective-permute-start | bytes 147464 | tf_op jit(solution)/shard_map/ppermute | solution.py:390
  42.8 0.0 collective-permute-done.8.b_ref
  42.9 2.8 %collective-permute-done.15.b_ref = bf16[96,256]{1,0:T(8,128)(2,1)S(1)} collective-permute-done((bf16[96,256]{1,0:T(8,128)(2,1)S(1)}, bf16[96,256]{1,0:T(8,128)(2,1)S(1)}, u32[]{:S(2)}, u32[]{:S(2)}) %collective-permute-start.15) | collective-permute-done | bytes 49184 | tf_op jit(solution)/shard_map/ppermute | solution.py:390
  45.7 2.9 %collective-permute-start.18 = (bf16[96,256]{1,0:T(8,128)(2,1)S(1)}, bf16[96,256]{1,0:T(8,128)(2,1)S(1)}, u32[]{:S(2)}, u32[]{:S(2)}) collective-permute-start(bf16[96,256]{1,0:T(8,128)(2,1)S(1)} %shard_map.103.refs_4_), channel_id=1, source_target_pairs={{0,6},{1,7},{2,4},{3,5},{4,2},{5,3},{6,0},{7,1},{8,14},{9,15},{10,... | collective-permute-start | bytes 147464 | tf_op jit(solution)/shard_map/ppermute | solution.py:372
  48.6 0.0 collective-permute-start.17
  48.6 1.5 %collective-permute-start.16 = (bf16[96,256]{1,0:T(8,128)(2,1)S(1)}, bf16[96,256]{1,0:T(8,128)(2,1)S(1)}, u32[]{:S(2)}, u32[]{:S(2)}) collective-permute-start(bf16[96,256]{1,0:T(8,128)(2,1)S(1)} %shard_map.103.refs_4_), channel_id=1, source_target_pairs={{0,2},{1,3},{2,0},{3,1},{4,6},{5,7},{6,4},{7,5},{8,10},{9,11},{10,... | collective-permute-start | bytes 147464 | tf_op jit(solution)/shard_map/ppermute | solution.py:372
  50.1 2.8 %collective-permute-start.11 = (bf16[96,256]{1,0:T(8,128)(2,1)S(1)}, bf16[96,256]{1,0:T(8,128)(2,1)S(1)}, u32[]{:S(2)}, u32[]{:S(2)}) collective-permute-start(bf16[96,256]{1,0:T(8,128)(2,1)S(1)} %shard_map.101.refs_0_), channel_id=1, source_target_pairs={{0,6},{1,7},{2,4},{3,5},{4,2},{5,3},{6,0},{7,1},{8,14},{9,15},{10,... | collective-permute-start | bytes 147464 | tf_op jit(solution)/shard_map/ppermute | solution.py:372
  53.0 0.0 collective-permute-start.10
  53.0 0.0 collective-permute-done.18.refs_7_
  53.0 1.5 %collective-permute-start.9 = (bf16[96,256]{1,0:T(8,128)(2,1)S(1)}, bf16[96,256]{1,0:T(8,128)(2,1)S(1)}, u32[]{:S(2)}, u32[]{:S(2)}) collective-permute-start(bf16[96,256]{1,0:T(8,128)(2,1)S(1)} %shard_map.101.refs_0_), channel_id=1, source_target_pairs={{0,2},{1,3},{2,0},{3,1},{4,6},{5,7},{6,4},{7,5},{8,10},{9,11},{10,... | collective-permute-start | bytes 147464 | tf_op jit(solution)/shard_map/ppermute | solution.py:372
  54.5 0.5 collective-permute-done.17.refs_6_
  55.0 0.0 collective-permute-done.16.refs_5_
  55.0 1.3 %collective-permute-done.11.refs_3_ = bf16[96,256]{1,0:T(8,128)(2,1)S(1)} collective-permute-done((bf16[96,256]{1,0:T(8,128)(2,1)S(1)}, bf16[96,256]{1,0:T(8,128)(2,1)S(1)}, u32[]{:S(2)}, u32[]{:S(2)}) %collective-permute-start.11) | collective-permute-done | bytes 49184 | tf_op jit(solution)/shard_map/ppermute | solution.py:372
  56.3 1.6 %collective-permute-done.10.refs_2_ = bf16[96,256]{1,0:T(8,128)(2,1)S(1)} collective-permute-done((bf16[96,256]{1,0:T(8,128)(2,1)S(1)}, bf16[96,256]{1,0:T(8,128)(2,1)S(1)}, u32[]{:S(2)}, u32[]{:S(2)}) %collective-permute-start.10) | collective-permute-done | bytes 49184 | tf_op jit(solution)/shard_map/ppermute | solution.py:372
  58.0 0.0 collective-permute-done.9.refs_1_
  58.0 1.5 %shard_map.104 = (f32[768,256]{1,0:T(8,128)}, f32[36,1,256]{2,1,0:T(1,128)}, f32[36,1,256]{2,1,0:T(1,128)}) custom-call(s32[4]{0:T(128)S(1)} %copy-done, bf16[112,256]{1,0:T(8,128)(2,1)S(1)} %shard_map.100.a_ref, bf16[112,256]{1,0:T(8,128)(2,1)S(1)} %collective-permute-done.8.b_ref, bf16[96,256]{1,0:T(8,128)(2,1)S(1)} %shard_map.101.refs_0_, ...), custom_call_target="tpu_custom_call" | custom-call | flops 1 | bytes 1048576 | tf_op jit(solution)/shard_map/pallas_call | solution.py:270
  (7 shorter events, 0.1 us)
Async XLA Ops:
  1.5 9.9 %collective-permute-start = (bf16[2,4,16,256]{3,2,1,0:T(8,128)(2,1)S(1)}, bf16[2,4,16,256]{3,2,1,0:T(8,128)(2,1)S(1)}, u32[]{:S(2)}, u32[]{:S(2)}) collective-permute-start(bf16[2,4,16,256]{3,2,1,0:T(8,128)(2,1)S(1)} %get-tuple-element.29), channel_id=1, source_target_pairs={{0,1},{1,0},{2,3},{3,2},{4,5},{5,4},{6,7},{7,6},{8,9},{9,8},{10,11... | collective-permute-start | bytes 196616 | tf_op jit(solution)/shard_map/ppermute | solution.py:304
  4.6 7.0 %collective-permute-start.1 = (bf16[2,4,16,256]{3,2,1,0:T(8,128)(2,1)S(1)}, bf16[2,4,16,256]{3,2,1,0:T(8,128)(2,1)S(1)}, u32[]{:S(2)}, u32[]{:S(2)}) collective-permute-start(bf16[2,4,16,256]{3,2,1,0:T(8,128)(2,1)S(1)} %get-tuple-element.30), channel_id=1, source_target_pairs={{0,7},{1,2},{2,1},{3,4},{4,3},{5,6},{6,5},{7,0},{8,15},{9,10},{10,... | collective-permute-start | bytes 196616 | tf_op jit(solution)/shard_map/ppermute | solution.py:303
  8.1 0.7 %copy-start = (s32[4]{0:T(128)S(1)}, s32[4]{0:T(128)}, u32[]{:S(2)}) copy-start(s32[4]{0:T(128)} %bins.3) | copy-start | bytes 52
  11.9 2.1 %collective-permute-start.2 = (bf16[4,288,256]{2,1,0:T(8,128)(2,1)S(1)}, bf16[4,288,256]{2,1,0:T(8,128)(2,1)S(1)}, u32[]{:S(2)}, u32[]{:S(2)}) collective-permute-start(bf16[4,288,256]{2,1,0:T(8,128)(2,1)S(1)} %shard_map.96), channel_id=1, source_target_pairs={{0,8},{8,0},{16,24},{24,16},{1,9},{9,1},{17,25},{25,17},{2,10},{10... | collective-permute-start | bytes 1769480 | tf_op jit(solution)/shard_map/ppermute | solution.py:348
  13.9 0.7 %collective-permute-start.3 = (bf16[4,288,256]{2,1,0:T(8,128)(2,1)S(1)}, bf16[4,288,256]{2,1,0:T(8,128)(2,1)S(1)}, u32[]{:S(2)}, u32[]{:S(2)}) collective-permute-start(bf16[4,288,256]{2,1,0:T(8,128)(2,1)S(1)} %shard_map.97), channel_id=1, source_target_pairs={{16,8},{17,9},{18,10},{19,11},{20,12},{21,13},{22,14},{23,15}} | collective-permute-start | bytes 1769480 | tf_op jit(solution)/shard_map/ppermute | solution.py:348
  14.7 13.1 %collective-permute-start.4 = (bf16[4,288,256]{2,1,0:T(8,128)(2,1)S(1)}, bf16[4,288,256]{2,1,0:T(8,128)(2,1)S(1)}, u32[]{:S(2)}, u32[]{:S(2)}) collective-permute-start(bf16[4,288,256]{2,1,0:T(8,128)(2,1)S(1)} %shard_map.98), channel_id=1, source_target_pairs={{0,8},{8,0},{16,24},{24,16},{1,9},{9,1},{17,25},{25,17},{2,10},{10... | collective-permute-start | bytes 1769480 | tf_op jit(solution)/shard_map/ppermute | solution.py:348
  29.8 6.5 %collective-permute-start.6 = (bf16[112,256]{1,0:T(8,128)(2,1)S(1)}, bf16[112,256]{1,0:T(8,128)(2,1)S(1)}, u32[]{:S(2)}, u32[]{:S(2)}) collective-permute-start(bf16[112,256]{1,0:T(8,128)(2,1)S(1)} %get-tuple-element.43), channel_id=1, source_target_pairs={{0,4},{1,5},{2,6},{3,7},{4,0},{5,1},{6,2},{7,3},{8,12},{9,13},{10,... | collective-permute-start | bytes 172040 | tf_op jit(solution)/shard_map/ppermute | solution.py:372
  30.6 6.6 %collective-permute-start.7 = (bf16[112,256]{1,0:T(8,128)(2,1)S(1)}, bf16[112,256]{1,0:T(8,128)(2,1)S(1)}, u32[]{:S(2)}, u32[]{:S(2)}) collective-permute-start(bf16[112,256]{1,0:T(8,128)(2,1)S(1)} %get-tuple-element.44), channel_id=1, source_target_pairs={{0,6},{1,7},{2,4},{3,5},{4,2},{5,3},{6,0},{7,1},{8,14},{9,15},{10,... | collective-permute-start | bytes 172040 | tf_op jit(solution)/shard_map/ppermute | solution.py:372
  31.9 5.9 %collective-permute-start.5 = (bf16[112,256]{1,0:T(8,128)(2,1)S(1)}, bf16[112,256]{1,0:T(8,128)(2,1)S(1)}, u32[]{:S(2)}, u32[]{:S(2)}) collective-permute-start(bf16[112,256]{1,0:T(8,128)(2,1)S(1)} %get-tuple-element.42.mine_ref), channel_id=1, source_target_pairs={{0,2},{1,3},{2,0},{3,1},{4,6},{5,7},{6,4},{7,5},{8,10},{9,11},{10,... | collective-permute-start | bytes 172040 | tf_op jit(solution)/shard_map/ppermute | solution.py:372
  33.3 7.5 %collective-permute-start.13 = (bf16[96,256]{1,0:T(8,128)(2,1)S(1)}, bf16[96,256]{1,0:T(8,128)(2,1)S(1)}, u32[]{:S(2)}, u32[]{:S(2)}) collective-permute-start(bf16[96,256]{1,0:T(8,128)(2,1)S(1)} %get-tuple-element.47), channel_id=1, source_target_pairs={{0,4},{1,5},{2,6},{3,7},{4,0},{5,1},{6,2},{7,3},{8,12},{9,13},{10,... | collective-permute-start | bytes 147464 | tf_op jit(solution)/shard_map/ppermute | solution.py:372
  35.0 6.3 %collective-permute-start.14 = (bf16[96,256]{1,0:T(8,128)(2,1)S(1)}, bf16[96,256]{1,0:T(8,128)(2,1)S(1)}, u32[]{:S(2)}, u32[]{:S(2)}) collective-permute-start(bf16[96,256]{1,0:T(8,128)(2,1)S(1)} %get-tuple-element.48), channel_id=1, source_target_pairs={{0,6},{1,7},{2,4},{3,5},{4,2},{5,3},{6,0},{7,1},{8,14},{9,15},{10,... | collective-permute-start | bytes 147464 | tf_op jit(solution)/shard_map/ppermute | solution.py:372
  36.3 5.2 %collective-permute-start.12 = (bf16[96,256]{1,0:T(8,128)(2,1)S(1)}, bf16[96,256]{1,0:T(8,128)(2,1)S(1)}, u32[]{:S(2)}, u32[]{:S(2)}) collective-permute-start(bf16[96,256]{1,0:T(8,128)(2,1)S(1)} %get-tuple-element.46.mine_ref), channel_id=1, source_target_pairs={{0,2},{1,3},{2,0},{3,1},{4,6},{5,7},{6,4},{7,5},{8,10},{9,11},{10,... | collective-permute-start | bytes 147464 | tf_op jit(solution)/shard_map/ppermute | solution.py:372
  37.8 5.0 %collective-permute-start.8 = (bf16[112,256]{1,0:T(8,128)(2,1)S(1)}, bf16[112,256]{1,0:T(8,128)(2,1)S(1)}, u32[]{:S(2)}, u32[]{:S(2)}) collective-permute-start(bf16[112,256]{1,0:T(8,128)(2,1)S(1)} %shard_map.100.a_ref), channel_id=1, source_target_pairs={{0,1},{1,0},{2,3},{3,2},{4,5},{5,4},{6,7},{7,6},{8,9},{9,8},{10,11... | collective-permute-start | bytes 172040 | tf_op jit(solution)/shard_map/ppermute | solution.py:390
  41.5 4.2 %collective-permute-start.15 = (bf16[96,256]{1,0:T(8,128)(2,1)S(1)}, bf16[96,256]{1,0:T(8,128)(2,1)S(1)}, u32[]{:S(2)}, u32[]{:S(2)}) collective-permute-start(bf16[96,256]{1,0:T(8,128)(2,1)S(1)} %shard_map.102.a_ref), channel_id=1, source_target_pairs={{0,1},{1,0},{2,3},{3,2},{4,5},{5,4},{6,7},{7,6},{8,9},{9,8},{10,11... | collective-permute-start | bytes 147464 | tf_op jit(solution)/shard_map/ppermute | solution.py:390
  45.7 7.3 %collective-permute-start.18 = (bf16[96,256]{1,0:T(8,128)(2,1)S(1)}, bf16[96,256]{1,0:T(8,128)(2,1)S(1)}, u32[]{:S(2)}, u32[]{:S(2)}) collective-permute-start(bf16[96,256]{1,0:T(8,128)(2,1)S(1)} %shard_map.103.refs_4_), channel_id=1, source_target_pairs={{0,6},{1,7},{2,4},{3,5},{4,2},{5,3},{6,0},{7,1},{8,14},{9,15},{10,... | collective-permute-start | bytes 147464 | tf_op jit(solution)/shard_map/ppermute | solution.py:372
  48.6 6.4 %collective-permute-start.17 = (bf16[96,256]{1,0:T(8,128)(2,1)S(1)}, bf16[96,256]{1,0:T(8,128)(2,1)S(1)}, u32[]{:S(2)}, u32[]{:S(2)}) collective-permute-start(bf16[96,256]{1,0:T(8,128)(2,1)S(1)} %shard_map.103.refs_4_), channel_id=1, source_target_pairs={{0,4},{1,5},{2,6},{3,7},{4,0},{5,1},{6,2},{7,3},{8,12},{9,13},{10,... | collective-permute-start | bytes 147464 | tf_op jit(solution)/shard_map/ppermute | solution.py:372
  48.6 6.4 %collective-permute-start.16 = (bf16[96,256]{1,0:T(8,128)(2,1)S(1)}, bf16[96,256]{1,0:T(8,128)(2,1)S(1)}, u32[]{:S(2)}, u32[]{:S(2)}) collective-permute-start(bf16[96,256]{1,0:T(8,128)(2,1)S(1)} %shard_map.103.refs_4_), channel_id=1, source_target_pairs={{0,2},{1,3},{2,0},{3,1},{4,6},{5,7},{6,4},{7,5},{8,10},{9,11},{10,... | collective-permute-start | bytes 147464 | tf_op jit(solution)/shard_map/ppermute | solution.py:372
  50.1 6.2 %collective-permute-start.11 = (bf16[96,256]{1,0:T(8,128)(2,1)S(1)}, bf16[96,256]{1,0:T(8,128)(2,1)S(1)}, u32[]{:S(2)}, u32[]{:S(2)}) collective-permute-start(bf16[96,256]{1,0:T(8,128)(2,1)S(1)} %shard_map.101.refs_0_), channel_id=1, source_target_pairs={{0,6},{1,7},{2,4},{3,5},{4,2},{5,3},{6,0},{7,1},{8,14},{9,15},{10,... | collective-permute-start | bytes 147464 | tf_op jit(solution)/shard_map/ppermute | solution.py:372
  53.0 5.0 %collective-permute-start.10 = (bf16[96,256]{1,0:T(8,128)(2,1)S(1)}, bf16[96,256]{1,0:T(8,128)(2,1)S(1)}, u32[]{:S(2)}, u32[]{:S(2)}) collective-permute-start(bf16[96,256]{1,0:T(8,128)(2,1)S(1)} %shard_map.101.refs_0_), channel_id=1, source_target_pairs={{0,4},{1,5},{2,6},{3,7},{4,0},{5,1},{6,2},{7,3},{8,12},{9,13},{10,... | collective-permute-start | bytes 147464 | tf_op jit(solution)/shard_map/ppermute | solution.py:372
  53.0 5.0 %collective-permute-start.9 = (bf16[96,256]{1,0:T(8,128)(2,1)S(1)}, bf16[96,256]{1,0:T(8,128)(2,1)S(1)}, u32[]{:S(2)}, u32[]{:S(2)}) collective-permute-start(bf16[96,256]{1,0:T(8,128)(2,1)S(1)} %shard_map.101.refs_0_), channel_id=1, source_target_pairs={{0,2},{1,3},{2,0},{3,1},{4,6},{5,7},{6,4},{7,5},{8,10},{9,11},{10,... | collective-permute-start | bytes 147464 | tf_op jit(solution)/shard_map/ppermute | solution.py:372
where the time goes:
time: 59.7 us; the launch traced here: 59.5 us
  starting transfers between devices  37.1 us (62%)
  waiting for transfers between devices  13.4 us (22%)
  Pallas kernels  7.53 us (13%)
  between operations  0.73 us (1%)
  local copies, waits for them, and re-layouts  0.65 us (1%)
    ppermute x12, starting transfers between devices, across(): return lax.ppermute(value, 'bulk', pairs)  15.8 us
    ppermute x3, starting transfers between devices, step(): sources.append(lax.ppermute(d_wide, 'section', pairs))  12.2 us
    pallas_call x12, Pallas kernels, call(): pl.pallas_call(kernel, in_specs=[smem] * len(scalars) + [kept] * len(remo...  7.53 us
    ppermute x12, waiting for transfers between devices, across(): return lax.ppermute(value, 'bulk', pairs)  6.92 us
    ppermute x3, waiting for transfers between devices, step(): sources.append(lax.ppermute(d_wide, 'section', pairs))  3.62 us
    ppermute x1, starting transfers between devices, step(): far = lax.ppermute(far, 'bulk', opposite)  3.54 us
    ppermute x1, starting transfers between devices, step(): near = lax.ppermute(near, 'bulk', [(i, i ^ 1) for i in range(bulk_count)])  3.06 us
    ppermute x2, waiting for transfers between devices, step(): summed.append((partial_sum, lax.ppermute(partial_sum, 'bulk', swap)))  2.8 us
  transfers between devices with their start and end apart: 19, of which 12 were waited for; matrix products, arithmetic and copies ran while one was open for 0% of the time, Pallas kernels for 5%

commit v1 on v0

--- a/solution.py
+++ b/solution.py
@@ -58,28 +58,37 @@
     return pre + jnp.dot(shifted(wide, -1).astype(BF16), w_ref[2], preferred_element_type=F32)
 
 
+def turn(half, micro, place):
+    start = half if place == 0 else 1 - half
+    return [start * (micro // 2) + j for j in range(micro // 2)]
+
+
 def forward_kernel(bins, x_in, cot_in, w_in, gain_in, shift_in, *refs):
-    x_ref, cot_ref, w_ref, gain_ref, shift_ref, slope_ref, pre_ref, sems = refs
+    x_ref, cot_ref, w_ref, gain_ref, shift_ref, keep_ref, send_ref, pre_ref, sems = refs
     micro = x_ref.shape[0]
+    half = lax.axis_index("section") % 2
     pairs = [(w_in, w_ref), (x_in, x_ref)]
     for m in range(micro):
         pairs.append((gain_in.at[bins[m]], gain_ref.at[m]))
         pairs.append((shift_in.at[bins[m]], shift_ref.at[m]))
-    started = copies(pairs + [(cot_in, cot_ref)], sems)
+    mine = cot_in.at[pl.ds(half * (micro // 2), micro // 2)]
+    started = copies(pairs + [(mine, cot_ref)], sems)
     for copy in started[:-1]:
         copy.wait()
-    for m in range(micro):
-        pre = taps(x_ref[m], w_ref)
-        slope_ref[m] = slopes(pre * gain_ref[m] + shift_ref[m])
-        pre_ref[m] = pre
+    for place, out in enumerate((keep_ref, send_ref)):
+        for j, m in enumerate(turn(half, micro, place)):
+            pre = taps(x_ref[m], w_ref)
+            out[j] = slopes(pre * gain_ref[m] + shift_ref[m]) * gain_ref[m]
+            pre_ref[m] = pre
     started[-1].wait()
 
 
 def rim_kernel(near_ref, far_ref, x_ref, w_ref, gain_ref, shift_ref, *refs):
-    slope_ref, pre_ref, g_ref, halo = refs
+    keep_ref, send_ref, pre_ref, g_ref, halo = refs
     micro, rows = x_ref.shape[:2]
     pad = near_ref.shape[2]
     odd = lax.axis_index("bulk") % 2
+    half = lax.axis_index("section") % 2
 
     @pl.when(odd == 1)
     def _():
@@ -92,17 +101,21 @@
         halo[1] = near_ref[...]
 
     parts = []
-    for m in range(micro):
+    order = turn(half, micro, 0) + turn(half, micro, 1)
+    for m in order:
         parts += [halo[0, 0, m], x_ref[m, :pad], x_ref[m, rows - pad :], halo[1, 0, m]]
-        g_ref[m, 0] = halo[0, 1, m]
-        g_ref[m, 1] = halo[1, 1, m]
+    for j, m in enumerate(turn(half, micro, 0)):
+        g_ref[j, 0] = halo[0, 1, m]
+        g_ref[j, 1] = halo[1, 1, m]
     pre = taps(jnp.concatenate(parts, axis=0), w_ref)
-    for m in range(micro):
+    for index, m in enumerate(order):
+        out = (keep_ref, send_ref)[index // (micro // 2)]
         for side in range(2):
-            start = (2 * m + side) * 2 * pad
+            start = (2 * index + side) * 2 * pad
             here = pre[start : start + 2 * pad]
             pre_ref[m, side] = here
-            slope_ref[m, side] = slopes(here * gain_ref[m] + shift_ref[m])
+            filmed = here * gain_ref[m] + shift_ref[m]
+            out[index % (micro // 2), side] = slopes(filmed) * gain_ref[m]
 
 
 def with_rim(main, rim, m):
@@ -120,30 +133,75 @@
     return lax.dot_general(left, right, (((0,), (0,)), ((), ())), preferred_element_type=F32)
 
 
-def backward(g, slope, gain_row, w_ref):
-    grad_film = g * slope
-    grad_pre = (grad_film * gain_row).astype(BF16)
+def both_sides(grad_pre):
     wide = grad_pre.astype(F32)
-    later = shifted(wide, -1).astype(BF16)
-    earlier = shifted(wide, 1).astype(BF16)
+    return shifted(wide, -1).astype(BF16), shifted(wide, 1).astype(BF16)
+
+
+def backward(g, slope, w_ref):
+    grad_pre = (g * slope).astype(BF16)
+    later, earlier = both_sides(grad_pre)
     d_in = g + times_trans(later, w_ref[0]) + times_trans(grad_pre, w_ref[1])
     d_in = d_in + times_trans(earlier, w_ref[2])
-    return grad_film, later, grad_pre, earlier, d_in.astype(BF16)
+    return grad_pre, d_in.astype(BF16)
 
 
 def top_gradient(cot_ref, rim_ref, m):
     return jnp.concatenate([rim_ref[m, 0], cot_ref[m], rim_ref[m, 1]], axis=0)
 
 
-def relay_kernel(upper, slope_ref, slope_rim, w_ref, gain_ref, *refs):
-    g_refs, d_ref = refs[:-1], refs[-1]
-
-    @pl.when(lax.axis_index("section") == upper)
+def factors(refs, j):
+    main, rim, w_ref = refs
+    return with_rim(main, rim, j), w_ref
+
+
+def relay_kernel(pair, *refs):
+    own, other, g_refs, d_ref = refs[:3], refs[3:6], refs[6:-1], refs[-1]
+    section_id = lax.axis_index("section")
+    for half in range(2):
+        upper, lower = (own, other) if half else (other, own)
+
+        @pl.when(section_id == 2 * pair + half)
+        def _(upper=upper, lower=lower):
+            for j in range(d_ref.shape[0]):
+                g = top_gradient(*g_refs, j) if len(g_refs) == 2 else g_refs[0][j]
+                middle = backward(g.astype(F32), *factors(upper, j))[1]
+                d_ref[j] = backward(middle.astype(F32), *factors(lower, j))[1]
+
+
+def chain_kernel(hops, *refs):
+    own, other, top_refs = refs[:3], refs[3:6], refs[6:8]
+    got_refs = refs[8 : 8 + hops]
+    grad_ref, d_ref, send_ref, g_now = refs[8 + hops :]
+    rows, wide = d_ref.shape[1], grad_ref.shape[1]
+    pad = (wide - rows) // 2
+    inner = slice(pad, pad + rows)
+    section_id = lax.axis_index("section")
+
+    @pl.when(section_id // 2 == hops)
     def _():
-        for m in range(slope_ref.shape[0]):
-            g = top_gradient(*g_refs, m) if len(g_refs) == 2 else g_refs[0][m]
-            slope = with_rim(slope_ref, slope_rim, m)
-            d_ref[m] = backward(g.astype(F32), slope, gain_ref[m], w_ref)[-1]
+        for j in range(d_ref.shape[0]):
+            g_now[j] = top_gradient(*top_refs, j)
+
+    for index in range(hops):
+
+        @pl.when(section_id // 2 == hops - 1 - index)
+        def _(index=index):
+            g_now[...] = got_refs[index][...]
+
+    for half in range(2):
+        upper, lower = (own, other) if half else (other, own)
+
+        @pl.when(section_id % 2 == half)
+        def _(upper=upper, lower=lower, half=half):
+            for j in range(d_ref.shape[0]):
+                first = backward(g_now[j].astype(F32), *factors(upper, j))
+                second = backward(first[1].astype(F32), *factors(lower, j))
+                mine, away = (first, second) if half else (second, first)
+                grad_ref[j] = mine[0]
+                d_ref[j] = mine[1][inner]
+                send_ref[j, :wide] = away[0]
+                send_ref[j, wide:] = away[1][inner]
 
 
 def split_rows(rows):
@@ -158,44 +216,31 @@
     return wide[:half] + wide[half:]
 
 
-def last_kernel(hops, outer, *refs):
-    slope_ref, slope_rim, pre_ref, pre_rim, x_ref, w_ref, gain_ref = refs[:7]
-    cot_ref, g_rim = refs[7:9]
-    got_refs = refs[9 : 9 + hops]
-    d_ref = refs[9 + hops]
-    own_refs = refs[10 + hops : 10 + hops + PARTS]
-    send_refs = refs[10 + hops + PARTS : -3]
-    g_now, total, sums = refs[-3:]
+def last_kernel(outer, *refs):
+    x_ref, pre_ref, pre_rim, gain_ref, grad_ref, d_mine, got_ref, d_ref = refs[:8]
+    own_refs = refs[8 : 8 + PARTS]
+    send_refs = refs[8 + PARTS : -2]
+    total, sums = refs[-2:]
     micro, rows, channels = x_ref.shape
-    pad = g_rim.shape[2]
+    wide = grad_ref.shape[1]
+    pad = (wide - rows) // 2
     inner = slice(pad, pad + rows)
-    section_id = lax.axis_index("section")
     mine = lax.axis_index("bulk") // 2
-
-    @pl.when(section_id == hops)
-    def _():
-        for m in range(micro):
-            g_now[m] = top_gradient(cot_ref, g_rim, m)
-
-    for index in range(hops):
-
-        @pl.when(section_id == hops - 1 - index)
-        def _(index=index):
-            g_now[...] = got_refs[index][...]
-
-    for m in range(micro):
-        g = g_now[m].astype(F32)
-        slope = with_rim(slope_ref, slope_rim, m)
-        parts = backward(g, slope, gain_ref[m], w_ref)
-        d_ref[m] = parts[4][inner]
-        for tap in range(3):
-            where = slice(tap * channels, (tap + 1) * channels)
-            term = trans_times(x_ref[m], parts[1 + tap][inner])
-            total[where] = term if m == 0 else total[where] + term
-        film_main = parts[0][inner]
-        pre = with_rim(pre_ref, pre_rim, m)[inner]
-        sums[m : m + 1] = jnp.sum(film_main * pre, axis=0, keepdims=True)
-        sums[micro + m : micro + m + 1] = jnp.sum(film_main, axis=0, keepdims=True)
+    half = lax.axis_index("section") % 2
+    for place, source in enumerate((grad_ref, got_ref)):
+        for j, m in enumerate(turn(half, micro, place)):
+            grad_pre = source[j, :wide]
+            later, earlier = both_sides(grad_pre)
+            d_ref[m] = got_ref[j, wide:] if place else d_mine[j]
+            for tap, side in enumerate((later, grad_pre, earlier)):
+                where = slice(tap * channels, (tap + 1) * channels)
+                term = trans_times(x_ref[m], side[inner])
+                total[where] = total[where] + term if place or j else term
+            film = grad_pre[inner].astype(F32)
+            pre = with_rim(pre_ref, pre_rim, m)[inner]
+            scale = 1.0 / gain_ref[m]
+            sums[pl.ds(m, 1)] = scale * jnp.sum(film * pre, axis=0, keepdims=True)
+            sums[pl.ds(micro + m, 1)] = scale * jnp.sum(film, axis=0, keepdims=True)
     rows_out = split_rows(sums[...])
     extra = rows_out.shape[0]
     chunk = own_refs[0].shape[0]
@@ -304,13 +349,14 @@
     near = lax.ppermute(near, "bulk", [(i, i ^ 1) for i in range(bulk_count)])
 
     matmul = 2 * 3 * micro * wide * channels * channels
-    wide_shape = (micro, wide, channels)
-    rim_shape = (micro, 2, 2 * pad, channels)
     picked = shape_of((micro, 1, channels), F32)
-    x, cot, w_set, gain_rows, shift_rows, slope, pre = call(
+    count = micro // 2
+    half_main = shape_of((count, rows, channels), F32)
+    x, cot, w_set, gain_rows, shift_rows, keep, send, pre = call(
         forward_kernel,
-        [shape_of(v.shape, v.dtype) for v in (x, cotangent, w_set)]
-        + [picked, picked, shape_of(x.shape, F32), shape_of(x.shape, F32)],
+        [shape_of(x.shape, BF16), shape_of((count, rows, channels), BF16)]
+        + [shape_of(w_set.shape, BF16), picked, picked]
+        + [half_main, half_main, shape_of(x.shape, F32)],
         [],
         scalars=[doa_bins],
         remote=[x, cotangent, w_set, gain_table, shift_table],
@@ -318,50 +364,71 @@
         flops=matmul,
         limit=12,
     )
-    slope_rim, pre_rim, g_rim = call(
+
+    def to_other(value):
+        return lax.ppermute(value, "section", [(i, i ^ 1) for i in range(sections)])
+
+    other_w = to_other(w_set)
+    other = to_other(send)
+    half_rim = shape_of((count, 2, 2 * pad, channels), F32)
+    keep_rim, send_rim, pre_rim, g_rim = call(
         rim_kernel,
-        [
-            shape_of(rim_shape, F32),
-            shape_of(rim_shape, F32),
-            shape_of((micro, 2, pad, channels), BF16),
+        [half_rim, half_rim]
+        + [
+            shape_of((micro, 2, 2 * pad, channels), F32),
+            shape_of((count, 2, pad, channels), BF16),
         ],
         [near, far, x, w_set, gain_rows, shift_rows],
         scratch=[pltpu.VMEM((2, 2, micro, pad, channels), BF16)],
         flops=matmul // 4,
         limit=8,
     )
+    other_rim = to_other(send_rim)
+    tables = [keep, keep_rim, w_set, other, other_rim, other_w]
 
     sources = []
-    for hop in range(sections - 1):
-        upper = sections - 1 - hop
+    half_wide = shape_of((count, wide, channels), BF16)
+    hops = sections // 2 - 1
+    for hop in range(hops):
+        pair = hops - hop
         d_wide = call(
-            functools.partial(relay_kernel, upper),
-            shape_of(wide_shape, BF16),
-            [slope, slope_rim, w_set, gain_rows] + (sources[-1:] if hop else [cot, g_rim]),
+            functools.partial(relay_kernel, pair),
+            half_wide,
+            tables + (sources[-1:] if hop else [cot, g_rim]),
             flops=matmul,
             limit=8,
         )
-        if upper % 2 and sections % 2 == 0:
-            pairs = [(i, i ^ 1) for i in range(sections)]
-        else:
-            pairs = [(upper, upper - 1)]
+        down = [(2 * pair + c, 2 * pair - 2 + c) for c in range(2)]
+        pairs = down + [(target, source) for source, target in down]
         sources.append(lax.ppermute(d_wide, "section", pairs))
+    grad_own, d_own, away = call(
+        functools.partial(chain_kernel, hops),
+        [
+            half_wide,
+            shape_of((count, rows, channels), BF16),
+            shape_of((count, wide + rows, channels), BF16),
+        ],
+        tables + [cot, g_rim] + sources,
+        scratch=[pltpu.VMEM(half_wide.shape, BF16)],
+        flops=matmul,
+        limit=12,
+    )
+    got_away = to_other(away)
 
     chunk = 3 * channels // outer // PARTS
     extra = 4 * micro
     messages = [shape_of((chunk + (0 if part else extra), channels), BF16) for part in range(PARTS)]
     made = call(
-        functools.partial(last_kernel, sections - 1, outer),
+        functools.partial(last_kernel, outer),
         [shape_of(x.shape, BF16)]
         + [shape_of((chunk, channels), F32)] * PARTS
         + [messages[part] for part in range(PARTS) for _ in range(outer - 1)],
-        [slope, slope_rim, pre, pre_rim, x, w_set, gain_rows, cot, g_rim, *sources],
+        [x, pre, pre_rim, gain_rows, grad_own, d_own, got_away],
         scratch=[
-            pltpu.VMEM(wide_shape, BF16),
             pltpu.VMEM((3 * channels, channels), F32),
             pltpu.VMEM((2 * micro, channels), F32),
         ],
-        flops=2 * matmul,
+        flops=matmul,
         limit=16,
     )
     d_local = made[0]
@@ -391,7 +458,9 @@
     spread = []
     for part in range(PARTS):
         done = call(
-            pair_kernel, shape_of((chunk, channels), BF16), list(summed[part]) + spread[-outer:][:1]
+            pair_kernel,
+            shape_of((chunk, channels), BF16),
+            list(summed[part]) + spread[-outer:][:1],
         )
         got = {k: across(done, k) for k in order}
         spread += [done] + [got[k] for k in range(1, outer)]

time: 59.7 us -> 61.1 us (1.023)
  waiting for transfers between devices: 13.4 us -> 24.6 us
  starting transfers between devices: 37.1 us -> 26.9 us
    ppermute x3 -> x1, starting transfers between devices: 12.2 us -> 2.51 us  [step(): sources.append(lax.ppermute(d_wide, 'section', pairs))]
    ppermute x3 -> x1, waiting for transfers between devices: 3.62 us -> 7.32 us  [step(): sources.append(lax.ppermute(d_wide, 'section', pairs))]
    ppermute x1, waiting for transfers between devices: 0.07 us -> 3.41 us  [step(): far = lax.ppermute(far, 'bulk', opposite)]
    ppermute x0 -> x4, waiting for transfers between devices: none -> 3.28 us  [to_other(): return lax.ppermute(value, 'section', [(i, i ^ 1) for i in range(sections)])]
    ppermute x2, starting transfers between devices: 2.52 us -> 1.71 us  [step(): summed.append((partial_sum, lax.ppermute(partial_sum, 'bulk', swap)))]
    ppermute x0 -> x4, starting transfers between devices: none -> 0.78 us  [to_other(): return lax.ppermute(value, 'section', [(i, i ^ 1) for i in range(sections)])]
    pallas_call x12 -> x11, Pallas kernels: 7.53 us -> 7.98 us  [call(): pl.pallas_call(kernel, in_specs=[smem] * len(scalars) + [kept] * len(remo...]
  transfers between devices with their start and end apart: 19 -> 21, of which waited for: 12 -> 12; matrix products, arithmetic and copies ran while one was open for 0% -> 0% of each run, Pallas kernels for 5% -> 2%
where the time goes in v1:
time: 61.1 us; the launch traced here: 60.9 us
  starting transfers between devices  26.9 us (44%)
  waiting for transfers between devices  24.6 us (40%)
  Pallas kernels  7.98 us (13%)
  between operations  0.72 us (1%)
  local copies, waits for them, and re-layouts  0.65 us (1%)
    ppermute x12, starting transfers between devices, across(): return lax.ppermute(value, 'bulk', pairs)  15.4 us
    pallas_call x11, Pallas kernels, call(): pl.pallas_call(kernel, in_specs=[smem] * len(scalars) + [kept] * len(remo...  7.98 us
    ppermute x12, waiting for transfers between devices, across(): return lax.ppermute(value, 'bulk', pairs)  7.36 us
    ppermute x1, waiting for transfers between devices, step(): sources.append(lax.ppermute(d_wide, 'section', pairs))  7.32 us
    ppermute x1, starting transfers between devices, step(): far = lax.ppermute(far, 'bulk', opposite)  3.55 us
    ppermute x1, waiting for transfers between devices, step(): far = lax.ppermute(far, 'bulk', opposite)  3.41 us
    ppermute x4, waiting for transfers between devices, to_other(): return lax.ppermute(value, 'section', [(i, i ^ 1) for i in range(sections)])  3.28 us
    ppermute x2, waiting for transfers between devices, step(): summed.append((partial_sum, lax.ppermute(partial_sum, 'bulk', swap)))  3.26 us
  transfers between devices with their start and end apart: 21, of which 12 were waited for; matrix products, arithmetic and copies ran while one was open for 0% of the time, Pallas kernels for 2%

profile of v1, /device:TPU:0, one launch (start us, length us, event | category | flops | bytes accessed | tf_op | source)
XLA Modules:
  0.0 60.9 jit_solution(17387011015467993170)
XLA Ops:
  0.6 0.0 copy-start
  0.6 0.6 %copy-done = s32[4]{0:T(128)S(1)} copy-done((s32[4]{0:T(128)S(1)}, s32[4]{0:T(128)}, u32[]{:S(2)}) %copy-start) | copy-done | bytes 40
  1.3 2.7 %shard_map.93 = (bf16[4,256,256]{2,1,0:T(8,128)(2,1)S(1)}, bf16[2,256,256]{2,1,0:T(8,128)(2,1)S(1)}, bf16[3,256,256]{2,1,0:T(8,128)(2,1)S(1)}, f32[4,1,256]{2,1,...) custom-call(s32[4]{0:T(128)S(1)} %copy-done, ...), custom_call_target="tpu_custom_call" | custom-call | flops 452984832 | bytes 1048576 | tf_op jit(solution)/shard_map/pallas_call | solution.py:315
  4.0 0.6 collective-permute-start.2
  4.6 0.1 collective-permute-start.4
  4.6 0.8 %shard_map.94 = (bf16[2,4,16,256]{3,2,1,0:T(8,128)(2,1)S(1)}, bf16[2,4,16,256]{3,2,1,0:T(8,128)(2,1)S(1)}) custom-call(bf16[4,256,256]{2,1,0:T(8,128)(2,1)} %bitcast.9, bf16[4,256,256]{2,1,0:T(8,128)(2,1)} %cot_ref.1), custom_call_target="tpu_custom_call" | custom-call | flops 1 | bytes 1048576 | tf_op jit(solution)/shard_map/pallas_call | solution.py:315
  5.5 3.0 %collective-permute-start = (bf16[2,4,16,256]{3,2,1,0:T(8,128)(2,1)S(1)}, bf16[2,4,16,256]{3,2,1,0:T(8,128)(2,1)S(1)}, u32[]{:S(2)}, u32[]{:S(2)}) collective-permute-start(bf16[2,4,16,256]{3,2,1,0:T(8,128)(2,1)S(1)} %get-tuple-element.35), channel_id=1, source_target_pairs={{0,1},{1,0},{2,3},{3,2},{4,5},{5,4},{6,7},{7,6},{8,9},{9,8},{10,11... | collective-permute-start | bytes 196616 | tf_op jit(solution)/shard_map/ppermute | solution.py:349
  8.5 3.5 %collective-permute-start.1 = (bf16[2,4,16,256]{3,2,1,0:T(8,128)(2,1)S(1)}, bf16[2,4,16,256]{3,2,1,0:T(8,128)(2,1)S(1)}, u32[]{:S(2)}, u32[]{:S(2)}) collective-permute-start(bf16[2,4,16,256]{3,2,1,0:T(8,128)(2,1)S(1)} %get-tuple-element.36), channel_id=1, source_target_pairs={{0,7},{1,2},{2,1},{3,4},{4,3},{5,6},{6,5},{7,0},{8,15},{9,10},{10,... | collective-permute-start | bytes 196616 | tf_op jit(solution)/shard_map/ppermute | solution.py:348
  12.0 0.0 collective-permute-done.near_ref
  12.0 3.4 %collective-permute-done.1.far_ref = bf16[2,4,16,256]{3,2,1,0:T(8,128)(2,1)S(1)} collective-permute-done((bf16[2,4,16,256]{3,2,1,0:T(8,128)(2,1)S(1)}, bf16[2,4,16,256]{3,2,1,0:T(8,128)(2,1)S(1)}, u32[]{:S(2)}, u32[]{:S(2)}) %collective-permute-start.1) | collective-permute-done | bytes 65568 | tf_op jit(solution)/shard_map/ppermute | solution.py:348
  15.5 0.3 shard_map.95
  15.8 0.1 collective-permute-start.3
  15.9 1.3 %collective-permute-done.3.refs_4_ = f32[2,2,32,256]{3,2,1,0:T(8,128)S(1)} collective-permute-done((f32[2,2,32,256]{3,2,1,0:T(8,128)S(1)}, f32[2,2,32,256]{3,2,1,0:T(8,128)S(1)}, u32[]{:S(2)}, u32[]{:S(2)}) %collective-permute-start.3) | collective-permute-done | bytes 131104 | tf_op jit(solution)/shard_map/ppermute | solution.py:369
  17.2 0.0 collective-permute-done.4.refs_5_
  17.2 0.0 collective-permute-done.2.refs_3_
  17.2 2.5 %collective-permute-start.5 = (bf16[2,288,256]{2,1,0:T(8,128)(2,1)S(1)}, bf16[2,288,256]{2,1,0:T(8,128)(2,1)S(1)}, u32[]{:S(2)}, u32[]{:S(2)}) collective-permute-start(bf16[2,288,256]{2,1,0:T(8,128)(2,1)S(1)} %shard_map.96), channel_id=1, source_target_pairs={{16,0},{24,8},{0,16},{8,24},{17,1},{25,9},{1,17},{9,25},{18,2},{26... | collective-permute-start | bytes 884744 | tf_op jit(solution)/shard_map/ppermute | solution.py:403
  19.7 7.3 %collective-permute-done.5.refs_8_ = bf16[2,288,256]{2,1,0:T(8,128)(2,1)S(1)} collective-permute-done((bf16[2,288,256]{2,1,0:T(8,128)(2,1)S(1)}, bf16[2,288,256]{2,1,0:T(8,128)(2,1)S(1)}, u32[]{:S(2)}, u32[]{:S(2)}) %collective-permute-start.5) | collective-permute-done | bytes 294944 | tf_op jit(solution)/shard_map/ppermute | solution.py:403
  27.0 1.0 %shard_map.97 = (bf16[2,288,256]{2,1,0:T(8,128)(2,1)S(1)}, bf16[2,256,256]{2,1,0:T(8,128)(2,1)S(1)}, bf16[2,544,256]{2,1,0:T(8,128)(2,1)S(1)}) custom-call(f32[2,256,256]{2,1,0:T(8,128)S(1)} %get-tuple-element.41.refs_0_, f32[2,2,32,256]{3,2,1,0:T(8,128)S(1)} %get-tuple-element.42.refs_1_, bf16[3,256,256]{2,1,0:T(8,128)(2,1)S(1)} %get-tuple-element.37.w_ref.refs_2_, ...), custom_call_target="tpu_custom_call" | custom-call | flops 452984832 | bytes 1048576 | tf_op jit(solution)/shard_map/pallas_call | solution.py:315
  28.0 0.1 collective-permute-start.6
  28.1 1.9 %collective-permute-done.6.refs_6_ = bf16[2,544,256]{2,1,0:T(8,128)(2,1)S(1)} collective-permute-done((bf16[2,544,256]{2,1,0:T(8,128)(2,1)S(1)}, bf16[2,544,256]{2,1,0:T(8,128)(2,1)S(1)}, u32[]{:S(2)}, u32[]{:S(2)}) %collective-permute-start.6) | collective-permute-done | bytes 557088 | tf_op jit(solution)/shard_map/ppermute | solution.py:369
  30.0 1.5 %shard_map.98 = (bf16[4,256,256]{2,1,0:T(8,128)(2,1)}, f32[96,256]{1,0:T(8,128)S(1)}, f32[96,256]{1,0:T(8,128)S(1)}, bf16[112,256]{1,0:T(8,128)(2,1)S(1)}, bf16[...) custom-call(bf16[4,256,256]{2,1,0:T(8,128)(2,1)S(1)} %get-tuple-elem, ...), custom_call_target="tpu_custom_call" | custom-call | flops 452984832 | bytes 1048576 | tf_op jit(solution)/shard_map/pallas_call | solution.py:315
  31.6 0.8 %collective-permute-start.8 = (bf16[112,256]{1,0:T(8,128)(2,1)S(1)}, bf16[112,256]{1,0:T(8,128)(2,1)S(1)}, u32[]{:S(2)}, u32[]{:S(2)}) collective-permute-start(bf16[112,256]{1,0:T(8,128)(2,1)S(1)} %get-tuple-element.53), channel_id=1, source_target_pairs={{0,4},{1,5},{2,6},{3,7},{4,0},{5,1},{6,2},{7,3},{8,12},{9,13},{10,... | collective-permute-start | bytes 172040 | tf_op jit(solution)/shard_map/ppermute | solution.py:439
  32.4 1.3 %collective-permute-start.9 = (bf16[112,256]{1,0:T(8,128)(2,1)S(1)}, bf16[112,256]{1,0:T(8,128)(2,1)S(1)}, u32[]{:S(2)}, u32[]{:S(2)}) collective-permute-start(bf16[112,256]{1,0:T(8,128)(2,1)S(1)} %get-tuple-element.54), channel_id=1, source_target_pairs={{0,6},{1,7},{2,4},{3,5},{4,2},{5,3},{6,0},{7,1},{8,14},{9,15},{10,... | collective-permute-start | bytes 172040 | tf_op jit(solution)/shard_map/ppermute | solution.py:439
  33.7 1.4 %collective-permute-start.7 = (bf16[112,256]{1,0:T(8,128)(2,1)S(1)}, bf16[112,256]{1,0:T(8,128)(2,1)S(1)}, u32[]{:S(2)}, u32[]{:S(2)}) collective-permute-start(bf16[112,256]{1,0:T(8,128)(2,1)S(1)} %get-tuple-element.52.mine_ref), channel_id=1, source_target_pairs={{0,2},{1,3},{2,0},{3,1},{4,6},{5,7},{6,4},{7,5},{8,10},{9,11},{10,... | collective-permute-start | bytes 172040 | tf_op jit(solution)/shard_map/ppermute | solution.py:439
  35.1 1.7 %collective-permute-start.15 = (bf16[96,256]{1,0:T(8,128)(2,1)S(1)}, bf16[96,256]{1,0:T(8,128)(2,1)S(1)}, u32[]{:S(2)}, u32[]{:S(2)}) collective-permute-start(bf16[96,256]{1,0:T(8,128)(2,1)S(1)} %get-tuple-element.57), channel_id=1, source_target_pairs={{0,4},{1,5},{2,6},{3,7},{4,0},{5,1},{6,2},{7,3},{8,12},{9,13},{10,... | collective-permute-start | bytes 147464 | tf_op jit(solution)/shard_map/ppermute | solution.py:439
  36.8 1.3 %collective-permute-start.16 = (bf16[96,256]{1,0:T(8,128)(2,1)S(1)}, bf16[96,256]{1,0:T(8,128)(2,1)S(1)}, u32[]{:S(2)}, u32[]{:S(2)}) collective-permute-start(bf16[96,256]{1,0:T(8,128)(2,1)S(1)} %get-tuple-element.58), channel_id=1, source_target_pairs={{0,6},{1,7},{2,4},{3,5},{4,2},{5,3},{6,0},{7,1},{8,14},{9,15},{10,... | collective-permute-start | bytes 147464 | tf_op jit(solution)/shard_map/ppermute | solution.py:439
  38.1 1.0 %collective-permute-done.8.refs_1_ = bf16[112,256]{1,0:T(8,128)(2,1)S(1)} collective-permute-done((bf16[112,256]{1,0:T(8,128)(2,1)S(1)}, bf16[112,256]{1,0:T(8,128)(2,1)S(1)}, u32[]{:S(2)}, u32[]{:S(2)}) %collective-permute-start.8) | collective-permute-done | bytes 57376 | tf_op jit(solution)/shard_map/ppermute | solution.py:439
  39.1 0.0 collective-permute-start.14
  39.1 0.0 collective-permute-done.9.refs_2_
  39.1 0.4 collective-permute-done.7.refs_0_
  39.5 0.8 %collective-permute-start.10 = (bf16[112,256]{1,0:T(8,128)(2,1)S(1)}, bf16[112,256]{1,0:T(8,128)(2,1)S(1)}, u32[]{:S(2)}, u32[]{:S(2)}) collective-permute-start(bf16[112,256]{1,0:T(8,128)(2,1)S(1)} %shard_map.99.a_ref), channel_id=1, source_target_pairs={{0,1},{1,0},{2,3},{3,2},{4,5},{5,4},{6,7},{7,6},{8,9},{9,8},{10,11... | collective-permute-start | bytes 172040 | tf_op jit(solution)/shard_map/ppermute | solution.py:457
  40.3 2.6 %collective-permute-done.15.refs_1_ = bf16[96,256]{1,0:T(8,128)(2,1)S(1)} collective-permute-done((bf16[96,256]{1,0:T(8,128)(2,1)S(1)}, bf16[96,256]{1,0:T(8,128)(2,1)S(1)}, u32[]{:S(2)}, u32[]{:S(2)}) %collective-permute-start.15) | collective-permute-done | bytes 49184 | tf_op jit(solution)/shard_map/ppermute | solution.py:439
  42.9 0.0 collective-permute-done.16.refs_2_
  42.9 0.4 collective-permute-done.14.refs_0_
  43.4 0.9 %collective-permute-start.17 = (bf16[96,256]{1,0:T(8,128)(2,1)S(1)}, bf16[96,256]{1,0:T(8,128)(2,1)S(1)}, u32[]{:S(2)}, u32[]{:S(2)}) collective-permute-start(bf16[96,256]{1,0:T(8,128)(2,1)S(1)} %shard_map.101.a_ref), channel_id=1, source_target_pairs={{0,1},{1,0},{2,3},{3,2},{4,5},{5,4},{6,7},{7,6},{8,9},{9,8},{10,11... | collective-permute-start | bytes 147464 | tf_op jit(solution)/shard_map/ppermute | solution.py:457
  44.3 0.0 collective-permute-done.10.b_ref
  44.3 3.3 %collective-permute-done.17.b_ref = bf16[96,256]{1,0:T(8,128)(2,1)S(1)} collective-permute-done((bf16[96,256]{1,0:T(8,128)(2,1)S(1)}, bf16[96,256]{1,0:T(8,128)(2,1)S(1)}, u32[]{:S(2)}, u32[]{:S(2)}) %collective-permute-start.17) | collective-permute-done | bytes 49184 | tf_op jit(solution)/shard_map/ppermute | solution.py:457
  47.6 2.5 %collective-permute-start.20 = (bf16[96,256]{1,0:T(8,128)(2,1)S(1)}, bf16[96,256]{1,0:T(8,128)(2,1)S(1)}, u32[]{:S(2)}, u32[]{:S(2)}) collective-permute-start(bf16[96,256]{1,0:T(8,128)(2,1)S(1)} %shard_map.102.refs_4_), channel_id=1, source_target_pairs={{0,6},{1,7},{2,4},{3,5},{4,2},{5,3},{6,0},{7,1},{8,14},{9,15},{10,... | collective-permute-start | bytes 147464 | tf_op jit(solution)/shard_map/ppermute | solution.py:439
  50.0 0.0 collective-permute-start.19
  50.1 2.0 %collective-permute-start.18 = (bf16[96,256]{1,0:T(8,128)(2,1)S(1)}, bf16[96,256]{1,0:T(8,128)(2,1)S(1)}, u32[]{:S(2)}, u32[]{:S(2)}) collective-permute-start(bf16[96,256]{1,0:T(8,128)(2,1)S(1)} %shard_map.102.refs_4_), channel_id=1, source_target_pairs={{0,2},{1,3},{2,0},{3,1},{4,6},{5,7},{6,4},{7,5},{8,10},{9,11},{10,... | collective-permute-start | bytes 147464 | tf_op jit(solution)/shard_map/ppermute | solution.py:439
  52.0 2.4 %collective-permute-start.13 = (bf16[96,256]{1,0:T(8,128)(2,1)S(1)}, bf16[96,256]{1,0:T(8,128)(2,1)S(1)}, u32[]{:S(2)}, u32[]{:S(2)}) collective-permute-start(bf16[96,256]{1,0:T(8,128)(2,1)S(1)} %shard_map.100.refs_0_), channel_id=1, source_target_pairs={{0,6},{1,7},{2,4},{3,5},{4,2},{5,3},{6,0},{7,1},{8,14},{9,15},{10,... | collective-permute-start | bytes 147464 | tf_op jit(solution)/shard_map/ppermute | solution.py:439
  54.4 0.0 collective-permute-start.12
  54.4 0.0 collective-permute-done.20.refs_7_
  54.4 2.0 %collective-permute-start.11 = (bf16[96,256]{1,0:T(8,128)(2,1)S(1)}, bf16[96,256]{1,0:T(8,128)(2,1)S(1)}, u32[]{:S(2)}, u32[]{:S(2)}) collective-permute-start(bf16[96,256]{1,0:T(8,128)(2,1)S(1)} %shard_map.100.refs_0_), channel_id=1, source_target_pairs={{0,2},{1,3},{2,0},{3,1},{4,6},{5,7},{6,4},{7,5},{8,10},{9,11},{10,... | collective-permute-start | bytes 147464 | tf_op jit(solution)/shard_map/ppermute | solution.py:439
  56.4 0.3 collective-permute-done.19.refs_6_
  56.7 0.0 collective-permute-done.18.refs_5_
  56.7 1.2 %collective-permute-done.13.refs_3_ = bf16[96,256]{1,0:T(8,128)(2,1)S(1)} collective-permute-done((bf16[96,256]{1,0:T(8,128)(2,1)S(1)}, bf16[96,256]{1,0:T(8,128)(2,1)S(1)}, u32[]{:S(2)}, u32[]{:S(2)}) %collective-permute-start.13) | collective-permute-done | bytes 49184 | tf_op jit(solution)/shard_map/ppermute | solution.py:439
  57.9 1.5 %collective-permute-done.12.refs_2_ = bf16[96,256]{1,0:T(8,128)(2,1)S(1)} collective-permute-done((bf16[96,256]{1,0:T(8,128)(2,1)S(1)}, bf16[96,256]{1,0:T(8,128)(2,1)S(1)}, u32[]{:S(2)}, u32[]{:S(2)}) %collective-permute-start.12) | collective-permute-done | bytes 49184 | tf_op jit(solution)/shard_map/ppermute | solution.py:439
  59.4 0.0 collective-permute-done.11.refs_1_
  59.4 1.5 %shard_map.103 = (f32[768,256]{1,0:T(8,128)}, f32[36,1,256]{2,1,0:T(1,128)}, f32[36,1,256]{2,1,0:T(1,128)}) custom-call(s32[4]{0:T(128)S(1)} %copy-done, bf16[112,256]{1,0:T(8,128)(2,1)S(1)} %shard_map.99.a_ref, bf16[112,256]{1,0:T(8,128)(2,1)S(1)} %collective-permute-done.10.b_ref, bf16[96,256]{1,0:T(8,128)(2,1)S(1)} %shard_map.100.refs_0_, ...), custom_call_target="tpu_custom_call" | custom-call | flops 1 | bytes 1048576 | tf_op jit(solution)/shard_map/pallas_call | solution.py:315
  (5 shorter events, 0.1 us)
Async XLA Ops:
  0.6 0.7 %copy-start = (s32[4]{0:T(128)S(1)}, s32[4]{0:T(128)}, u32[]{:S(2)}) copy-start(s32[4]{0:T(128)} %bins.3) | copy-start | bytes 52
  4.0 13.2 %collective-permute-start.2 = (f32[2,256,256]{2,1,0:T(8,128)S(1)}, f32[2,256,256]{2,1,0:T(8,128)S(1)}, u32[]{:S(2)}, u32[]{:S(2)}) collective-permute-start(f32[2,256,256]{2,1,0:T(8,128)S(1)} %get-tuple-element.43), channel_id=1, source_target_pairs={{0,8},{8,0},{16,24},{24,16},{1,9},{9,1},{17,25},{25,17},{2,10},{10... | collective-permute-start | bytes 1572872 | tf_op jit(solution)/shard_map/ppermute | solution.py:369
  4.6 12.6 %collective-permute-start.4 = (bf16[3,256,256]{2,1,0:T(8,128)(2,1)S(1)}, bf16[3,256,256]{2,1,0:T(8,128)(2,1)S(1)}, u32[]{:S(2)}, u32[]{:S(2)}) collective-permute-start(bf16[3,256,256]{2,1,0:T(8,128)(2,1)S(1)} %get-tuple-element.37.w_ref.refs_2_), channel_id=1, source_target_pairs={{0,8},{8,0},{16,24},{24,16},{1,9},{9,1},{17,25},{25,17},{2,10},{10... | collective-permute-start | bytes 1179656 | tf_op jit(solution)/shard_map/ppermute | solution.py:369
  5.5 6.5 %collective-permute-start = (bf16[2,4,16,256]{3,2,1,0:T(8,128)(2,1)S(1)}, bf16[2,4,16,256]{3,2,1,0:T(8,128)(2,1)S(1)}, u32[]{:S(2)}, u32[]{:S(2)}) collective-permute-start(bf16[2,4,16,256]{3,2,1,0:T(8,128)(2,1)S(1)} %get-tuple-element.35), channel_id=1, source_target_pairs={{0,1},{1,0},{2,3},{3,2},{4,5},{5,4},{6,7},{7,6},{8,9},{9,8},{10,11... | collective-permute-start | bytes 196616 | tf_op jit(solution)/shard_map/ppermute | solution.py:349
  8.5 7.0 %collective-permute-start.1 = (bf16[2,4,16,256]{3,2,1,0:T(8,128)(2,1)S(1)}, bf16[2,4,16,256]{3,2,1,0:T(8,128)(2,1)S(1)}, u32[]{:S(2)}, u32[]{:S(2)}) collective-permute-start(bf16[2,4,16,256]{3,2,1,0:T(8,128)(2,1)S(1)} %get-tuple-element.36), channel_id=1, source_target_pairs={{0,7},{1,2},{2,1},{3,4},{4,3},{5,6},{6,5},{7,0},{8,15},{9,10},{10,... | collective-permute-start | bytes 196616 | tf_op jit(solution)/shard_map/ppermute | solution.py:348
  15.8 1.4 %collective-permute-start.3 = (f32[2,2,32,256]{3,2,1,0:T(8,128)S(1)}, f32[2,2,32,256]{3,2,1,0:T(8,128)S(1)}, u32[]{:S(2)}, u32[]{:S(2)}) collective-permute-start(f32[2,2,32,256]{3,2,1,0:T(8,128)S(1)} %get-tuple-element.44), channel_id=1, source_target_pairs={{0,8},{8,0},{16,24},{24,16},{1,9},{9,1},{17,25},{25,17},{2,10},{10... | collective-permute-start | bytes 393224 | tf_op jit(solution)/shard_map/ppermute | solution.py:369
  17.2 9.8 %collective-permute-start.5 = (bf16[2,288,256]{2,1,0:T(8,128)(2,1)S(1)}, bf16[2,288,256]{2,1,0:T(8,128)(2,1)S(1)}, u32[]{:S(2)}, u32[]{:S(2)}) collective-permute-start(bf16[2,288,256]{2,1,0:T(8,128)(2,1)S(1)} %shard_map.96), channel_id=1, source_target_pairs={{16,0},{24,8},{0,16},{8,24},{17,1},{25,9},{1,17},{9,25},{18,2},{26... | collective-permute-start | bytes 884744 | tf_op jit(solution)/shard_map/ppermute | solution.py:403
  28.0 2.0 %collective-permute-start.6 = (bf16[2,544,256]{2,1,0:T(8,128)(2,1)S(1)}, bf16[2,544,256]{2,1,0:T(8,128)(2,1)S(1)}, u32[]{:S(2)}, u32[]{:S(2)}) collective-permute-start(bf16[2,544,256]{2,1,0:T(8,128)(2,1)S(1)} %get-tuple-element.49), channel_id=1, source_target_pairs={{0,8},{8,0},{16,24},{24,16},{1,9},{9,1},{17,25},{25,17},{2,10},{10... | collective-permute-start | bytes 1671176 | tf_op jit(solution)/shard_map/ppermute | solution.py:369
  31.6 7.5 %collective-permute-start.8 = (bf16[112,256]{1,0:T(8,128)(2,1)S(1)}, bf16[112,256]{1,0:T(8,128)(2,1)S(1)}, u32[]{:S(2)}, u32[]{:S(2)}) collective-permute-start(bf16[112,256]{1,0:T(8,128)(2,1)S(1)} %get-tuple-element.53), channel_id=1, source_target_pairs={{0,4},{1,5},{2,6},{3,7},{4,0},{5,1},{6,2},{7,3},{8,12},{9,13},{10,... | collective-permute-start | bytes 172040 | tf_op jit(solution)/shard_map/ppermute | solution.py:439
  32.4 6.7 %collective-permute-start.9 = (bf16[112,256]{1,0:T(8,128)(2,1)S(1)}, bf16[112,256]{1,0:T(8,128)(2,1)S(1)}, u32[]{:S(2)}, u32[]{:S(2)}) collective-permute-start(bf16[112,256]{1,0:T(8,128)(2,1)S(1)} %get-tuple-element.54), channel_id=1, source_target_pairs={{0,6},{1,7},{2,4},{3,5},{4,2},{5,3},{6,0},{7,1},{8,14},{9,15},{10,... | collective-permute-start | bytes 172040 | tf_op jit(solution)/shard_map/ppermute | solution.py:439
  33.7 5.7 %collective-permute-start.7 = (bf16[112,256]{1,0:T(8,128)(2,1)S(1)}, bf16[112,256]{1,0:T(8,128)(2,1)S(1)}, u32[]{:S(2)}, u32[]{:S(2)}) collective-permute-start(bf16[112,256]{1,0:T(8,128)(2,1)S(1)} %get-tuple-element.52.mine_ref), channel_id=1, source_target_pairs={{0,2},{1,3},{2,0},{3,1},{4,6},{5,7},{6,4},{7,5},{8,10},{9,11},{10,... | collective-permute-start | bytes 172040 | tf_op jit(solution)/shard_map/ppermute | solution.py:439
  35.1 7.9 %collective-permute-start.15 = (bf16[96,256]{1,0:T(8,128)(2,1)S(1)}, bf16[96,256]{1,0:T(8,128)(2,1)S(1)}, u32[]{:S(2)}, u32[]{:S(2)}) collective-permute-start(bf16[96,256]{1,0:T(8,128)(2,1)S(1)} %get-tuple-element.57), channel_id=1, source_target_pairs={{0,4},{1,5},{2,6},{3,7},{4,0},{5,1},{6,2},{7,3},{8,12},{9,13},{10,... | collective-permute-start | bytes 147464 | tf_op jit(solution)/shard_map/ppermute | solution.py:439
  36.8 6.2 %collective-permute-start.16 = (bf16[96,256]{1,0:T(8,128)(2,1)S(1)}, bf16[96,256]{1,0:T(8,128)(2,1)S(1)}, u32[]{:S(2)}, u32[]{:S(2)}) collective-permute-start(bf16[96,256]{1,0:T(8,128)(2,1)S(1)} %get-tuple-element.58), channel_id=1, source_target_pairs={{0,6},{1,7},{2,4},{3,5},{4,2},{5,3},{6,0},{7,1},{8,14},{9,15},{10,... | collective-permute-start | bytes 147464 | tf_op jit(solution)/shard_map/ppermute | solution.py:439
  39.1 4.3 %collective-permute-start.14 = (bf16[96,256]{1,0:T(8,128)(2,1)S(1)}, bf16[96,256]{1,0:T(8,128)(2,1)S(1)}, u32[]{:S(2)}, u32[]{:S(2)}) collective-permute-start(bf16[96,256]{1,0:T(8,128)(2,1)S(1)} %get-tuple-element.56.mine_ref), channel_id=1, source_target_pairs={{0,2},{1,3},{2,0},{3,1},{4,6},{5,7},{6,4},{7,5},{8,10},{9,11},{10,... | collective-permute-start | bytes 147464 | tf_op jit(solution)/shard_map/ppermute | solution.py:439
  39.5 4.8 %collective-permute-start.10 = (bf16[112,256]{1,0:T(8,128)(2,1)S(1)}, bf16[112,256]{1,0:T(8,128)(2,1)S(1)}, u32[]{:S(2)}, u32[]{:S(2)}) collective-permute-start(bf16[112,256]{1,0:T(8,128)(2,1)S(1)} %shard_map.99.a_ref), channel_id=1, source_target_pairs={{0,1},{1,0},{2,3},{3,2},{4,5},{5,4},{6,7},{7,6},{8,9},{9,8},{10,11... | collective-permute-start | bytes 172040 | tf_op jit(solution)/shard_map/ppermute | solution.py:457
  43.4 4.2 %collective-permute-start.17 = (bf16[96,256]{1,0:T(8,128)(2,1)S(1)}, bf16[96,256]{1,0:T(8,128)(2,1)S(1)}, u32[]{:S(2)}, u32[]{:S(2)}) collective-permute-start(bf16[96,256]{1,0:T(8,128)(2,1)S(1)} %shard_map.101.a_ref), channel_id=1, source_target_pairs={{0,1},{1,0},{2,3},{3,2},{4,5},{5,4},{6,7},{7,6},{8,9},{9,8},{10,11... | collective-permute-start | bytes 147464 | tf_op jit(solution)/shard_map/ppermute | solution.py:457
  47.6 6.8 %collective-permute-start.20 = (bf16[96,256]{1,0:T(8,128)(2,1)S(1)}, bf16[96,256]{1,0:T(8,128)(2,1)S(1)}, u32[]{:S(2)}, u32[]{:S(2)}) collective-permute-start(bf16[96,256]{1,0:T(8,128)(2,1)S(1)} %shard_map.102.refs_4_), channel_id=1, source_target_pairs={{0,6},{1,7},{2,4},{3,5},{4,2},{5,3},{6,0},{7,1},{8,14},{9,15},{10,... | collective-permute-start | bytes 147464 | tf_op jit(solution)/shard_map/ppermute | solution.py:439
  50.0 6.7 %collective-permute-start.19 = (bf16[96,256]{1,0:T(8,128)(2,1)S(1)}, bf16[96,256]{1,0:T(8,128)(2,1)S(1)}, u32[]{:S(2)}, u32[]{:S(2)}) collective-permute-start(bf16[96,256]{1,0:T(8,128)(2,1)S(1)} %shard_map.102.refs_4_), channel_id=1, source_target_pairs={{0,4},{1,5},{2,6},{3,7},{4,0},{5,1},{6,2},{7,3},{8,12},{9,13},{10,... | collective-permute-start | bytes 147464 | tf_op jit(solution)/shard_map/ppermute | solution.py:439
  50.1 6.6 %collective-permute-start.18 = (bf16[96,256]{1,0:T(8,128)(2,1)S(1)}, bf16[96,256]{1,0:T(8,128)(2,1)S(1)}, u32[]{:S(2)}, u32[]{:S(2)}) collective-permute-start(bf16[96,256]{1,0:T(8,128)(2,1)S(1)} %shard_map.102.refs_4_), channel_id=1, source_target_pairs={{0,2},{1,3},{2,0},{3,1},{4,6},{5,7},{6,4},{7,5},{8,10},{9,11},{10,... | collective-permute-start | bytes 147464 | tf_op jit(solution)/shard_map/ppermute | solution.py:439
  52.0 5.9 %collective-permute-start.13 = (bf16[96,256]{1,0:T(8,128)(2,1)S(1)}, bf16[96,256]{1,0:T(8,128)(2,1)S(1)}, u32[]{:S(2)}, u32[]{:S(2)}) collective-permute-start(bf16[96,256]{1,0:T(8,128)(2,1)S(1)} %shard_map.100.refs_0_), channel_id=1, source_target_pairs={{0,6},{1,7},{2,4},{3,5},{4,2},{5,3},{6,0},{7,1},{8,14},{9,15},{10,... | collective-permute-start | bytes 147464 | tf_op jit(solution)/shard_map/ppermute | solution.py:439
  54.4 5.0 %collective-permute-start.12 = (bf16[96,256]{1,0:T(8,128)(2,1)S(1)}, bf16[96,256]{1,0:T(8,128)(2,1)S(1)}, u32[]{:S(2)}, u32[]{:S(2)}) collective-permute-start(bf16[96,256]{1,0:T(8,128)(2,1)S(1)} %shard_map.100.refs_0_), channel_id=1, source_target_pairs={{0,4},{1,5},{2,6},{3,7},{4,0},{5,1},{6,2},{7,3},{8,12},{9,13},{10,... | collective-permute-start | bytes 147464 | tf_op jit(solution)/shard_map/ppermute | solution.py:439
  54.4 5.0 %collective-permute-start.11 = (bf16[96,256]{1,0:T(8,128)(2,1)S(1)}, bf16[96,256]{1,0:T(8,128)(2,1)S(1)}, u32[]{:S(2)}, u32[]{:S(2)}) collective-permute-start(bf16[96,256]{1,0:T(8,128)(2,1)S(1)} %shard_map.100.refs_0_), channel_id=1, source_target_pairs={{0,2},{1,3},{2,0},{3,1},{4,6},{5,7},{6,4},{7,5},{8,10},{9,11},{10,... | collective-permute-start | bytes 147464 | tf_op jit(solution)/shard_map/ppermute | solution.py:439

commit v2 on v1

--- a/solution.py
+++ b/solution.py
@@ -63,23 +63,27 @@
     return [start * (micro // 2) + j for j in range(micro // 2)]
 
 
-def forward_kernel(bins, x_in, cot_in, w_in, gain_in, shift_in, *refs):
-    x_ref, cot_ref, w_ref, gain_ref, shift_ref, keep_ref, send_ref, pre_ref, sems = refs
+def forward_kernel(bins_in, x_in, cot_in, w_in, gain_in, shift_in, *refs):
+    x_ref, cot_ref, w_ref, gain_ref, shift_ref, keep_ref, send_ref, pre_ref = refs[:8]
+    bins, gains, shifts, sems = refs[8:]
     micro = x_ref.shape[0]
     half = lax.axis_index("section") % 2
-    pairs = [(w_in, w_ref), (x_in, x_ref)]
-    for m in range(micro):
-        pairs.append((gain_in.at[bins[m]], gain_ref.at[m]))
-        pairs.append((shift_in.at[bins[m]], shift_ref.at[m]))
+    order = turn(half, micro, 1) + turn(half, micro, 0)
+    pairs = [(bins_in, bins), (gain_in, gains), (shift_in, shifts), (w_in, w_ref)]
+    pairs += [(x_in.at[m], x_ref.at[m]) for m in order]
     mine = cot_in.at[pl.ds(half * (micro // 2), micro // 2)]
     started = copies(pairs + [(mine, cot_ref)], sems)
-    for copy in started[:-1]:
+    for copy in started[:4]:
         copy.wait()
-    for place, out in enumerate((keep_ref, send_ref)):
-        for j, m in enumerate(turn(half, micro, place)):
-            pre = taps(x_ref[m], w_ref)
-            out[j] = slopes(pre * gain_ref[m] + shift_ref[m]) * gain_ref[m]
-            pre_ref[m] = pre
+    for m in range(micro):
+        gain_ref[m] = gains[bins[m]]
+        shift_ref[m] = shifts[bins[m]]
+    for index, m in enumerate(order):
+        started[4 + index].wait()
+        out = (send_ref, keep_ref)[index // (micro // 2)]
+        pre = taps(x_ref[m], w_ref)
+        out[index % (micro // 2)] = slopes(pre * gain_ref[m] + shift_ref[m]) * gain_ref[m]
+        pre_ref[m] = pre
     started[-1].wait()
 
 
@@ -143,7 +147,7 @@
     later, earlier = both_sides(grad_pre)
     d_in = g + times_trans(later, w_ref[0]) + times_trans(grad_pre, w_ref[1])
     d_in = d_in + times_trans(earlier, w_ref[2])
-    return grad_pre, d_in.astype(BF16)
+    return grad_pre, d_in.astype(BF16), d_in
 
 
 def top_gradient(cot_ref, rim_ref, m):
@@ -155,24 +159,86 @@
     return with_rim(main, rim, j), w_ref
 
 
-def relay_kernel(pair, *refs):
-    own, other, g_refs, d_ref = refs[:3], refs[3:6], refs[6:-1], refs[-1]
+def by_half(pair, own, other, run):
     section_id = lax.axis_index("section")
     for half in range(2):
         upper, lower = (own, other) if half else (other, own)
-
-        @pl.when(section_id == 2 * pair + half)
-        def _(upper=upper, lower=lower):
-            for j in range(d_ref.shape[0]):
-                g = top_gradient(*g_refs, j) if len(g_refs) == 2 else g_refs[0][j]
-                middle = backward(g.astype(F32), *factors(upper, j))[1]
-                d_ref[j] = backward(middle.astype(F32), *factors(lower, j))[1]
+        here = section_id % 2 == half if pair is None else section_id == 2 * pair + half
+
+        @pl.when(here)
+        def _(upper=upper, lower=lower, half=half):
+            run(upper, lower, half)
+
+
+def inner_kernel(pair, *refs):
+    own, other, cot_ref, d_ref = refs[:2], refs[2:4], refs[4], refs[5]
+    rows = cot_ref.shape[1]
+    cut = (rows - d_ref.shape[1]) // 2
+
+    def run(upper, lower, half):
+        for j in range(d_ref.shape[0]):
+            g = cot_ref[j].astype(F32)
+            middle = backward(g, upper[0][j], upper[1])[1].astype(F32)
+            d_ref[j] = backward(middle, lower[0][j], lower[1])[2][cut : rows - cut].astype(BF16)
+
+    by_half(pair, own, other, run)
+
+
+def outer_kernel(pair, *refs):
+    own, other, cot_ref, rim_ref, d_ref = refs[:2], refs[2:4], refs[4], refs[5], refs[6]
+    count, rows = cot_ref.shape[:2]
+    pad = rim_ref.shape[2]
+    cut = d_ref.shape[2] // 2
+
+    def stacked(ref):
+        return jnp.concatenate([ref[j, side] for j in range(count) for side in range(2)], axis=0)
+
+    def run(upper, lower, half):
+        parts = []
+        for j in range(count):
+            parts += [rim_ref[j, 0], cot_ref[j, :pad], cot_ref[j, rows - pad :], rim_ref[j, 1]]
+        g = jnp.concatenate(parts, axis=0).astype(F32)
+        middle = backward(g, stacked(upper[0]), upper[1])[1].astype(F32)
+        d_in = backward(middle, stacked(lower[0]), lower[1])[2]
+        for j in range(count):
+            for side in range(2):
+                start = (2 * j + side) * 2 * pad + pad - cut
+                d_ref[j, side] = d_in[start : start + 2 * cut].astype(BF16)
+
+    by_half(pair, own, other, run)
+
+
+def arrived(inner_ref, outer_ref, j, wide):
+    rest = wide - inner_ref.shape[1] - 2 * outer_ref.shape[2]
+    fill = jnp.zeros((rest // 2, inner_ref.shape[2]), F32)
+    parts = [outer_ref[j, 0], inner_ref[j], outer_ref[j, 1]]
+    return jnp.concatenate([fill] + [part.astype(F32) for part in parts] + [fill], axis=0)
+
+
+def relay_kernel(pair, *refs):
+    own, other, got_refs = refs[:3], refs[3:6], refs[6:8]
+    inner_ref, outer_ref = refs[8:]
+    cut = outer_ref.shape[2] // 2
+    size = inner_ref.shape[1]
+    wide = own[0].shape[1] + own[1].shape[2]
+
+    def run(upper, lower, half):
+        for j in range(inner_ref.shape[0]):
+            g = arrived(*got_refs, j, wide)
+            middle = backward(g, *factors(upper, j))[1].astype(F32)
+            d_in = backward(middle, *factors(lower, j))[2]
+            start = (wide - size) // 2
+            inner_ref[j] = d_in[start : start + size].astype(BF16)
+            outer_ref[j, 0] = d_in[start - 2 * cut : start].astype(BF16)
+            outer_ref[j, 1] = d_in[start + size : start + size + 2 * cut].astype(BF16)
+
+    by_half(pair, own, other, run)
 
 
 def chain_kernel(hops, *refs):
     own, other, top_refs = refs[:3], refs[3:6], refs[6:8]
-    got_refs = refs[8 : 8 + hops]
-    grad_ref, d_ref, send_ref, g_now = refs[8 + hops :]
+    got_refs = refs[8 : 8 + 2 * hops]
+    grad_ref, d_ref, send_ref, g_now = refs[8 + 2 * hops :]
     rows, wide = d_ref.shape[1], grad_ref.shape[1]
     pad = (wide - rows) // 2
     inner = slice(pad, pad + rows)
@@ -181,27 +247,26 @@
     @pl.when(section_id // 2 == hops)
     def _():
         for j in range(d_ref.shape[0]):
-            g_now[j] = top_gradient(*top_refs, j)
+            g_now[j] = top_gradient(*top_refs, j).astype(F32)
 
     for index in range(hops):
 
         @pl.when(section_id // 2 == hops - 1 - index)
         def _(index=index):
-            g_now[...] = got_refs[index][...]
-
-    for half in range(2):
-        upper, lower = (own, other) if half else (other, own)
-
-        @pl.when(section_id % 2 == half)
-        def _(upper=upper, lower=lower, half=half):
             for j in range(d_ref.shape[0]):
-                first = backward(g_now[j].astype(F32), *factors(upper, j))
-                second = backward(first[1].astype(F32), *factors(lower, j))
-                mine, away = (first, second) if half else (second, first)
-                grad_ref[j] = mine[0]
-                d_ref[j] = mine[1][inner]
-                send_ref[j, :wide] = away[0]
-                send_ref[j, wide:] = away[1][inner]
+                g_now[j] = arrived(*got_refs[2 * index : 2 * index + 2], j, wide)
+
+    def run(upper, lower, half):
+        for j in range(d_ref.shape[0]):
+            first = backward(g_now[j], *factors(upper, j))
+            second = backward(first[1].astype(F32), *factors(lower, j))
+            mine, away = (first, second) if half else (second, first)
+            grad_ref[j] = mine[0]
+            d_ref[j] = mine[1][inner]
+            send_ref[j, :wide] = away[0]
+            send_ref[j, wide:] = away[1][inner]
+
+    by_half(None, own, other, run)
 
 
 def split_rows(rows):
@@ -358,9 +423,13 @@
         + [shape_of(w_set.shape, BF16), picked, picked]
         + [half_main, half_main, shape_of(x.shape, F32)],
         [],
-        scalars=[doa_bins],
-        remote=[x, cotangent, w_set, gain_table, shift_table],
-        scratch=[pltpu.SemaphoreType.DMA((3 + 2 * micro,))],
+        remote=[doa_bins, x, cotangent, w_set, gain_table, shift_table],
+        scratch=[
+            pltpu.SMEM(doa_bins.shape, jnp.int32),
+            pltpu.VMEM(gain_table.shape, F32),
+            pltpu.VMEM(shift_table.shape, F32),
+            pltpu.SemaphoreType.DMA((5 + micro,)),
+        ],
         flops=matmul,
         limit=12,
     )
@@ -374,10 +443,7 @@
     keep_rim, send_rim, pre_rim, g_rim = call(
         rim_kernel,
         [half_rim, half_rim]
-        + [
-            shape_of((micro, 2, 2 * pad, channels), F32),
-            shape_of((count, 2, pad, channels), BF16),
-        ],
+        + [shape_of((micro, 2, 2 * pad, channels), F32), shape_of((count, 2, pad, channels), BF16)],
         [near, far, x, w_set, gain_rows, shift_rows],
         scratch=[pltpu.VMEM((2, 2, micro, pad, channels), BF16)],
         flops=matmul // 4,
@@ -386,21 +452,46 @@
     other_rim = to_other(send_rim)
     tables = [keep, keep_rim, w_set, other, other_rim, other_w]
 
-    sources = []
     half_wide = shape_of((count, wide, channels), BF16)
     hops = sections // 2 - 1
+    cut = 8 * -(-sections // 8)
+    inner_shape = shape_of((count, rows - 2 * cut, channels), BF16)
+    outer_shape = shape_of((count, 2, 2 * cut, channels), BF16)
+
+    def down(value, pair):
+        pairs = [(2 * pair + c, 2 * pair - 2 + c) for c in range(2)]
+        return lax.ppermute(value, "section", pairs + [(low, high) for high, low in pairs])
+
+    sources = []
     for hop in range(hops):
         pair = hops - hop
-        d_wide = call(
-            functools.partial(relay_kernel, pair),
-            half_wide,
-            tables + (sources[-1:] if hop else [cot, g_rim]),
+        if hop:
+            inner, outer_rows = call(
+                functools.partial(relay_kernel, pair),
+                [inner_shape, outer_shape],
+                tables + sources[-2:],
+                flops=matmul,
+                limit=8,
+            )
+            sources += [down(inner, pair), down(outer_rows, pair)]
+            continue
+        inner = call(
+            functools.partial(inner_kernel, pair),
+            inner_shape,
+            [keep, w_set, other, other_w, cot],
             flops=matmul,
             limit=8,
         )
-        down = [(2 * pair + c, 2 * pair - 2 + c) for c in range(2)]
-        pairs = down + [(target, source) for source, target in down]
-        sources.append(lax.ppermute(d_wide, "section", pairs))
+        inner = down(inner, pair)
+        outer_rows = call(
+            functools.partial(outer_kernel, pair),
+            outer_shape,
+            [keep_rim, w_set, other_rim, other_w, cot, g_rim],
+            flops=matmul // 2,
+            limit=8,
+        )
+        outer_rows = down(outer_rows, pair)
+        sources += [inner, outer_rows]
     grad_own, d_own, away = call(
         functools.partial(chain_kernel, hops),
         [
@@ -409,7 +500,7 @@
             shape_of((count, wide + rows, channels), BF16),
         ],
         tables + [cot, g_rim] + sources,
-        scratch=[pltpu.VMEM(half_wide.shape, BF16)],
+        scratch=[pltpu.VMEM(half_wide.shape, F32)],
         flops=matmul,
         limit=12,
     )
@@ -458,9 +549,7 @@
     spread = []
     for part in range(PARTS):
         done = call(
-            pair_kernel,
-            shape_of((chunk, channels), BF16),
-            list(summed[part]) + spread[-outer:][:1],
+            pair_kernel, shape_of((chunk, channels), BF16), list(summed[part]) + spread[-outer:][:1]
         )
         got = {k: across(done, k) for k in order}
         spread += [done] + [got[k] for k in range(1, outer)]

time: 61.1 us -> 54.7 us (0.90)
  waiting for transfers between devices: 24.6 us -> 16.7 us
  starting transfers between devices: 26.9 us -> 29.1 us
  local copies, waits for them, and re-layouts: 0.65 us -> 0.01 us
    ppermute x1 -> x2, waiting for transfers between devices: 7.32 us -> 1.9 us  [down(): lax.ppermute(value, 'section', pairs + [(low, high) for high, low in pairs])]
    ppermute x1, waiting for transfers between devices: 3.41 us -> 0.97 us  [step(): far = lax.ppermute(far, 'bulk', opposite)]
    ppermute x1 -> x2, starting transfers between devices: 2.51 us -> 4.63 us  [down(): lax.ppermute(value, 'section', pairs + [(low, high) for high, low in pairs])]
    unnamed x2, local copies, waits for them, and re-layouts: 0.65 us -> 0.01 us
    pallas_call x11 -> x12, Pallas kernels: 7.98 us -> 8.01 us  [call(): pl.pallas_call(kernel, in_specs=[smem] * len(scalars) + [kept] * len(remo...]
  transfers between devices with their start and end apart: 21 -> 22, of which waited for: 12 -> 12; matrix products, arithmetic and copies ran while one was open for 0% -> 0% of each run, Pallas kernels for 2% -> 2%
where the time goes in v2:
time: 54.7 us; the launch traced here: 54.5 us
  starting transfers between devices  29.1 us (53%)
  waiting for transfers between devices  16.7 us (31%)
  Pallas kernels  8.01 us (15%)
  between operations  0.72 us (1%)
    ppermute x12, starting transfers between devices, across(): return lax.ppermute(value, 'bulk', pairs)  15.4 us
    pallas_call x12, Pallas kernels, call(): pl.pallas_call(kernel, in_specs=[smem] * len(scalars) + [kept] * len(remo...  8.01 us
    ppermute x12, waiting for transfers between devices, across(): return lax.ppermute(value, 'bulk', pairs)  7.3 us
    ppermute x2, starting transfers between devices, down(): lax.ppermute(value, 'section', pairs + [(low, high) for high, low in pairs])  4.63 us
    ppermute x1, starting transfers between devices, step(): far = lax.ppermute(far, 'bulk', opposite)  3.54 us
    ppermute x4, waiting for transfers between devices, to_other(): return lax.ppermute(value, 'section', [(i, i ^ 1) for i in range(sections)])  3.28 us
    ppermute x2, waiting for transfers between devices, step(): summed.append((partial_sum, lax.ppermute(partial_sum, 'bulk', swap)))  3.25 us
    ppermute x1, starting transfers between devices, step(): near = lax.ppermute(near, 'bulk', [(i, i ^ 1) for i in range(bulk_count)])  3 us
  transfers between devices with their start and end apart: 22, of which 12 were waited for; matrix products, arithmetic and copies ran while one was open for 0% of the time, Pallas kernels for 2%

profile of v2, /device:TPU:0, one launch (start us, length us, event | category | flops | bytes accessed | tf_op | source)
XLA Modules:
  0.0 54.5 jit_solution(14375811328967671198)
XLA Ops:
  0.6 2.7 %shard_map.93 = (bf16[4,256,256]{2,1,0:T(8,128)(2,1)S(1)}, bf16[2,256,256]{2,1,0:T(8,128)(2,1)S(1)}, bf16[3,256,256]{2,1,0:T(8,128)(2,1)S(1)}, f32[4,1,256]{2,1,...) custom-call(s32[4]{0:T(128)} %bins.1, ...), custom_call_target="tpu_custom_call" | custom-call | flops 452984832 | bytes 1048576 | tf_op jit(solution)/shard_map/pallas_call | solution.py:380
  3.4 0.6 %collective-permute-start.2 = (f32[2,256,256]{2,1,0:T(8,128)S(1)}, f32[2,256,256]{2,1,0:T(8,128)S(1)}, u32[]{:S(2)}, u32[]{:S(2)}) collective-permute-start(f32[2,256,256]{2,1,0:T(8,128)S(1)} %get-tuple-element.43), channel_id=1, source_target_pairs={{0,8},{8,0},{16,24},{24,16},{1,9},{9,1},{17,25},{25,17},{2,10},{10... | collective-permute-start | bytes 1572872 | tf_op jit(solution)/shard_map/ppermute | solution.py:438
  3.9 0.1 collective-permute-start.4
  4.0 0.8 %shard_map.94 = (bf16[2,4,16,256]{3,2,1,0:T(8,128)(2,1)S(1)}, bf16[2,4,16,256]{3,2,1,0:T(8,128)(2,1)S(1)}) custom-call(bf16[4,256,256]{2,1,0:T(8,128)(2,1)} %bitcast.9, bf16[4,256,256]{2,1,0:T(8,128)(2,1)} %cot_ref.1), custom_call_target="tpu_custom_call" | custom-call | flops 1 | bytes 1048576 | tf_op jit(solution)/shard_map/pallas_call | solution.py:380
  4.9 3.0 %collective-permute-start = (bf16[2,4,16,256]{3,2,1,0:T(8,128)(2,1)S(1)}, bf16[2,4,16,256]{3,2,1,0:T(8,128)(2,1)S(1)}, u32[]{:S(2)}, u32[]{:S(2)}) collective-permute-start(bf16[2,4,16,256]{3,2,1,0:T(8,128)(2,1)S(1)} %get-tuple-element.35), channel_id=1, source_target_pairs={{0,1},{1,0},{2,3},{3,2},{4,5},{5,4},{6,7},{7,6},{8,9},{9,8},{10,11... | collective-permute-start | bytes 196616 | tf_op jit(solution)/shard_map/ppermute | solution.py:414
  7.9 3.5 %collective-permute-start.1 = (bf16[2,4,16,256]{3,2,1,0:T(8,128)(2,1)S(1)}, bf16[2,4,16,256]{3,2,1,0:T(8,128)(2,1)S(1)}, u32[]{:S(2)}, u32[]{:S(2)}) collective-permute-start(bf16[2,4,16,256]{3,2,1,0:T(8,128)(2,1)S(1)} %get-tuple-element.36), channel_id=1, source_target_pairs={{0,7},{1,2},{2,1},{3,4},{4,3},{5,6},{6,5},{7,0},{8,15},{9,10},{10,... | collective-permute-start | bytes 196616 | tf_op jit(solution)/shard_map/ppermute | solution.py:413
  11.4 0.0 collective-permute-done.4.refs_3_.refs_5_
  11.4 0.0 collective-permute-done.2.refs_2_.refs_3_
  11.4 2.4 %collective-permute-start.5 = (bf16[2,240,256]{2,1,0:T(8,128)(2,1)S(1)}, bf16[2,240,256]{2,1,0:T(8,128)(2,1)S(1)}, u32[]{:S(2)}, u32[]{:S(2)}) collective-permute-start(bf16[2,240,256]{2,1,0:T(8,128)(2,1)S(1)} %shard_map.96), channel_id=1, source_target_pairs={{16,0},{24,8},{0,16},{8,24},{17,1},{25,9},{1,17},{9,25},{18,2},{26... | collective-permute-start | bytes 737288 | tf_op jit(solution)/shard_map/ppermute | solution.py:463
  13.9 0.0 collective-permute-done.near_ref
  13.9 1.0 %collective-permute-done.1.far_ref = bf16[2,4,16,256]{3,2,1,0:T(8,128)(2,1)S(1)} collective-permute-done((bf16[2,4,16,256]{3,2,1,0:T(8,128)(2,1)S(1)}, bf16[2,4,16,256]{3,2,1,0:T(8,128)(2,1)S(1)}, u32[]{:S(2)}, u32[]{:S(2)}) %collective-permute-start.1) | collective-permute-done | bytes 65568 | tf_op jit(solution)/shard_map/ppermute | solution.py:413
  14.8 0.3 shard_map.95
  15.2 0.1 collective-permute-start.3
  15.2 1.3 %collective-permute-done.3.refs_2_.refs_4_ = f32[2,2,32,256]{3,2,1,0:T(8,128)S(1)} collective-permute-done((f32[2,2,32,256]{3,2,1,0:T(8,128)S(1)}, f32[2,2,32,256]{3,2,1,0:T(8,128)S(1)}, u32[]{:S(2)}, u32[]{:S(2)}) %collective-permute-start.3) | collective-permute-done | bytes 131104 | tf_op jit(solution)/shard_map/ppermute | solution.py:438
  16.6 2.2 %collective-permute-start.6 = (bf16[2,2,16,256]{3,2,1,0:T(8,128)(2,1)S(1)}, bf16[2,2,16,256]{3,2,1,0:T(8,128)(2,1)S(1)}, u32[]{:S(2)}, u32[]{:S(2)}) collective-permute-start(bf16[2,2,16,256]{3,2,1,0:T(8,128)(2,1)S(1)} %shard_map.97), channel_id=1, source_target_pairs={{16,0},{24,8},{0,16},{8,24},{17,1},{25,9},{1,17},{9,25},{18,2},{26... | collective-permute-start | bytes 98312 | tf_op jit(solution)/shard_map/ppermute | solution.py:463
  18.8 1.9 %collective-permute-done.6.refs_9_ = bf16[2,2,16,256]{3,2,1,0:T(8,128)(2,1)S(1)} collective-permute-done((bf16[2,2,16,256]{3,2,1,0:T(8,128)(2,1)S(1)}, bf16[2,2,16,256]{3,2,1,0:T(8,128)(2,1)S(1)}, u32[]{:S(2)}, u32[]{:S(2)}) %collective-permute-start.6) | collective-permute-done | bytes 32800 | tf_op jit(solution)/shard_map/ppermute | solution.py:463
  20.7 0.0 collective-permute-done.5.refs_8_
  20.7 1.0 %shard_map.98 = (bf16[2,288,256]{2,1,0:T(8,128)(2,1)S(1)}, bf16[2,256,256]{2,1,0:T(8,128)(2,1)S(1)}, bf16[2,544,256]{2,1,0:T(8,128)(2,1)S(1)}) custom-call(f32[2,256,256]{2,1,0:T(8,128)S(1)} %get-tuple-element.41.refs_0_, f32[2,2,32,256]{3,2,1,0:T(8,128)S(1)} %get-tuple-element.42.refs_0_.refs_1_, ...), custom_call_target="tpu_custom_call" | custom-call | flops 452984832 | bytes 1048576 | tf_op jit(solution)/shard_map/pallas_call | solution.py:380
  21.6 0.1 collective-permute-start.7
  21.7 1.9 %collective-permute-done.7.refs_6_ = bf16[2,544,256]{2,1,0:T(8,128)(2,1)S(1)} collective-permute-done((bf16[2,544,256]{2,1,0:T(8,128)(2,1)S(1)}, bf16[2,544,256]{2,1,0:T(8,128)(2,1)S(1)}, u32[]{:S(2)}, u32[]{:S(2)}) %collective-permute-start.7) | collective-permute-done | bytes 557088 | tf_op jit(solution)/shard_map/ppermute | solution.py:438
  23.7 1.5 %shard_map.99 = (bf16[4,256,256]{2,1,0:T(8,128)(2,1)}, f32[96,256]{1,0:T(8,128)S(1)}, f32[96,256]{1,0:T(8,128)S(1)}, bf16[112,256]{1,0:T(8,128)(2,1)S(1)}, bf16[...) custom-call(bf16[4,256,256]{2,1,0:T(8,128)(2,1)S(1)} %get-tuple-elem, ...), custom_call_target="tpu_custom_call" | custom-call | flops 452984832 | bytes 1048576 | tf_op jit(solution)/shard_map/pallas_call | solution.py:380
  25.2 0.8 %collective-permute-start.9 = (bf16[112,256]{1,0:T(8,128)(2,1)S(1)}, bf16[112,256]{1,0:T(8,128)(2,1)S(1)}, u32[]{:S(2)}, u32[]{:S(2)}) collective-permute-start(bf16[112,256]{1,0:T(8,128)(2,1)S(1)} %get-tuple-element.53), channel_id=1, source_target_pairs={{0,4},{1,5},{2,6},{3,7},{4,0},{5,1},{6,2},{7,3},{8,12},{9,13},{10,... | collective-permute-start | bytes 172040 | tf_op jit(solution)/shard_map/ppermute | solution.py:530
  26.0 1.3 %collective-permute-start.10 = (bf16[112,256]{1,0:T(8,128)(2,1)S(1)}, bf16[112,256]{1,0:T(8,128)(2,1)S(1)}, u32[]{:S(2)}, u32[]{:S(2)}) collective-permute-start(bf16[112,256]{1,0:T(8,128)(2,1)S(1)} %get-tuple-element.54), channel_id=1, source_target_pairs={{0,6},{1,7},{2,4},{3,5},{4,2},{5,3},{6,0},{7,1},{8,14},{9,15},{10,... | collective-permute-start | bytes 172040 | tf_op jit(solution)/shard_map/ppermute | solution.py:530
  27.3 1.3 %collective-permute-start.8 = (bf16[112,256]{1,0:T(8,128)(2,1)S(1)}, bf16[112,256]{1,0:T(8,128)(2,1)S(1)}, u32[]{:S(2)}, u32[]{:S(2)}) collective-permute-start(bf16[112,256]{1,0:T(8,128)(2,1)S(1)} %get-tuple-element.52.mine_ref), channel_id=1, source_target_pairs={{0,2},{1,3},{2,0},{3,1},{4,6},{5,7},{6,4},{7,5},{8,10},{9,11},{10,... | collective-permute-start | bytes 172040 | tf_op jit(solution)/shard_map/ppermute | solution.py:530
  28.7 1.7 %collective-permute-start.16 = (bf16[96,256]{1,0:T(8,128)(2,1)S(1)}, bf16[96,256]{1,0:T(8,128)(2,1)S(1)}, u32[]{:S(2)}, u32[]{:S(2)}) collective-permute-start(bf16[96,256]{1,0:T(8,128)(2,1)S(1)} %get-tuple-element.57), channel_id=1, source_target_pairs={{0,4},{1,5},{2,6},{3,7},{4,0},{5,1},{6,2},{7,3},{8,12},{9,13},{10,... | collective-permute-start | bytes 147464 | tf_op jit(solution)/shard_map/ppermute | solution.py:530
  30.4 1.3 %collective-permute-start.17 = (bf16[96,256]{1,0:T(8,128)(2,1)S(1)}, bf16[96,256]{1,0:T(8,128)(2,1)S(1)}, u32[]{:S(2)}, u32[]{:S(2)}) collective-permute-start(bf16[96,256]{1,0:T(8,128)(2,1)S(1)} %get-tuple-element.58), channel_id=1, source_target_pairs={{0,6},{1,7},{2,4},{3,5},{4,2},{5,3},{6,0},{7,1},{8,14},{9,15},{10,... | collective-permute-start | bytes 147464 | tf_op jit(solution)/shard_map/ppermute | solution.py:530
  31.7 1.0 %collective-permute-done.9.refs_1_ = bf16[112,256]{1,0:T(8,128)(2,1)S(1)} collective-permute-done((bf16[112,256]{1,0:T(8,128)(2,1)S(1)}, bf16[112,256]{1,0:T(8,128)(2,1)S(1)}, u32[]{:S(2)}, u32[]{:S(2)}) %collective-permute-start.9) | collective-permute-done | bytes 57376 | tf_op jit(solution)/shard_map/ppermute | solution.py:530
  32.7 0.0 collective-permute-start.15
  32.7 0.0 collective-permute-done.10.refs_2_
  32.7 0.3 collective-permute-done.8.refs_0_
  33.1 0.9 %collective-permute-start.11 = (bf16[112,256]{1,0:T(8,128)(2,1)S(1)}, bf16[112,256]{1,0:T(8,128)(2,1)S(1)}, u32[]{:S(2)}, u32[]{:S(2)}) collective-permute-start(bf16[112,256]{1,0:T(8,128)(2,1)S(1)} %shard_map.100.a_ref), channel_id=1, source_target_pairs={{0,1},{1,0},{2,3},{3,2},{4,5},{5,4},{6,7},{7,6},{8,9},{9,8},{10,11... | collective-permute-start | bytes 172040 | tf_op jit(solution)/shard_map/ppermute | solution.py:548
  34.0 2.6 %collective-permute-done.16.refs_1_ = bf16[96,256]{1,0:T(8,128)(2,1)S(1)} collective-permute-done((bf16[96,256]{1,0:T(8,128)(2,1)S(1)}, bf16[96,256]{1,0:T(8,128)(2,1)S(1)}, u32[]{:S(2)}, u32[]{:S(2)}) %collective-permute-start.16) | collective-permute-done | bytes 49184 | tf_op jit(solution)/shard_map/ppermute | solution.py:530
  36.5 0.0 collective-permute-done.17.refs_2_
  36.5 0.4 collective-permute-done.15.refs_0_
  37.0 0.9 %collective-permute-start.18 = (bf16[96,256]{1,0:T(8,128)(2,1)S(1)}, bf16[96,256]{1,0:T(8,128)(2,1)S(1)}, u32[]{:S(2)}, u32[]{:S(2)}) collective-permute-start(bf16[96,256]{1,0:T(8,128)(2,1)S(1)} %shard_map.102.a_ref), channel_id=1, source_target_pairs={{0,1},{1,0},{2,3},{3,2},{4,5},{5,4},{6,7},{7,6},{8,9},{9,8},{10,11... | collective-permute-start | bytes 147464 | tf_op jit(solution)/shard_map/ppermute | solution.py:548
  37.9 0.0 collective-permute-done.11.b_ref
  37.9 0.0 copy-start
  37.9 3.2 %collective-permute-done.18.b_ref = bf16[96,256]{1,0:T(8,128)(2,1)S(1)} collective-permute-done((bf16[96,256]{1,0:T(8,128)(2,1)S(1)}, bf16[96,256]{1,0:T(8,128)(2,1)S(1)}, u32[]{:S(2)}, u32[]{:S(2)}) %collective-permute-start.18) | collective-permute-done | bytes 49184 | tf_op jit(solution)/shard_map/ppermute | solution.py:548
  41.2 2.5 %collective-permute-start.21 = (bf16[96,256]{1,0:T(8,128)(2,1)S(1)}, bf16[96,256]{1,0:T(8,128)(2,1)S(1)}, u32[]{:S(2)}, u32[]{:S(2)}) collective-permute-start(bf16[96,256]{1,0:T(8,128)(2,1)S(1)} %shard_map.103.refs_4_), channel_id=1, source_target_pairs={{0,6},{1,7},{2,4},{3,5},{4,2},{5,3},{6,0},{7,1},{8,14},{9,15},{10,... | collective-permute-start | bytes 147464 | tf_op jit(solution)/shard_map/ppermute | solution.py:530
  43.6 0.0 collective-permute-start.20
  43.7 2.0 %collective-permute-start.19 = (bf16[96,256]{1,0:T(8,128)(2,1)S(1)}, bf16[96,256]{1,0:T(8,128)(2,1)S(1)}, u32[]{:S(2)}, u32[]{:S(2)}) collective-permute-start(bf16[96,256]{1,0:T(8,128)(2,1)S(1)} %shard_map.103.refs_4_), channel_id=1, source_target_pairs={{0,2},{1,3},{2,0},{3,1},{4,6},{5,7},{6,4},{7,5},{8,10},{9,11},{10,... | collective-permute-start | bytes 147464 | tf_op jit(solution)/shard_map/ppermute | solution.py:530
  45.6 2.4 %collective-permute-start.14 = (bf16[96,256]{1,0:T(8,128)(2,1)S(1)}, bf16[96,256]{1,0:T(8,128)(2,1)S(1)}, u32[]{:S(2)}, u32[]{:S(2)}) collective-permute-start(bf16[96,256]{1,0:T(8,128)(2,1)S(1)} %shard_map.101.refs_0_), channel_id=1, source_target_pairs={{0,6},{1,7},{2,4},{3,5},{4,2},{5,3},{6,0},{7,1},{8,14},{9,15},{10,... | collective-permute-start | bytes 147464 | tf_op jit(solution)/shard_map/ppermute | solution.py:530
  48.0 0.0 collective-permute-start.13
  48.0 0.0 collective-permute-done.21.refs_7_
  48.0 2.0 %collective-permute-start.12 = (bf16[96,256]{1,0:T(8,128)(2,1)S(1)}, bf16[96,256]{1,0:T(8,128)(2,1)S(1)}, u32[]{:S(2)}, u32[]{:S(2)}) collective-permute-start(bf16[96,256]{1,0:T(8,128)(2,1)S(1)} %shard_map.101.refs_0_), channel_id=1, source_target_pairs={{0,2},{1,3},{2,0},{3,1},{4,6},{5,7},{6,4},{7,5},{8,10},{9,11},{10,... | collective-permute-start | bytes 147464 | tf_op jit(solution)/shard_map/ppermute | solution.py:530
  50.0 0.3 collective-permute-done.20.refs_6_
  50.3 0.0 collective-permute-done.19.refs_5_
  50.3 1.2 %collective-permute-done.14.refs_3_ = bf16[96,256]{1,0:T(8,128)(2,1)S(1)} collective-permute-done((bf16[96,256]{1,0:T(8,128)(2,1)S(1)}, bf16[96,256]{1,0:T(8,128)(2,1)S(1)}, u32[]{:S(2)}, u32[]{:S(2)}) %collective-permute-start.14) | collective-permute-done | bytes 49184 | tf_op jit(solution)/shard_map/ppermute | solution.py:530
  51.5 1.5 %collective-permute-done.13.refs_2_ = bf16[96,256]{1,0:T(8,128)(2,1)S(1)} collective-permute-done((bf16[96,256]{1,0:T(8,128)(2,1)S(1)}, bf16[96,256]{1,0:T(8,128)(2,1)S(1)}, u32[]{:S(2)}, u32[]{:S(2)}) %collective-permute-start.13) | collective-permute-done | bytes 49184 | tf_op jit(solution)/shard_map/ppermute | solution.py:530
  53.0 0.0 collective-permute-done.12.refs_1_
  53.0 0.0 copy-done
  53.0 1.5 %shard_map.104 = (f32[768,256]{1,0:T(8,128)}, f32[36,1,256]{2,1,0:T(1,128)}, f32[36,1,256]{2,1,0:T(1,128)}) custom-call(s32[4]{0:T(128)S(1)} %copy-done, bf16[112,256]{1,0:T(8,128)(2,1)S(1)} %shard_map.100.a_ref, bf16[112,256]{1,0:T(8,128)(2,1)S(1)} %collective-permute-done.11.b_ref, bf16[96,256]{1,0:T(8,128)(2,1)S(1)} %shard_map.101.refs_0_, ...), custom_call_target="tpu_custom_call" | custom-call | flops 1 | bytes 1048576 | tf_op jit(solution)/shard_map/pallas_call | solution.py:380
  (6 shorter events, 0.1 us)
Async XLA Ops:
  3.4 8.0 %collective-permute-start.2 = (f32[2,256,256]{2,1,0:T(8,128)S(1)}, f32[2,256,256]{2,1,0:T(8,128)S(1)}, u32[]{:S(2)}, u32[]{:S(2)}) collective-permute-start(f32[2,256,256]{2,1,0:T(8,128)S(1)} %get-tuple-element.43), channel_id=1, source_target_pairs={{0,8},{8,0},{16,24},{24,16},{1,9},{9,1},{17,25},{25,17},{2,10},{10... | collective-permute-start | bytes 1572872 | tf_op jit(solution)/shard_map/ppermute | solution.py:438
  3.9 7.5 %collective-permute-start.4 = (bf16[3,256,256]{2,1,0:T(8,128)(2,1)S(1)}, bf16[3,256,256]{2,1,0:T(8,128)(2,1)S(1)}, u32[]{:S(2)}, u32[]{:S(2)}) collective-permute-start(bf16[3,256,256]{2,1,0:T(8,128)(2,1)S(1)} %get-tuple-element.37.w_ref.refs_1_.refs_2_), channel_id=1, source_target_pairs={{0,8},{8,0},{16,24},{24,16},{1,9},{9,1},{17,25},{25,17},{2,10},{10... | collective-permute-start | bytes 1179656 | tf_op jit(solution)/shard_map/ppermute | solution.py:438
  4.9 9.0 %collective-permute-start = (bf16[2,4,16,256]{3,2,1,0:T(8,128)(2,1)S(1)}, bf16[2,4,16,256]{3,2,1,0:T(8,128)(2,1)S(1)}, u32[]{:S(2)}, u32[]{:S(2)}) collective-permute-start(bf16[2,4,16,256]{3,2,1,0:T(8,128)(2,1)S(1)} %get-tuple-element.35), channel_id=1, source_target_pairs={{0,1},{1,0},{2,3},{3,2},{4,5},{5,4},{6,7},{7,6},{8,9},{9,8},{10,11... | collective-permute-start | bytes 196616 | tf_op jit(solution)/shard_map/ppermute | solution.py:414
  7.9 7.0 %collective-permute-start.1 = (bf16[2,4,16,256]{3,2,1,0:T(8,128)(2,1)S(1)}, bf16[2,4,16,256]{3,2,1,0:T(8,128)(2,1)S(1)}, u32[]{:S(2)}, u32[]{:S(2)}) collective-permute-start(bf16[2,4,16,256]{3,2,1,0:T(8,128)(2,1)S(1)} %get-tuple-element.36), channel_id=1, source_target_pairs={{0,7},{1,2},{2,1},{3,4},{4,3},{5,6},{6,5},{7,0},{8,15},{9,10},{10,... | collective-permute-start | bytes 196616 | tf_op jit(solution)/shard_map/ppermute | solution.py:413
  11.4 9.2 %collective-permute-start.5 = (bf16[2,240,256]{2,1,0:T(8,128)(2,1)S(1)}, bf16[2,240,256]{2,1,0:T(8,128)(2,1)S(1)}, u32[]{:S(2)}, u32[]{:S(2)}) collective-permute-start(bf16[2,240,256]{2,1,0:T(8,128)(2,1)S(1)} %shard_map.96), channel_id=1, source_target_pairs={{16,0},{24,8},{0,16},{8,24},{17,1},{25,9},{1,17},{9,25},{18,2},{26... | collective-permute-start | bytes 737288 | tf_op jit(solution)/shard_map/ppermute | solution.py:463
  15.2 1.4 %collective-permute-start.3 = (f32[2,2,32,256]{3,2,1,0:T(8,128)S(1)}, f32[2,2,32,256]{3,2,1,0:T(8,128)S(1)}, u32[]{:S(2)}, u32[]{:S(2)}) collective-permute-start(f32[2,2,32,256]{3,2,1,0:T(8,128)S(1)} %get-tuple-element.44), channel_id=1, source_target_pairs={{0,8},{8,0},{16,24},{24,16},{1,9},{9,1},{17,25},{25,17},{2,10},{10... | collective-permute-start | bytes 393224 | tf_op jit(solution)/shard_map/ppermute | solution.py:438
  16.6 4.1 %collective-permute-start.6 = (bf16[2,2,16,256]{3,2,1,0:T(8,128)(2,1)S(1)}, bf16[2,2,16,256]{3,2,1,0:T(8,128)(2,1)S(1)}, u32[]{:S(2)}, u32[]{:S(2)}) collective-permute-start(bf16[2,2,16,256]{3,2,1,0:T(8,128)(2,1)S(1)} %shard_map.97), channel_id=1, source_target_pairs={{16,0},{24,8},{0,16},{8,24},{17,1},{25,9},{1,17},{9,25},{18,2},{26... | collective-permute-start | bytes 98312 | tf_op jit(solution)/shard_map/ppermute | solution.py:463
  21.6 2.0 %collective-permute-start.7 = (bf16[2,544,256]{2,1,0:T(8,128)(2,1)S(1)}, bf16[2,544,256]{2,1,0:T(8,128)(2,1)S(1)}, u32[]{:S(2)}, u32[]{:S(2)}) collective-permute-start(bf16[2,544,256]{2,1,0:T(8,128)(2,1)S(1)} %get-tuple-element.49), channel_id=1, source_target_pairs={{0,8},{8,0},{16,24},{24,16},{1,9},{9,1},{17,25},{25,17},{2,10},{10... | collective-permute-start | bytes 1671176 | tf_op jit(solution)/shard_map/ppermute | solution.py:438
  25.2 7.5 %collective-permute-start.9 = (bf16[112,256]{1,0:T(8,128)(2,1)S(1)}, bf16[112,256]{1,0:T(8,128)(2,1)S(1)}, u32[]{:S(2)}, u32[]{:S(2)}) collective-permute-start(bf16[112,256]{1,0:T(8,128)(2,1)S(1)} %get-tuple-element.53), channel_id=1, source_target_pairs={{0,4},{1,5},{2,6},{3,7},{4,0},{5,1},{6,2},{7,3},{8,12},{9,13},{10,... | collective-permute-start | bytes 172040 | tf_op jit(solution)/shard_map/ppermute | solution.py:530
  26.0 6.7 %collective-permute-start.10 = (bf16[112,256]{1,0:T(8,128)(2,1)S(1)}, bf16[112,256]{1,0:T(8,128)(2,1)S(1)}, u32[]{:S(2)}, u32[]{:S(2)}) collective-permute-start(bf16[112,256]{1,0:T(8,128)(2,1)S(1)} %get-tuple-element.54), channel_id=1, source_target_pairs={{0,6},{1,7},{2,4},{3,5},{4,2},{5,3},{6,0},{7,1},{8,14},{9,15},{10,... | collective-permute-start | bytes 172040 | tf_op jit(solution)/shard_map/ppermute | solution.py:530
  27.3 5.7 %collective-permute-start.8 = (bf16[112,256]{1,0:T(8,128)(2,1)S(1)}, bf16[112,256]{1,0:T(8,128)(2,1)S(1)}, u32[]{:S(2)}, u32[]{:S(2)}) collective-permute-start(bf16[112,256]{1,0:T(8,128)(2,1)S(1)} %get-tuple-element.52.mine_ref), channel_id=1, source_target_pairs={{0,2},{1,3},{2,0},{3,1},{4,6},{5,7},{6,4},{7,5},{8,10},{9,11},{10,... | collective-permute-start | bytes 172040 | tf_op jit(solution)/shard_map/ppermute | solution.py:530
  28.7 7.9 %collective-permute-start.16 = (bf16[96,256]{1,0:T(8,128)(2,1)S(1)}, bf16[96,256]{1,0:T(8,128)(2,1)S(1)}, u32[]{:S(2)}, u32[]{:S(2)}) collective-permute-start(bf16[96,256]{1,0:T(8,128)(2,1)S(1)} %get-tuple-element.57), channel_id=1, source_target_pairs={{0,4},{1,5},{2,6},{3,7},{4,0},{5,1},{6,2},{7,3},{8,12},{9,13},{10,... | collective-permute-start | bytes 147464 | tf_op jit(solution)/shard_map/ppermute | solution.py:530
  30.4 6.2 %collective-permute-start.17 = (bf16[96,256]{1,0:T(8,128)(2,1)S(1)}, bf16[96,256]{1,0:T(8,128)(2,1)S(1)}, u32[]{:S(2)}, u32[]{:S(2)}) collective-permute-start(bf16[96,256]{1,0:T(8,128)(2,1)S(1)} %get-tuple-element.58), channel_id=1, source_target_pairs={{0,6},{1,7},{2,4},{3,5},{4,2},{5,3},{6,0},{7,1},{8,14},{9,15},{10,... | collective-permute-start | bytes 147464 | tf_op jit(solution)/shard_map/ppermute | solution.py:530
  32.7 4.3 %collective-permute-start.15 = (bf16[96,256]{1,0:T(8,128)(2,1)S(1)}, bf16[96,256]{1,0:T(8,128)(2,1)S(1)}, u32[]{:S(2)}, u32[]{:S(2)}) collective-permute-start(bf16[96,256]{1,0:T(8,128)(2,1)S(1)} %get-tuple-element.56.mine_ref), channel_id=1, source_target_pairs={{0,2},{1,3},{2,0},{3,1},{4,6},{5,7},{6,4},{7,5},{8,10},{9,11},{10,... | collective-permute-start | bytes 147464 | tf_op jit(solution)/shard_map/ppermute | solution.py:530
  33.1 4.8 %collective-permute-start.11 = (bf16[112,256]{1,0:T(8,128)(2,1)S(1)}, bf16[112,256]{1,0:T(8,128)(2,1)S(1)}, u32[]{:S(2)}, u32[]{:S(2)}) collective-permute-start(bf16[112,256]{1,0:T(8,128)(2,1)S(1)} %shard_map.100.a_ref), channel_id=1, source_target_pairs={{0,1},{1,0},{2,3},{3,2},{4,5},{5,4},{6,7},{7,6},{8,9},{9,8},{10,11... | collective-permute-start | bytes 172040 | tf_op jit(solution)/shard_map/ppermute | solution.py:548
  37.0 4.2 %collective-permute-start.18 = (bf16[96,256]{1,0:T(8,128)(2,1)S(1)}, bf16[96,256]{1,0:T(8,128)(2,1)S(1)}, u32[]{:S(2)}, u32[]{:S(2)}) collective-permute-start(bf16[96,256]{1,0:T(8,128)(2,1)S(1)} %shard_map.102.a_ref), channel_id=1, source_target_pairs={{0,1},{1,0},{2,3},{3,2},{4,5},{5,4},{6,7},{7,6},{8,9},{9,8},{10,11... | collective-permute-start | bytes 147464 | tf_op jit(solution)/shard_map/ppermute | solution.py:548
  37.9 15.1 %copy-start = (s32[4]{0:T(128)S(1)}, s32[4]{0:T(128)}, u32[]{:S(2)}) copy-start(s32[4]{0:T(128)} %bins.1) | copy-start | bytes 52
  41.2 6.8 %collective-permute-start.21 = (bf16[96,256]{1,0:T(8,128)(2,1)S(1)}, bf16[96,256]{1,0:T(8,128)(2,1)S(1)}, u32[]{:S(2)}, u32[]{:S(2)}) collective-permute-start(bf16[96,256]{1,0:T(8,128)(2,1)S(1)} %shard_map.103.refs_4_), channel_id=1, source_target_pairs={{0,6},{1,7},{2,4},{3,5},{4,2},{5,3},{6,0},{7,1},{8,14},{9,15},{10,... | collective-permute-start | bytes 147464 | tf_op jit(solution)/shard_map/ppermute | solution.py:530
  43.6 6.7 %collective-permute-start.20 = (bf16[96,256]{1,0:T(8,128)(2,1)S(1)}, bf16[96,256]{1,0:T(8,128)(2,1)S(1)}, u32[]{:S(2)}, u32[]{:S(2)}) collective-permute-start(bf16[96,256]{1,0:T(8,128)(2,1)S(1)} %shard_map.103.refs_4_), channel_id=1, source_target_pairs={{0,4},{1,5},{2,6},{3,7},{4,0},{5,1},{6,2},{7,3},{8,12},{9,13},{10,... | collective-permute-start | bytes 147464 | tf_op jit(solution)/shard_map/ppermute | solution.py:530
  43.7 6.6 %collective-permute-start.19 = (bf16[96,256]{1,0:T(8,128)(2,1)S(1)}, bf16[96,256]{1,0:T(8,128)(2,1)S(1)}, u32[]{:S(2)}, u32[]{:S(2)}) collective-permute-start(bf16[96,256]{1,0:T(8,128)(2,1)S(1)} %shard_map.103.refs_4_), channel_id=1, source_target_pairs={{0,2},{1,3},{2,0},{3,1},{4,6},{5,7},{6,4},{7,5},{8,10},{9,11},{10,... | collective-permute-start | bytes 147464 | tf_op jit(solution)/shard_map/ppermute | solution.py:530
  45.6 5.9 %collective-permute-start.14 = (bf16[96,256]{1,0:T(8,128)(2,1)S(1)}, bf16[96,256]{1,0:T(8,128)(2,1)S(1)}, u32[]{:S(2)}, u32[]{:S(2)}) collective-permute-start(bf16[96,256]{1,0:T(8,128)(2,1)S(1)} %shard_map.101.refs_0_), channel_id=1, source_target_pairs={{0,6},{1,7},{2,4},{3,5},{4,2},{5,3},{6,0},{7,1},{8,14},{9,15},{10,... | collective-permute-start | bytes 147464 | tf_op jit(solution)/shard_map/ppermute | solution.py:530
  48.0 5.0 %collective-permute-start.13 = (bf16[96,256]{1,0:T(8,128)(2,1)S(1)}, bf16[96,256]{1,0:T(8,128)(2,1)S(1)}, u32[]{:S(2)}, u32[]{:S(2)}) collective-permute-start(bf16[96,256]{1,0:T(8,128)(2,1)S(1)} %shard_map.101.refs_0_), channel_id=1, source_target_pairs={{0,4},{1,5},{2,6},{3,7},{4,0},{5,1},{6,2},{7,3},{8,12},{9,13},{10,... | collective-permute-start | bytes 147464 | tf_op jit(solution)/shard_map/ppermute | solution.py:530
  48.0 5.0 %collective-permute-start.12 = (bf16[96,256]{1,0:T(8,128)(2,1)S(1)}, bf16[96,256]{1,0:T(8,128)(2,1)S(1)}, u32[]{:S(2)}, u32[]{:S(2)}) collective-permute-start(bf16[96,256]{1,0:T(8,128)(2,1)S(1)} %shard_map.101.refs_0_), channel_id=1, source_target_pairs={{0,2},{1,3},{2,0},{3,1},{4,6},{5,7},{6,4},{7,5},{8,10},{9,11},{10,... | collective-permute-start | bytes 147464 | tf_op jit(solution)/shard_map/ppermute | solution.py:530

commit v3 on v2

--- a/solution.py
+++ b/solution.py
@@ -31,19 +31,28 @@
     return started
 
 
-def edge_kernel(x_ref, cot_ref, near_ref, far_ref, sems):
-    rows = x_ref.shape[1]
-    pad = near_ref.shape[2]
+def load_kernel(bins_in, x_in, cot_in, w_in, gain_in, shift_in, *refs):
+    near_ref, far_ref, x_ref, cot_ref, w_ref, gain_ref, shift_ref = refs[:7]
+    bins, gains, shifts, sems = refs[7:]
+    micro, rows = x_ref.shape[:2]
+    count = micro // 2
+    pad = near_ref.shape[1]
     odd = lax.axis_index("bulk") % 2
-    last = rows - pad
-    near = pl.multiple_of((1 - odd) * last, pad)
-    far = pl.multiple_of(odd * last, pad)
-    pairs = []
-    for index, ref in enumerate((x_ref, cot_ref)):
-        pairs.append((ref.at[:, pl.ds(near, pad), :], near_ref.at[index]))
-        pairs.append((ref.at[:, pl.ds(far, pad), :], far_ref.at[index]))
-    for copy in copies(pairs, sems):
+    mine = cot_in.at[pl.ds(lax.axis_index("section") % 2 * count, count)]
+    pairs = [(x_in, x_ref), (mine, cot_ref), (bins_in, bins), (gain_in, gains)]
+    started = copies(pairs + [(shift_in, shifts), (w_in, w_ref)], sems)
+    for copy in started[:2]:
         copy.wait()
+    near = pl.multiple_of((1 - odd) * (rows - pad), pad)
+    far = pl.multiple_of(odd * (rows - pad), pad)
+    for out, start in ((near_ref, near), (far_ref, far)):
+        out[:micro] = x_ref[:, pl.ds(start, pad), :]
+        out[micro:] = cot_ref[:, pl.ds(start, pad), :]
+    for copy in started[2:]:
+        copy.wait()
+    for m in range(micro):
+        gain_ref[m] = gains[bins[m]]
+        shift_ref[m] = shifts[bins[m]]
 
 
 def slopes(filmed):
@@ -63,34 +72,20 @@
     return [start * (micro // 2) + j for j in range(micro // 2)]
 
 
-def forward_kernel(bins_in, x_in, cot_in, w_in, gain_in, shift_in, *refs):
-    x_ref, cot_ref, w_ref, gain_ref, shift_ref, keep_ref, send_ref, pre_ref = refs[:8]
-    bins, gains, shifts, sems = refs[8:]
+def forward_kernel(x_ref, w_ref, gain_ref, shift_ref, send_ref, keep_ref, pre_ref):
     micro = x_ref.shape[0]
     half = lax.axis_index("section") % 2
-    order = turn(half, micro, 1) + turn(half, micro, 0)
-    pairs = [(bins_in, bins), (gain_in, gains), (shift_in, shifts), (w_in, w_ref)]
-    pairs += [(x_in.at[m], x_ref.at[m]) for m in order]
-    mine = cot_in.at[pl.ds(half * (micro // 2), micro // 2)]
-    started = copies(pairs + [(mine, cot_ref)], sems)
-    for copy in started[:4]:
-        copy.wait()
-    for m in range(micro):
-        gain_ref[m] = gains[bins[m]]
-        shift_ref[m] = shifts[bins[m]]
-    for index, m in enumerate(order):
-        started[4 + index].wait()
-        out = (send_ref, keep_ref)[index // (micro // 2)]
-        pre = taps(x_ref[m], w_ref)
-        out[index % (micro // 2)] = slopes(pre * gain_ref[m] + shift_ref[m]) * gain_ref[m]
-        pre_ref[m] = pre
-    started[-1].wait()
+    for place, out in ((1, send_ref), (0, keep_ref)):
+        for j, m in enumerate(turn(half, micro, place)):
+            pre = taps(x_ref[m], w_ref)
+            out[j] = slopes(pre * gain_ref[m] + shift_ref[m]) * gain_ref[m]
+            pre_ref[m] = pre
 
 
 def rim_kernel(near_ref, far_ref, x_ref, w_ref, gain_ref, shift_ref, *refs):
     keep_ref, send_ref, pre_ref, g_ref, halo = refs
     micro, rows = x_ref.shape[:2]
-    pad = near_ref.shape[2]
+    pad = near_ref.shape[1]
     odd = lax.axis_index("bulk") % 2
     half = lax.axis_index("section") % 2
 
@@ -107,10 +102,10 @@
     parts = []
     order = turn(half, micro, 0) + turn(half, micro, 1)
     for m in order:
-        parts += [halo[0, 0, m], x_ref[m, :pad], x_ref[m, rows - pad :], halo[1, 0, m]]
-    for j, m in enumerate(turn(half, micro, 0)):
-        g_ref[j, 0] = halo[0, 1, m]
-        g_ref[j, 1] = halo[1, 1, m]
+        parts += [halo[0, m], x_ref[m, :pad], x_ref[m, rows - pad :], halo[1, m]]
+    for j in range(micro // 2):
+        g_ref[j, 0] = halo[0, micro + j]
+        g_ref[j, 1] = halo[1, micro + j]
     pre = taps(jnp.concatenate(parts, axis=0), w_ref)
     for index, m in enumerate(order):
         out = (keep_ref, send_ref)[index // (micro // 2)]
@@ -401,37 +396,38 @@
     pad = 16 * -(-(sections + 1) // 16)
     wide = rows + 2 * pad
 
-    edges = shape_of((2, micro, pad, channels), BF16)
-    near, far = call(
-        edge_kernel,
-        [edges, edges],
-        [],
-        remote=[x, cotangent],
-        scratch=[pltpu.SemaphoreType.DMA((4,))],
-    )
-    opposite = [(i, (i + 1 if i % 2 else i - 1) % bulk_count) for i in range(bulk_count)]
-    far = lax.ppermute(far, "bulk", opposite)
-    near = lax.ppermute(near, "bulk", [(i, i ^ 1) for i in range(bulk_count)])
-
-    matmul = 2 * 3 * micro * wide * channels * channels
+    count = micro // 2
+    edges = shape_of((micro + count, pad, channels), BF16)
     picked = shape_of((micro, 1, channels), F32)
-    count = micro // 2
-    half_main = shape_of((count, rows, channels), F32)
-    x, cot, w_set, gain_rows, shift_rows, keep, send, pre = call(
-        forward_kernel,
-        [shape_of(x.shape, BF16), shape_of((count, rows, channels), BF16)]
-        + [shape_of(w_set.shape, BF16), picked, picked]
-        + [half_main, half_main, shape_of(x.shape, F32)],
+    near, far, x, cot, w_set, gain_rows, shift_rows = call(
+        load_kernel,
+        [edges, edges, shape_of(x.shape, BF16), shape_of((count, rows, channels), BF16)]
+        + [shape_of(w_set.shape, BF16), picked, picked],
         [],
         remote=[doa_bins, x, cotangent, w_set, gain_table, shift_table],
         scratch=[
             pltpu.SMEM(doa_bins.shape, jnp.int32),
             pltpu.VMEM(gain_table.shape, F32),
             pltpu.VMEM(shift_table.shape, F32),
-            pltpu.SemaphoreType.DMA((5 + micro,)),
+            pltpu.SemaphoreType.DMA((6,)),
         ],
+        limit=8,
+    )
+    opposite = [(i, (i + 1 if i % 2 else i - 1) % bulk_count) for i in range(bulk_count)]
+    far = lax.ppermute(far, "bulk", opposite)
+    near = lax.ppermute(near, "bulk", [(i, i ^ 1) for i in range(bulk_count)])
+
+    matmul = 2 * 3 * micro * wide * channels * channels
+    picked = shape_of((micro, 1, channels), F32)
+    count = micro // 2
+    half_main = shape_of((count, rows, channels), F32)
+    half_main = shape_of((count, rows, channels), F32)
+    send, keep, pre = call(
+        forward_kernel,
+        [half_main, half_main, shape_of(x.shape, F32)],
+        [x, w_set, gain_rows, shift_rows],
         flops=matmul,
-        limit=12,
+        limit=8,
     )
 
     def to_other(value):
@@ -445,7 +441,7 @@
         [half_rim, half_rim]
         + [shape_of((micro, 2, 2 * pad, channels), F32), shape_of((count, 2, pad, channels), BF16)],
         [near, far, x, w_set, gain_rows, shift_rows],
-        scratch=[pltpu.VMEM((2, 2, micro, pad, channels), BF16)],
+        scratch=[pltpu.VMEM((2, *edges.shape), BF16)],
         flops=matmul // 4,
         limit=8,
     )

time: 54.7 us -> 57.3 us (1.048)
  waiting for transfers between devices: 16.7 us -> 22.3 us
  starting transfers between devices: 29.1 us -> 27.5 us
  Pallas kernels: 8.01 us -> 6.68 us
    ppermute x1, waiting for transfers between devices: 0.97 us -> 3.24 us  [step(): far = lax.ppermute(far, 'bulk', opposite)]
    ppermute x4, waiting for transfers between devices: 3.28 us -> 5.3 us  [to_other(): return lax.ppermute(value, 'section', [(i, i ^ 1) for i in range(sections)])]
    ppermute x1, starting transfers between devices: 3 us -> 1.52 us  [step(): near = lax.ppermute(near, 'bulk', [(i, i ^ 1) for i in range(bulk_count)])]
    pallas_call x12, Pallas kernels: 8.01 us -> 6.68 us  [call(): pl.pallas_call(kernel, in_specs=[smem] * len(scalars) + [kept] * len(remo...]
    ppermute x2, waiting for transfers between devices: 1.9 us -> 3.15 us  [down(): lax.ppermute(value, 'section', pairs + [(low, high) for high, low in pairs])]
  transfers between devices with their start and end apart: 22 -> 22, of which waited for: 12 -> 13; matrix products, arithmetic and copies ran while one was open for 0% -> 0% of each run, Pallas kernels for 2% -> 1%
where the time goes in v3:
time: 57.3 us; the launch traced here: 57.2 us
  starting transfers between devices  27.5 us (48%)
  waiting for transfers between devices  22.3 us (39%)
  Pallas kernels  6.68 us (12%)
  between operations  0.72 us (1%)
    ppermute x12, starting transfers between devices, across(): return lax.ppermute(value, 'bulk', pairs)  15.4 us
    ppermute x12, waiting for transfers between devices, across(): return lax.ppermute(value, 'bulk', pairs)  7.36 us
    pallas_call x12, Pallas kernels, call(): pl.pallas_call(kernel, in_specs=[smem] * len(scalars) + [kept] * len(remo...  6.68 us
    ppermute x4, waiting for transfers between devices, to_other(): return lax.ppermute(value, 'section', [(i, i ^ 1) for i in range(sections)])  5.3 us
    ppermute x2, starting transfers between devices, down(): lax.ppermute(value, 'section', pairs + [(low, high) for high, low in pairs])  4.55 us
    ppermute x1, starting transfers between devices, step(): far = lax.ppermute(far, 'bulk', opposite)  3.54 us
    ppermute x2, waiting for transfers between devices, step(): summed.append((partial_sum, lax.ppermute(partial_sum, 'bulk', swap)))  3.26 us
    ppermute x1, waiting for transfers between devices, step(): far = lax.ppermute(far, 'bulk', opposite)  3.24 us
  transfers between devices with their start and end apart: 22, of which 13 were waited for; matrix products, arithmetic and copies ran while one was open for 0% of the time, Pallas kernels for 1%

profile of v3, /device:TPU:0, one launch (start us, length us, event | category | flops | bytes accessed | tf_op | source)
XLA Modules:
  0.0 57.2 jit_solution(3890478121127892423)
XLA Ops:
  0.6 1.3 %shard_map.93 = (bf16[6,16,256]{2,1,0:T(8,128)(2,1)S(1)}, bf16[6,16,256]{2,1,0:T(8,128)(2,1)S(1)}, bf16[4,256,256]{2,1,0:T(8,128)(2,1)S(1)}, bf16[2,256,256]{2,1...) custom-call(s32[4]{0:T(128)} %bins.1, ...), custom_call_target="tpu_custom_call" | custom-call | flops 1 | bytes 1048576 | tf_op jit(solution)/shard_map/pallas_call | solution.py:375
  2.0 0.9 %shard_map.94 = (f32[2,256,256]{2,1,0:T(8,128)S(1)}, f32[2,256,256]{2,1,0:T(8,128)S(1)}, f32[4,256,256]{2,1,0:T(8,128)S(1)}) custom-call(bf16[4,256,256]{2,1,0:T(8,128)(2,1)S(1)} %get-tuple-element.33.x_ref.refs_0_, bf16[3,256,256]{2,1,0:T(8,128)(2,1)S(1)} %get-tuple-element.34.w_ref.refs_1_.refs_2_, f32[4,1,256]{2,1,0:T(1,128)S(1)} %get-tuple-element.35.gain_ref.refs_3_, ...), custom_call_target="tpu_custom_call" | custom-call | flops 452984832 | bytes 1048576 | tf_op jit(solution)/shard_map/pallas_call | solution.py:375
  2.9 0.6 collective-permute-start.2
  3.4 0.1 collective-permute-start.4
  3.5 2.0 %collective-permute-done.4.refs_3_.refs_5_ = bf16[3,256,256]{2,1,0:T(8,128)(2,1)S(1)} collective-permute-done((bf16[3,256,256]{2,1,0:T(8,128)(2,1)S(1)}, bf16[3,256,256]{2,1,0:T(8,128)(2,1)S(1)}, u32[]{:S(2)}, u32[]{:S(2)}) %collective-permute-start.4) | collective-permute-done | bytes 393248 | tf_op jit(solution)/shard_map/ppermute | solution.py:434
  5.5 0.0 collective-permute-done.2.refs_2_.refs_3_
  5.5 3.8 %collective-permute-start.5 = (bf16[2,240,256]{2,1,0:T(8,128)(2,1)S(1)}, bf16[2,240,256]{2,1,0:T(8,128)(2,1)S(1)}, u32[]{:S(2)}, u32[]{:S(2)}) collective-permute-start(bf16[2,240,256]{2,1,0:T(8,128)(2,1)S(1)} %shard_map.96), channel_id=1, source_target_pairs={{16,0},{24,8},{0,16},{8,24},{17,1},{25,9},{1,17},{9,25},{18,2},{26... | collective-permute-start | bytes 737288 | tf_op jit(solution)/shard_map/ppermute | solution.py:459
  9.3 1.5 %collective-permute-start = (bf16[6,16,256]{2,1,0:T(8,128)(2,1)S(1)}, bf16[6,16,256]{2,1,0:T(8,128)(2,1)S(1)}, u32[]{:S(2)}, u32[]{:S(2)}) collective-permute-start(bf16[6,16,256]{2,1,0:T(8,128)(2,1)S(1)} %get-tuple-element.38), channel_id=1, source_target_pairs={{0,1},{1,0},{2,3},{3,2},{4,5},{5,4},{6,7},{7,6},{8,9},{9,8},{10,11... | collective-permute-start | bytes 147464 | tf_op jit(solution)/shard_map/ppermute | solution.py:418
  10.9 3.5 %collective-permute-start.1 = (bf16[6,16,256]{2,1,0:T(8,128)(2,1)S(1)}, bf16[6,16,256]{2,1,0:T(8,128)(2,1)S(1)}, u32[]{:S(2)}, u32[]{:S(2)}) collective-permute-start(bf16[6,16,256]{2,1,0:T(8,128)(2,1)S(1)} %get-tuple-element.39), channel_id=1, source_target_pairs={{0,7},{1,2},{2,1},{3,4},{4,3},{5,6},{6,5},{7,0},{8,15},{9,10},{10,... | collective-permute-start | bytes 147464 | tf_op jit(solution)/shard_map/ppermute | solution.py:417
  14.4 0.0 collective-permute-done.near_ref
  14.4 3.2 %collective-permute-done.1.far_ref = bf16[6,16,256]{2,1,0:T(8,128)(2,1)S(1)} collective-permute-done((bf16[6,16,256]{2,1,0:T(8,128)(2,1)S(1)}, bf16[6,16,256]{2,1,0:T(8,128)(2,1)S(1)}, u32[]{:S(2)}, u32[]{:S(2)}) %collective-permute-start.1) | collective-permute-done | bytes 49184 | tf_op jit(solution)/shard_map/ppermute | solution.py:417
  17.6 0.3 shard_map.95
  18.0 0.1 collective-permute-start.3
  18.1 1.3 %collective-permute-done.3.refs_2_.refs_4_ = f32[2,2,32,256]{3,2,1,0:T(8,128)S(1)} collective-permute-done((f32[2,2,32,256]{3,2,1,0:T(8,128)S(1)}, f32[2,2,32,256]{3,2,1,0:T(8,128)S(1)}, u32[]{:S(2)}, u32[]{:S(2)}) %collective-permute-start.3) | collective-permute-done | bytes 131104 | tf_op jit(solution)/shard_map/ppermute | solution.py:434
  19.4 0.8 %collective-permute-start.6 = (bf16[2,2,16,256]{3,2,1,0:T(8,128)(2,1)S(1)}, bf16[2,2,16,256]{3,2,1,0:T(8,128)(2,1)S(1)}, u32[]{:S(2)}, u32[]{:S(2)}) collective-permute-start(bf16[2,2,16,256]{3,2,1,0:T(8,128)(2,1)S(1)} %shard_map.97), channel_id=1, source_target_pairs={{16,0},{24,8},{0,16},{8,24},{17,1},{25,9},{1,17},{9,25},{18,2},{26... | collective-permute-start | bytes 98312 | tf_op jit(solution)/shard_map/ppermute | solution.py:459
  20.2 3.1 %collective-permute-done.6.refs_9_ = bf16[2,2,16,256]{3,2,1,0:T(8,128)(2,1)S(1)} collective-permute-done((bf16[2,2,16,256]{3,2,1,0:T(8,128)(2,1)S(1)}, bf16[2,2,16,256]{3,2,1,0:T(8,128)(2,1)S(1)}, u32[]{:S(2)}, u32[]{:S(2)}) %collective-permute-start.6) | collective-permute-done | bytes 32800 | tf_op jit(solution)/shard_map/ppermute | solution.py:459
  23.3 0.0 collective-permute-done.5.refs_8_
  23.3 1.0 %shard_map.98 = (bf16[2,288,256]{2,1,0:T(8,128)(2,1)S(1)}, bf16[2,256,256]{2,1,0:T(8,128)(2,1)S(1)}, bf16[2,544,256]{2,1,0:T(8,128)(2,1)S(1)}) custom-call(f32[2,256,256]{2,1,0:T(8,128)S(1)} %get-tuple-element.41.refs_0_, f32[2,2,32,256]{3,2,1,0:T(8,128)S(1)} %get-tuple-element.42.refs_0_.refs_1_, ...), custom_call_target="tpu_custom_call" | custom-call | flops 452984832 | bytes 1048576 | tf_op jit(solution)/shard_map/pallas_call | solution.py:375
  24.3 0.1 collective-permute-start.7
  24.4 1.9 %collective-permute-done.7.refs_6_ = bf16[2,544,256]{2,1,0:T(8,128)(2,1)S(1)} collective-permute-done((bf16[2,544,256]{2,1,0:T(8,128)(2,1)S(1)}, bf16[2,544,256]{2,1,0:T(8,128)(2,1)S(1)}, u32[]{:S(2)}, u32[]{:S(2)}) %collective-permute-start.7) | collective-permute-done | bytes 557088 | tf_op jit(solution)/shard_map/ppermute | solution.py:434
  26.3 1.5 %shard_map.99 = (bf16[4,256,256]{2,1,0:T(8,128)(2,1)}, f32[96,256]{1,0:T(8,128)S(1)}, f32[96,256]{1,0:T(8,128)S(1)}, bf16[112,256]{1,0:T(8,128)(2,1)S(1)}, bf16[...) custom-call(bf16[4,256,256]{2,1,0:T(8,128)(2,1)S(1)} %get-tuple-elem, ...), custom_call_target="tpu_custom_call" | custom-call | flops 452984832 | bytes 1048576 | tf_op jit(solution)/shard_map/pallas_call | solution.py:375
  27.8 0.8 %collective-permute-start.9 = (bf16[112,256]{1,0:T(8,128)(2,1)S(1)}, bf16[112,256]{1,0:T(8,128)(2,1)S(1)}, u32[]{:S(2)}, u32[]{:S(2)}) collective-permute-start(bf16[112,256]{1,0:T(8,128)(2,1)S(1)} %get-tuple-element.53), channel_id=1, source_target_pairs={{0,4},{1,5},{2,6},{3,7},{4,0},{5,1},{6,2},{7,3},{8,12},{9,13},{10,... | collective-permute-start | bytes 172040 | tf_op jit(solution)/shard_map/ppermute | solution.py:526
  28.6 1.3 %collective-permute-start.10 = (bf16[112,256]{1,0:T(8,128)(2,1)S(1)}, bf16[112,256]{1,0:T(8,128)(2,1)S(1)}, u32[]{:S(2)}, u32[]{:S(2)}) collective-permute-start(bf16[112,256]{1,0:T(8,128)(2,1)S(1)} %get-tuple-element.54), channel_id=1, source_target_pairs={{0,6},{1,7},{2,4},{3,5},{4,2},{5,3},{6,0},{7,1},{8,14},{9,15},{10,... | collective-permute-start | bytes 172040 | tf_op jit(solution)/shard_map/ppermute | solution.py:526
  30.0 1.4 %collective-permute-start.8 = (bf16[112,256]{1,0:T(8,128)(2,1)S(1)}, bf16[112,256]{1,0:T(8,128)(2,1)S(1)}, u32[]{:S(2)}, u32[]{:S(2)}) collective-permute-start(bf16[112,256]{1,0:T(8,128)(2,1)S(1)} %get-tuple-element.52.mine_ref), channel_id=1, source_target_pairs={{0,2},{1,3},{2,0},{3,1},{4,6},{5,7},{6,4},{7,5},{8,10},{9,11},{10,... | collective-permute-start | bytes 172040 | tf_op jit(solution)/shard_map/ppermute | solution.py:526
  31.3 1.7 %collective-permute-start.16 = (bf16[96,256]{1,0:T(8,128)(2,1)S(1)}, bf16[96,256]{1,0:T(8,128)(2,1)S(1)}, u32[]{:S(2)}, u32[]{:S(2)}) collective-permute-start(bf16[96,256]{1,0:T(8,128)(2,1)S(1)} %get-tuple-element.57), channel_id=1, source_target_pairs={{0,4},{1,5},{2,6},{3,7},{4,0},{5,1},{6,2},{7,3},{8,12},{9,13},{10,... | collective-permute-start | bytes 147464 | tf_op jit(solution)/shard_map/ppermute | solution.py:526
  33.0 1.3 %collective-permute-start.17 = (bf16[96,256]{1,0:T(8,128)(2,1)S(1)}, bf16[96,256]{1,0:T(8,128)(2,1)S(1)}, u32[]{:S(2)}, u32[]{:S(2)}) collective-permute-start(bf16[96,256]{1,0:T(8,128)(2,1)S(1)} %get-tuple-element.58), channel_id=1, source_target_pairs={{0,6},{1,7},{2,4},{3,5},{4,2},{5,3},{6,0},{7,1},{8,14},{9,15},{10,... | collective-permute-start | bytes 147464 | tf_op jit(solution)/shard_map/ppermute | solution.py:526
  34.4 1.0 %collective-permute-done.9.refs_1_ = bf16[112,256]{1,0:T(8,128)(2,1)S(1)} collective-permute-done((bf16[112,256]{1,0:T(8,128)(2,1)S(1)}, bf16[112,256]{1,0:T(8,128)(2,1)S(1)}, u32[]{:S(2)}, u32[]{:S(2)}) %collective-permute-start.9) | collective-permute-done | bytes 57376 | tf_op jit(solution)/shard_map/ppermute | solution.py:526
  35.3 0.0 collective-permute-start.15
  35.3 0.0 collective-permute-done.10.refs_2_
  35.3 0.3 collective-permute-done.8.refs_0_
  35.7 0.8 %collective-permute-start.11 = (bf16[112,256]{1,0:T(8,128)(2,1)S(1)}, bf16[112,256]{1,0:T(8,128)(2,1)S(1)}, u32[]{:S(2)}, u32[]{:S(2)}) collective-permute-start(bf16[112,256]{1,0:T(8,128)(2,1)S(1)} %shard_map.100.a_ref), channel_id=1, source_target_pairs={{0,1},{1,0},{2,3},{3,2},{4,5},{5,4},{6,7},{7,6},{8,9},{9,8},{10,11... | collective-permute-start | bytes 172040 | tf_op jit(solution)/shard_map/ppermute | solution.py:544
  36.6 2.6 %collective-permute-done.16.refs_1_ = bf16[96,256]{1,0:T(8,128)(2,1)S(1)} collective-permute-done((bf16[96,256]{1,0:T(8,128)(2,1)S(1)}, bf16[96,256]{1,0:T(8,128)(2,1)S(1)}, u32[]{:S(2)}, u32[]{:S(2)}) %collective-permute-start.16) | collective-permute-done | bytes 49184 | tf_op jit(solution)/shard_map/ppermute | solution.py:526
  39.2 0.0 collective-permute-done.17.refs_2_
  39.2 0.4 collective-permute-done.15.refs_0_
  39.7 0.9 %collective-permute-start.18 = (bf16[96,256]{1,0:T(8,128)(2,1)S(1)}, bf16[96,256]{1,0:T(8,128)(2,1)S(1)}, u32[]{:S(2)}, u32[]{:S(2)}) collective-permute-start(bf16[96,256]{1,0:T(8,128)(2,1)S(1)} %shard_map.102.a_ref), channel_id=1, source_target_pairs={{0,1},{1,0},{2,3},{3,2},{4,5},{5,4},{6,7},{7,6},{8,9},{9,8},{10,11... | collective-permute-start | bytes 147464 | tf_op jit(solution)/shard_map/ppermute | solution.py:544
  40.5 0.0 collective-permute-done.11.b_ref
  40.6 0.0 copy-start
  40.6 3.3 %collective-permute-done.18.b_ref = bf16[96,256]{1,0:T(8,128)(2,1)S(1)} collective-permute-done((bf16[96,256]{1,0:T(8,128)(2,1)S(1)}, bf16[96,256]{1,0:T(8,128)(2,1)S(1)}, u32[]{:S(2)}, u32[]{:S(2)}) %collective-permute-start.18) | collective-permute-done | bytes 49184 | tf_op jit(solution)/shard_map/ppermute | solution.py:544
  43.8 2.4 %collective-permute-start.21 = (bf16[96,256]{1,0:T(8,128)(2,1)S(1)}, bf16[96,256]{1,0:T(8,128)(2,1)S(1)}, u32[]{:S(2)}, u32[]{:S(2)}) collective-permute-start(bf16[96,256]{1,0:T(8,128)(2,1)S(1)} %shard_map.103.refs_4_), channel_id=1, source_target_pairs={{0,6},{1,7},{2,4},{3,5},{4,2},{5,3},{6,0},{7,1},{8,14},{9,15},{10,... | collective-permute-start | bytes 147464 | tf_op jit(solution)/shard_map/ppermute | solution.py:526
  46.3 0.1 collective-permute-start.20
  46.3 2.0 %collective-permute-start.19 = (bf16[96,256]{1,0:T(8,128)(2,1)S(1)}, bf16[96,256]{1,0:T(8,128)(2,1)S(1)}, u32[]{:S(2)}, u32[]{:S(2)}) collective-permute-start(bf16[96,256]{1,0:T(8,128)(2,1)S(1)} %shard_map.103.refs_4_), channel_id=1, source_target_pairs={{0,2},{1,3},{2,0},{3,1},{4,6},{5,7},{6,4},{7,5},{8,10},{9,11},{10,... | collective-permute-start | bytes 147464 | tf_op jit(solution)/shard_map/ppermute | solution.py:526
  48.3 2.4 %collective-permute-start.14 = (bf16[96,256]{1,0:T(8,128)(2,1)S(1)}, bf16[96,256]{1,0:T(8,128)(2,1)S(1)}, u32[]{:S(2)}, u32[]{:S(2)}) collective-permute-start(bf16[96,256]{1,0:T(8,128)(2,1)S(1)} %shard_map.101.refs_0_), channel_id=1, source_target_pairs={{0,6},{1,7},{2,4},{3,5},{4,2},{5,3},{6,0},{7,1},{8,14},{9,15},{10,... | collective-permute-start | bytes 147464 | tf_op jit(solution)/shard_map/ppermute | solution.py:526
  50.7 0.0 collective-permute-start.13
  50.7 0.0 collective-permute-done.21.refs_7_
  50.7 2.0 %collective-permute-start.12 = (bf16[96,256]{1,0:T(8,128)(2,1)S(1)}, bf16[96,256]{1,0:T(8,128)(2,1)S(1)}, u32[]{:S(2)}, u32[]{:S(2)}) collective-permute-start(bf16[96,256]{1,0:T(8,128)(2,1)S(1)} %shard_map.101.refs_0_), channel_id=1, source_target_pairs={{0,2},{1,3},{2,0},{3,1},{4,6},{5,7},{6,4},{7,5},{8,10},{9,11},{10,... | collective-permute-start | bytes 147464 | tf_op jit(solution)/shard_map/ppermute | solution.py:526
  52.7 0.3 collective-permute-done.20.refs_6_
  53.0 0.0 collective-permute-done.19.refs_5_
  53.0 1.2 %collective-permute-done.14.refs_3_ = bf16[96,256]{1,0:T(8,128)(2,1)S(1)} collective-permute-done((bf16[96,256]{1,0:T(8,128)(2,1)S(1)}, bf16[96,256]{1,0:T(8,128)(2,1)S(1)}, u32[]{:S(2)}, u32[]{:S(2)}) %collective-permute-start.14) | collective-permute-done | bytes 49184 | tf_op jit(solution)/shard_map/ppermute | solution.py:526
  54.2 1.5 %collective-permute-done.13.refs_2_ = bf16[96,256]{1,0:T(8,128)(2,1)S(1)} collective-permute-done((bf16[96,256]{1,0:T(8,128)(2,1)S(1)}, bf16[96,256]{1,0:T(8,128)(2,1)S(1)}, u32[]{:S(2)}, u32[]{:S(2)}) %collective-permute-start.13) | collective-permute-done | bytes 49184 | tf_op jit(solution)/shard_map/ppermute | solution.py:526
  55.7 0.0 collective-permute-done.12.refs_1_
  55.7 0.0 copy-done
  55.7 1.5 %shard_map.104 = (f32[768,256]{1,0:T(8,128)}, f32[36,1,256]{2,1,0:T(1,128)}, f32[36,1,256]{2,1,0:T(1,128)}) custom-call(s32[4]{0:T(128)S(1)} %copy-done, bf16[112,256]{1,0:T(8,128)(2,1)S(1)} %shard_map.100.a_ref, bf16[112,256]{1,0:T(8,128)(2,1)S(1)} %collective-permute-done.11.b_ref, bf16[96,256]{1,0:T(8,128)(2,1)S(1)} %shard_map.101.refs_0_, ...), custom_call_target="tpu_custom_call" | custom-call | flops 1 | bytes 1048576 | tf_op jit(solution)/shard_map/pallas_call | solution.py:375
  (6 shorter events, 0.1 us)
Async XLA Ops:
  2.9 2.7 %collective-permute-start.2 = (f32[2,256,256]{2,1,0:T(8,128)S(1)}, f32[2,256,256]{2,1,0:T(8,128)S(1)}, u32[]{:S(2)}, u32[]{:S(2)}) collective-permute-start(f32[2,256,256]{2,1,0:T(8,128)S(1)} %get-tuple-element.43), channel_id=1, source_target_pairs={{0,8},{8,0},{16,24},{24,16},{1,9},{9,1},{17,25},{25,17},{2,10},{10... | collective-permute-start | bytes 1572872 | tf_op jit(solution)/shard_map/ppermute | solution.py:434
  3.4 2.1 %collective-permute-start.4 = (bf16[3,256,256]{2,1,0:T(8,128)(2,1)S(1)}, bf16[3,256,256]{2,1,0:T(8,128)(2,1)S(1)}, u32[]{:S(2)}, u32[]{:S(2)}) collective-permute-start(bf16[3,256,256]{2,1,0:T(8,128)(2,1)S(1)} %get-tuple-element.34.w_ref.refs_1_.refs_2_), channel_id=1, source_target_pairs={{0,8},{8,0},{16,24},{24,16},{1,9},{9,1},{17,25},{25,17},{2,10},{10... | collective-permute-start | bytes 1179656 | tf_op jit(solution)/shard_map/ppermute | solution.py:434
  5.5 17.8 %collective-permute-start.5 = (bf16[2,240,256]{2,1,0:T(8,128)(2,1)S(1)}, bf16[2,240,256]{2,1,0:T(8,128)(2,1)S(1)}, u32[]{:S(2)}, u32[]{:S(2)}) collective-permute-start(bf16[2,240,256]{2,1,0:T(8,128)(2,1)S(1)} %shard_map.96), channel_id=1, source_target_pairs={{16,0},{24,8},{0,16},{8,24},{17,1},{25,9},{1,17},{9,25},{18,2},{26... | collective-permute-start | bytes 737288 | tf_op jit(solution)/shard_map/ppermute | solution.py:459
  9.3 5.1 %collective-permute-start = (bf16[6,16,256]{2,1,0:T(8,128)(2,1)S(1)}, bf16[6,16,256]{2,1,0:T(8,128)(2,1)S(1)}, u32[]{:S(2)}, u32[]{:S(2)}) collective-permute-start(bf16[6,16,256]{2,1,0:T(8,128)(2,1)S(1)} %get-tuple-element.38), channel_id=1, source_target_pairs={{0,1},{1,0},{2,3},{3,2},{4,5},{5,4},{6,7},{7,6},{8,9},{9,8},{10,11... | collective-permute-start | bytes 147464 | tf_op jit(solution)/shard_map/ppermute | solution.py:418
  10.9 6.8 %collective-permute-start.1 = (bf16[6,16,256]{2,1,0:T(8,128)(2,1)S(1)}, bf16[6,16,256]{2,1,0:T(8,128)(2,1)S(1)}, u32[]{:S(2)}, u32[]{:S(2)}) collective-permute-start(bf16[6,16,256]{2,1,0:T(8,128)(2,1)S(1)} %get-tuple-element.39), channel_id=1, source_target_pairs={{0,7},{1,2},{2,1},{3,4},{4,3},{5,6},{6,5},{7,0},{8,15},{9,10},{10,... | collective-permute-start | bytes 147464 | tf_op jit(solution)/shard_map/ppermute | solution.py:417
  18.0 1.4 %collective-permute-start.3 = (f32[2,2,32,256]{3,2,1,0:T(8,128)S(1)}, f32[2,2,32,256]{3,2,1,0:T(8,128)S(1)}, u32[]{:S(2)}, u32[]{:S(2)}) collective-permute-start(f32[2,2,32,256]{3,2,1,0:T(8,128)S(1)} %get-tuple-element.44), channel_id=1, source_target_pairs={{0,8},{8,0},{16,24},{24,16},{1,9},{9,1},{17,25},{25,17},{2,10},{10... | collective-permute-start | bytes 393224 | tf_op jit(solution)/shard_map/ppermute | solution.py:434
  19.4 3.9 %collective-permute-start.6 = (bf16[2,2,16,256]{3,2,1,0:T(8,128)(2,1)S(1)}, bf16[2,2,16,256]{3,2,1,0:T(8,128)(2,1)S(1)}, u32[]{:S(2)}, u32[]{:S(2)}) collective-permute-start(bf16[2,2,16,256]{3,2,1,0:T(8,128)(2,1)S(1)} %shard_map.97), channel_id=1, source_target_pairs={{16,0},{24,8},{0,16},{8,24},{17,1},{25,9},{1,17},{9,25},{18,2},{26... | collective-permute-start | bytes 98312 | tf_op jit(solution)/shard_map/ppermute | solution.py:459
  24.3 2.0 %collective-permute-start.7 = (bf16[2,544,256]{2,1,0:T(8,128)(2,1)S(1)}, bf16[2,544,256]{2,1,0:T(8,128)(2,1)S(1)}, u32[]{:S(2)}, u32[]{:S(2)}) collective-permute-start(bf16[2,544,256]{2,1,0:T(8,128)(2,1)S(1)} %get-tuple-element.49), channel_id=1, source_target_pairs={{0,8},{8,0},{16,24},{24,16},{1,9},{9,1},{17,25},{25,17},{2,10},{10... | collective-permute-start | bytes 1671176 | tf_op jit(solution)/shard_map/ppermute | solution.py:434
  27.8 7.5 %collective-permute-start.9 = (bf16[112,256]{1,0:T(8,128)(2,1)S(1)}, bf16[112,256]{1,0:T(8,128)(2,1)S(1)}, u32[]{:S(2)}, u32[]{:S(2)}) collective-permute-start(bf16[112,256]{1,0:T(8,128)(2,1)S(1)} %get-tuple-element.53), channel_id=1, source_target_pairs={{0,4},{1,5},{2,6},{3,7},{4,0},{5,1},{6,2},{7,3},{8,12},{9,13},{10,... | collective-permute-start | bytes 172040 | tf_op jit(solution)/shard_map/ppermute | solution.py:526
  28.6 6.7 %collective-permute-start.10 = (bf16[112,256]{1,0:T(8,128)(2,1)S(1)}, bf16[112,256]{1,0:T(8,128)(2,1)S(1)}, u32[]{:S(2)}, u32[]{:S(2)}) collective-permute-start(bf16[112,256]{1,0:T(8,128)(2,1)S(1)} %get-tuple-element.54), channel_id=1, source_target_pairs={{0,6},{1,7},{2,4},{3,5},{4,2},{5,3},{6,0},{7,1},{8,14},{9,15},{10,... | collective-permute-start | bytes 172040 | tf_op jit(solution)/shard_map/ppermute | solution.py:526
  30.0 5.7 %collective-permute-start.8 = (bf16[112,256]{1,0:T(8,128)(2,1)S(1)}, bf16[112,256]{1,0:T(8,128)(2,1)S(1)}, u32[]{:S(2)}, u32[]{:S(2)}) collective-permute-start(bf16[112,256]{1,0:T(8,128)(2,1)S(1)} %get-tuple-element.52.mine_ref), channel_id=1, source_target_pairs={{0,2},{1,3},{2,0},{3,1},{4,6},{5,7},{6,4},{7,5},{8,10},{9,11},{10,... | collective-permute-start | bytes 172040 | tf_op jit(solution)/shard_map/ppermute | solution.py:526
  31.3 7.9 %collective-permute-start.16 = (bf16[96,256]{1,0:T(8,128)(2,1)S(1)}, bf16[96,256]{1,0:T(8,128)(2,1)S(1)}, u32[]{:S(2)}, u32[]{:S(2)}) collective-permute-start(bf16[96,256]{1,0:T(8,128)(2,1)S(1)} %get-tuple-element.57), channel_id=1, source_target_pairs={{0,4},{1,5},{2,6},{3,7},{4,0},{5,1},{6,2},{7,3},{8,12},{9,13},{10,... | collective-permute-start | bytes 147464 | tf_op jit(solution)/shard_map/ppermute | solution.py:526
  33.0 6.2 %collective-permute-start.17 = (bf16[96,256]{1,0:T(8,128)(2,1)S(1)}, bf16[96,256]{1,0:T(8,128)(2,1)S(1)}, u32[]{:S(2)}, u32[]{:S(2)}) collective-permute-start(bf16[96,256]{1,0:T(8,128)(2,1)S(1)} %get-tuple-element.58), channel_id=1, source_target_pairs={{0,6},{1,7},{2,4},{3,5},{4,2},{5,3},{6,0},{7,1},{8,14},{9,15},{10,... | collective-permute-start | bytes 147464 | tf_op jit(solution)/shard_map/ppermute | solution.py:526
  35.3 4.3 %collective-permute-start.15 = (bf16[96,256]{1,0:T(8,128)(2,1)S(1)}, bf16[96,256]{1,0:T(8,128)(2,1)S(1)}, u32[]{:S(2)}, u32[]{:S(2)}) collective-permute-start(bf16[96,256]{1,0:T(8,128)(2,1)S(1)} %get-tuple-element.56.mine_ref), channel_id=1, source_target_pairs={{0,2},{1,3},{2,0},{3,1},{4,6},{5,7},{6,4},{7,5},{8,10},{9,11},{10,... | collective-permute-start | bytes 147464 | tf_op jit(solution)/shard_map/ppermute | solution.py:526
  35.7 4.8 %collective-permute-start.11 = (bf16[112,256]{1,0:T(8,128)(2,1)S(1)}, bf16[112,256]{1,0:T(8,128)(2,1)S(1)}, u32[]{:S(2)}, u32[]{:S(2)}) collective-permute-start(bf16[112,256]{1,0:T(8,128)(2,1)S(1)} %shard_map.100.a_ref), channel_id=1, source_target_pairs={{0,1},{1,0},{2,3},{3,2},{4,5},{5,4},{6,7},{7,6},{8,9},{9,8},{10,11... | collective-permute-start | bytes 172040 | tf_op jit(solution)/shard_map/ppermute | solution.py:544
  39.7 4.2 %collective-permute-start.18 = (bf16[96,256]{1,0:T(8,128)(2,1)S(1)}, bf16[96,256]{1,0:T(8,128)(2,1)S(1)}, u32[]{:S(2)}, u32[]{:S(2)}) collective-permute-start(bf16[96,256]{1,0:T(8,128)(2,1)S(1)} %shard_map.102.a_ref), channel_id=1, source_target_pairs={{0,1},{1,0},{2,3},{3,2},{4,5},{5,4},{6,7},{7,6},{8,9},{9,8},{10,11... | collective-permute-start | bytes 147464 | tf_op jit(solution)/shard_map/ppermute | solution.py:544
  40.6 15.1 %copy-start = (s32[4]{0:T(128)S(1)}, s32[4]{0:T(128)}, u32[]{:S(2)}) copy-start(s32[4]{0:T(128)} %bins.1) | copy-start | bytes 52
  43.8 6.8 %collective-permute-start.21 = (bf16[96,256]{1,0:T(8,128)(2,1)S(1)}, bf16[96,256]{1,0:T(8,128)(2,1)S(1)}, u32[]{:S(2)}, u32[]{:S(2)}) collective-permute-start(bf16[96,256]{1,0:T(8,128)(2,1)S(1)} %shard_map.103.refs_4_), channel_id=1, source_target_pairs={{0,6},{1,7},{2,4},{3,5},{4,2},{5,3},{6,0},{7,1},{8,14},{9,15},{10,... | collective-permute-start | bytes 147464 | tf_op jit(solution)/shard_map/ppermute | solution.py:526
  46.3 6.7 %collective-permute-start.20 = (bf16[96,256]{1,0:T(8,128)(2,1)S(1)}, bf16[96,256]{1,0:T(8,128)(2,1)S(1)}, u32[]{:S(2)}, u32[]{:S(2)}) collective-permute-start(bf16[96,256]{1,0:T(8,128)(2,1)S(1)} %shard_map.103.refs_4_), channel_id=1, source_target_pairs={{0,4},{1,5},{2,6},{3,7},{4,0},{5,1},{6,2},{7,3},{8,12},{9,13},{10,... | collective-permute-start | bytes 147464 | tf_op jit(solution)/shard_map/ppermute | solution.py:526
  46.3 6.6 %collective-permute-start.19 = (bf16[96,256]{1,0:T(8,128)(2,1)S(1)}, bf16[96,256]{1,0:T(8,128)(2,1)S(1)}, u32[]{:S(2)}, u32[]{:S(2)}) collective-permute-start(bf16[96,256]{1,0:T(8,128)(2,1)S(1)} %shard_map.103.refs_4_), channel_id=1, source_target_pairs={{0,2},{1,3},{2,0},{3,1},{4,6},{5,7},{6,4},{7,5},{8,10},{9,11},{10,... | collective-permute-start | bytes 147464 | tf_op jit(solution)/shard_map/ppermute | solution.py:526
  48.3 5.9 %collective-permute-start.14 = (bf16[96,256]{1,0:T(8,128)(2,1)S(1)}, bf16[96,256]{1,0:T(8,128)(2,1)S(1)}, u32[]{:S(2)}, u32[]{:S(2)}) collective-permute-start(bf16[96,256]{1,0:T(8,128)(2,1)S(1)} %shard_map.101.refs_0_), channel_id=1, source_target_pairs={{0,6},{1,7},{2,4},{3,5},{4,2},{5,3},{6,0},{7,1},{8,14},{9,15},{10,... | collective-permute-start | bytes 147464 | tf_op jit(solution)/shard_map/ppermute | solution.py:526
  50.7 5.0 %collective-permute-start.13 = (bf16[96,256]{1,0:T(8,128)(2,1)S(1)}, bf16[96,256]{1,0:T(8,128)(2,1)S(1)}, u32[]{:S(2)}, u32[]{:S(2)}) collective-permute-start(bf16[96,256]{1,0:T(8,128)(2,1)S(1)} %shard_map.101.refs_0_), channel_id=1, source_target_pairs={{0,4},{1,5},{2,6},{3,7},{4,0},{5,1},{6,2},{7,3},{8,12},{9,13},{10,... | collective-permute-start | bytes 147464 | tf_op jit(solution)/shard_map/ppermute | solution.py:526
  50.7 5.0 %collective-permute-start.12 = (bf16[96,256]{1,0:T(8,128)(2,1)S(1)}, bf16[96,256]{1,0:T(8,128)(2,1)S(1)}, u32[]{:S(2)}, u32[]{:S(2)}) collective-permute-start(bf16[96,256]{1,0:T(8,128)(2,1)S(1)} %shard_map.101.refs_0_), channel_id=1, source_target_pairs={{0,2},{1,3},{2,0},{3,1},{4,6},{5,7},{6,4},{7,5},{8,10},{9,11},{10,... | collective-permute-start | bytes 147464 | tf_op jit(solution)/shard_map/ppermute | solution.py:526

commit v4 on v3

--- a/solution.py
+++ b/solution.py
@@ -276,31 +276,47 @@
     return wide[:half] + wide[half:]
 
 
-def last_kernel(outer, *refs):
-    x_ref, pre_ref, pre_rim, gain_ref, grad_ref, d_mine, got_ref, d_ref = refs[:8]
-    own_refs = refs[8 : 8 + PARTS]
-    send_refs = refs[8 + PARTS : -2]
-    total, sums = refs[-2:]
+def add_terms(place, source, wide, x_ref, pre_ref, pre_rim, gain_ref, total, sums):
     micro, rows, channels = x_ref.shape
-    wide = grad_ref.shape[1]
     pad = (wide - rows) // 2
     inner = slice(pad, pad + rows)
+    half = lax.axis_index("section") % 2
+    for j, m in enumerate(turn(half, micro, place)):
+        grad_pre = source[j, :wide]
+        later, earlier = both_sides(grad_pre)
+        for tap, side in enumerate((later, grad_pre, earlier)):
+            where = slice(tap * channels, (tap + 1) * channels)
+            term = trans_times(x_ref[m], side[inner])
+            total[where] = total[where] + term if place or j else term
+        film = grad_pre[inner].astype(F32)
+        pre = with_rim(pre_ref, pre_rim, m)[inner]
+        scale = 1.0 / gain_ref[m]
+        sums[pl.ds(m, 1)] = scale * jnp.sum(film * pre, axis=0, keepdims=True)
+        sums[pl.ds(micro + m, 1)] = scale * jnp.sum(film, axis=0, keepdims=True)
+
+
+def own_kernel(x_ref, pre_ref, pre_rim, gain_ref, grad_ref, total, sums):
+    sums[...] = jnp.zeros_like(sums)
+    wide = grad_ref.shape[1]
+    add_terms(0, grad_ref, wide, x_ref, pre_ref, pre_rim, gain_ref, total, sums)
+
+
+def last_kernel(outer, *refs):
+    x_ref, pre_ref, pre_rim, gain_ref, total_in, sums_in, d_mine, got_ref, d_ref = refs[:9]
+    own_refs = refs[9 : 9 + PARTS]
+    send_refs = refs[9 + PARTS : -2]
+    total, sums = refs[-2:]
+    micro, rows, _ = x_ref.shape
+    wide = got_ref.shape[1] - rows
     mine = lax.axis_index("bulk") // 2
     half = lax.axis_index("section") % 2
-    for place, source in enumerate((grad_ref, got_ref)):
-        for j, m in enumerate(turn(half, micro, place)):
-            grad_pre = source[j, :wide]
-            later, earlier = both_sides(grad_pre)
-            d_ref[m] = got_ref[j, wide:] if place else d_mine[j]
-            for tap, side in enumerate((later, grad_pre, earlier)):
-                where = slice(tap * channels, (tap + 1) * channels)
-                term = trans_times(x_ref[m], side[inner])
-                total[where] = total[where] + term if place or j else term
-            film = grad_pre[inner].astype(F32)
-            pre = with_rim(pre_ref, pre_rim, m)[inner]
-            scale = 1.0 / gain_ref[m]
-            sums[pl.ds(m, 1)] = scale * jnp.sum(film * pre, axis=0, keepdims=True)
-            sums[pl.ds(micro + m, 1)] = scale * jnp.sum(film, axis=0, keepdims=True)
+    total[...] = total_in[...]
+    sums[...] = sums_in[...]
+    add_terms(1, got_ref, wide, x_ref, pre_ref, pre_rim, gain_ref, total, sums)
+    for j, m in enumerate(turn(half, micro, 0)):
+        d_ref[m] = d_mine[j]
+    for j, m in enumerate(turn(half, micro, 1)):
+        d_ref[m] = got_ref[j, wide:]
     rows_out = split_rows(sums[...])
     extra = rows_out.shape[0]
     chunk = own_refs[0].shape[0]
@@ -344,16 +360,7 @@
     out_ref[...] = (a_ref[extra:].astype(F32) + b_ref[extra:].astype(F32)).astype(BF16)
 
 
-def spread_kernel(micro, outer, bins, a_ref, b_ref, *refs):
-    chunk_refs = refs[:-3]
-    out_ref, gain_ref, shift_ref = refs[-3:]
-    chunk = chunk_refs[0].shape[0]
-    parts_count = len(chunk_refs) // outer
-    mine = lax.axis_index("bulk") // 2
-    for part in range(parts_count):
-        for k in range(outer):
-            start = pl.multiple_of(((mine ^ k) * parts_count + part) * chunk, 8)
-            out_ref[pl.ds(start, chunk), :] = chunk_refs[part * outer + k][...].astype(F32)
+def bins_kernel(micro, bins, a_ref, b_ref, gain_ref, shift_ref):
     extra = 4 * micro
     rows = joined_rows(a_ref[:extra]) + joined_rows(b_ref[:extra])
     gain_ref[...] = jnp.zeros_like(gain_ref)
@@ -361,6 +368,39 @@
     for m in range(micro):
         gain_ref[bins[m]] += rows[m : m + 1]
         shift_ref[bins[m]] += rows[micro + m : micro + m + 1]
+
+
+def spread_kernel(outer, part, *refs):
+    chunk_refs = refs[-3 - outer : -3]
+    out_ref, held, sems = refs[-3:]
+    chunk = chunk_refs[0].shape[0]
+    mine = lax.axis_index("bulk") // 2
+    pairs = []
+    for k in range(outer):
+        held[k] = chunk_refs[k][...].astype(F32)
+        start = pl.multiple_of(((mine ^ k) * PARTS + part) * chunk, 8)
+        pairs.append((held.at[k], out_ref.at[pl.ds(start, chunk), :]))
+    for copy in copies(pairs, sems):
+        copy.wait()
+
+
+def written(chunks, outer, part, before, rows):
+    chunk, channels = chunks[0].shape
+    hbm = pl.BlockSpec(memory_space=pltpu.HBM)
+    return pl.pallas_call(
+        functools.partial(spread_kernel, outer, part),
+        in_specs=[hbm] * len(before) + [pl.BlockSpec(memory_space=pltpu.VMEM)] * outer,
+        out_specs=hbm,
+        out_shape=shape_of((rows, channels), F32),
+        scratch_shapes=[
+            pltpu.VMEM((outer, chunk, channels), F32),
+            pltpu.SemaphoreType.DMA((outer,)),
+        ],
+        input_output_aliases={0: 0} if before else {},
+        compiler_params=pltpu.CompilerParams(vmem_limit_bytes=4 << 20),
+        cost_estimate=cost(1, 1 << 20),
+        name="spread",
+    )(*before, *chunks)
 
 
 def shape_of(shape, dtype):
@@ -501,6 +541,14 @@
         limit=12,
     )
     got_away = to_other(away)
+    shared = [x, pre, pre_rim, gain_rows]
+    total_own, sums_own = call(
+        own_kernel,
+        [shape_of((3 * channels, channels), F32), shape_of((2 * micro, channels), F32)],
+        shared + [grad_own],
+        flops=matmul // 2,
+        limit=8,
+    )
 
     chunk = 3 * channels // outer // PARTS
     extra = 4 * micro
@@ -510,7 +558,7 @@
         [shape_of(x.shape, BF16)]
         + [shape_of((chunk, channels), F32)] * PARTS
         + [messages[part] for part in range(PARTS) for _ in range(outer - 1)],
-        [x, pre, pre_rim, gain_rows, grad_own, d_own, got_away],
+        shared + [total_own, sums_own, d_own, got_away],
         scratch=[
             pltpu.VMEM((3 * channels, channels), F32),
             pltpu.VMEM((2 * micro, channels), F32),
@@ -550,12 +598,14 @@
         got = {k: across(done, k) for k in order}
         spread += [done] + [got[k] for k in range(1, outer)]
     table = shape_of((bins_count, 1, channels), F32)
-    d_weights, d_gain, d_shift = call(
-        functools.partial(spread_kernel, micro, outer),
-        [shape_of((3 * channels, channels), F32), table, table],
-        [*summed[0], *spread],
-        scalars=[doa_bins],
-    )
+    d_gain, d_shift = call(
+        functools.partial(bins_kernel, micro), [table, table], list(summed[0]), scalars=[doa_bins]
+    )
+    before = []
+    for part in range(PARTS):
+        chunks = spread[part * outer : (part + 1) * outer]
+        before = [written(chunks, outer, part, before, 3 * channels)]
+    d_weights = before[0]
     return (
         d_local[None],
         d_weights.reshape(1, 3, channels, channels),

time: 57.3 us -> 57.8 us (level)
  waiting for transfers between devices: 22.3 us -> 20.5 us
  Pallas kernels: 6.68 us -> 8.12 us
  starting transfers between devices: 27.5 us -> 28.3 us
    ppermute x2, waiting for transfers between devices: 3.26 us -> 0.01 us  [step(): summed.append((partial_sum, lax.ppermute(partial_sum, 'bulk', swap)))]
    ppermute x12, waiting for transfers between devices: 7.36 us -> 9.25 us  [across(): return lax.ppermute(value, 'bulk', pairs)]
    pallas_call x0 -> x2, Pallas kernels: none -> 1.6 us  [written(): pl.pallas_call(functools.partial(spread_kernel, outer, part), in_specs=[h...]
    pallas_call x12 -> x13, Pallas kernels: 6.68 us -> 6.52 us  [call(): pl.pallas_call(kernel, in_specs=[smem] * len(scalars) + [kept] * len(remo...]
  transfers between devices with their start and end apart: 22 -> 22, of which waited for: 13 -> 10; matrix products, arithmetic and copies ran while one was open for 0% -> 0% of each run, Pallas kernels for 1% -> 5%
where the time goes in v4:
time: 57.8 us; the launch traced here: 57.7 us
  starting transfers between devices  28.3 us (49%)
  waiting for transfers between devices  20.5 us (35%)
  Pallas kernels  8.12 us (14%)
  between operations  0.74 us (1%)
    ppermute x12, starting transfers between devices, across(): return lax.ppermute(value, 'bulk', pairs)  15.9 us
    ppermute x12, waiting for transfers between devices, across(): return lax.ppermute(value, 'bulk', pairs)  9.25 us
    pallas_call x13, Pallas kernels, call(): pl.pallas_call(kernel, in_specs=[smem] * len(scalars) + [kept] * len(remo...  6.52 us
    ppermute x4, waiting for transfers between devices, to_other(): return lax.ppermute(value, 'section', [(i, i ^ 1) for i in range(sections)])  4.86 us
    ppermute x2, starting transfers between devices, down(): lax.ppermute(value, 'section', pairs + [(low, high) for high, low in pairs])  4.55 us
    ppermute x1, starting transfers between devices, step(): far = lax.ppermute(far, 'bulk', opposite)  3.54 us
    ppermute x1, waiting for transfers between devices, step(): far = lax.ppermute(far, 'bulk', opposite)  3.24 us
    ppermute x2, waiting for transfers between devices, down(): lax.ppermute(value, 'section', pairs + [(low, high) for high, low in pairs])  3.15 us
  transfers between devices with their start and end apart: 22, of which 10 were waited for; matrix products, arithmetic and copies ran while one was open for 0% of the time, Pallas kernels for 5%

profile of v4, /device:TPU:0, one launch (start us, length us, event | category | flops | bytes accessed | tf_op | source)
XLA Modules:
  0.0 57.7 jit_solution(16290367230199822013)
XLA Ops:
  0.6 1.3 %shard_map.93 = (bf16[6,16,256]{2,1,0:T(8,128)(2,1)S(1)}, bf16[6,16,256]{2,1,0:T(8,128)(2,1)S(1)}, bf16[4,256,256]{2,1,0:T(8,128)(2,1)S(1)}, bf16[2,256,256]{2,1...) custom-call(s32[4]{0:T(128)} %bins.1, ...), custom_call_target="tpu_custom_call" | custom-call | flops 1 | bytes 1048576 | tf_op jit(solution)/shard_map/pallas_call | solution.py:415
  2.0 0.9 %shard_map.94 = (f32[2,256,256]{2,1,0:T(8,128)S(1)}, f32[2,256,256]{2,1,0:T(8,128)S(1)}, f32[4,256,256]{2,1,0:T(8,128)S(1)}) custom-call(bf16[4,256,256]{2,1,0:T(8,128)(2,1)S(1)} %get-tuple-element.34.x_ref.refs_0_, bf16[3,256,256]{2,1,0:T(8,128)(2,1)S(1)} %get-tuple-element.35.w_ref.refs_1_.refs_2_, f32[4,1,256]{2,1,0:T(1,128)S(1)} %get-tuple-element.36.gain_ref.refs_3_, ...), custom_call_target="tpu_custom_call" | custom-call | flops 452984832 | bytes 1048576 | tf_op jit(solution)/shard_map/pallas_call | solution.py:415
  2.9 0.6 collective-permute-start.2
  3.4 0.1 collective-permute-start.4
  3.5 2.0 %collective-permute-done.4.refs_3_.refs_5_ = bf16[3,256,256]{2,1,0:T(8,128)(2,1)S(1)} collective-permute-done((bf16[3,256,256]{2,1,0:T(8,128)(2,1)S(1)}, bf16[3,256,256]{2,1,0:T(8,128)(2,1)S(1)}, u32[]{:S(2)}, u32[]{:S(2)}) %collective-permute-start.4) | collective-permute-done | bytes 393248 | tf_op jit(solution)/shard_map/ppermute | solution.py:474
  5.5 0.0 collective-permute-done.2.refs_2_.refs_3_
  5.5 3.8 %collective-permute-start.5 = (bf16[2,240,256]{2,1,0:T(8,128)(2,1)S(1)}, bf16[2,240,256]{2,1,0:T(8,128)(2,1)S(1)}, u32[]{:S(2)}, u32[]{:S(2)}) collective-permute-start(bf16[2,240,256]{2,1,0:T(8,128)(2,1)S(1)} %shard_map.96), channel_id=1, source_target_pairs={{16,0},{24,8},{0,16},{8,24},{17,1},{25,9},{1,17},{9,25},{18,2},{26... | collective-permute-start | bytes 737288 | tf_op jit(solution)/shard_map/ppermute | solution.py:499
  9.3 1.5 %collective-permute-start = (bf16[6,16,256]{2,1,0:T(8,128)(2,1)S(1)}, bf16[6,16,256]{2,1,0:T(8,128)(2,1)S(1)}, u32[]{:S(2)}, u32[]{:S(2)}) collective-permute-start(bf16[6,16,256]{2,1,0:T(8,128)(2,1)S(1)} %get-tuple-element.39), channel_id=1, source_target_pairs={{0,1},{1,0},{2,3},{3,2},{4,5},{5,4},{6,7},{7,6},{8,9},{9,8},{10,11... | collective-permute-start | bytes 147464 | tf_op jit(solution)/shard_map/ppermute | solution.py:458
  10.9 3.5 %collective-permute-start.1 = (bf16[6,16,256]{2,1,0:T(8,128)(2,1)S(1)}, bf16[6,16,256]{2,1,0:T(8,128)(2,1)S(1)}, u32[]{:S(2)}, u32[]{:S(2)}) collective-permute-start(bf16[6,16,256]{2,1,0:T(8,128)(2,1)S(1)} %get-tuple-element.40), channel_id=1, source_target_pairs={{0,7},{1,2},{2,1},{3,4},{4,3},{5,6},{6,5},{7,0},{8,15},{9,10},{10,... | collective-permute-start | bytes 147464 | tf_op jit(solution)/shard_map/ppermute | solution.py:457
  14.4 0.0 collective-permute-done.near_ref
  14.4 3.2 %collective-permute-done.1.far_ref = bf16[6,16,256]{2,1,0:T(8,128)(2,1)S(1)} collective-permute-done((bf16[6,16,256]{2,1,0:T(8,128)(2,1)S(1)}, bf16[6,16,256]{2,1,0:T(8,128)(2,1)S(1)}, u32[]{:S(2)}, u32[]{:S(2)}) %collective-permute-start.1) | collective-permute-done | bytes 49184 | tf_op jit(solution)/shard_map/ppermute | solution.py:457
  17.6 0.3 shard_map.95
  18.0 0.1 collective-permute-start.3
  18.1 1.3 %collective-permute-done.3.refs_2_.refs_4_ = f32[2,2,32,256]{3,2,1,0:T(8,128)S(1)} collective-permute-done((f32[2,2,32,256]{3,2,1,0:T(8,128)S(1)}, f32[2,2,32,256]{3,2,1,0:T(8,128)S(1)}, u32[]{:S(2)}, u32[]{:S(2)}) %collective-permute-start.3) | collective-permute-done | bytes 131104 | tf_op jit(solution)/shard_map/ppermute | solution.py:474
  19.4 0.8 %collective-permute-start.6 = (bf16[2,2,16,256]{3,2,1,0:T(8,128)(2,1)S(1)}, bf16[2,2,16,256]{3,2,1,0:T(8,128)(2,1)S(1)}, u32[]{:S(2)}, u32[]{:S(2)}) collective-permute-start(bf16[2,2,16,256]{3,2,1,0:T(8,128)(2,1)S(1)} %shard_map.97), channel_id=1, source_target_pairs={{16,0},{24,8},{0,16},{8,24},{17,1},{25,9},{1,17},{9,25},{18,2},{26... | collective-permute-start | bytes 98312 | tf_op jit(solution)/shard_map/ppermute | solution.py:499
  20.2 3.1 %collective-permute-done.6.refs_9_ = bf16[2,2,16,256]{3,2,1,0:T(8,128)(2,1)S(1)} collective-permute-done((bf16[2,2,16,256]{3,2,1,0:T(8,128)(2,1)S(1)}, bf16[2,2,16,256]{3,2,1,0:T(8,128)(2,1)S(1)}, u32[]{:S(2)}, u32[]{:S(2)}) %collective-permute-start.6) | collective-permute-done | bytes 32800 | tf_op jit(solution)/shard_map/ppermute | solution.py:499
  23.3 0.0 collective-permute-done.5.refs_8_
  23.3 1.0 %shard_map.98 = (bf16[2,288,256]{2,1,0:T(8,128)(2,1)S(1)}, bf16[2,256,256]{2,1,0:T(8,128)(2,1)S(1)}, bf16[2,544,256]{2,1,0:T(8,128)(2,1)S(1)}) custom-call(f32[2,256,256]{2,1,0:T(8,128)S(1)} %get-tuple-element.42.refs_0_, f32[2,2,32,256]{3,2,1,0:T(8,128)S(1)} %get-tuple-element.43.refs_0_.refs_1_, ...), custom_call_target="tpu_custom_call" | custom-call | flops 452984832 | bytes 1048576 | tf_op jit(solution)/shard_map/pallas_call | solution.py:415
  24.3 0.1 collective-permute-start.7
  24.4 0.4 shard_map.99
  24.8 1.5 %collective-permute-done.7.refs_7_ = bf16[2,544,256]{2,1,0:T(8,128)(2,1)S(1)} collective-permute-done((bf16[2,544,256]{2,1,0:T(8,128)(2,1)S(1)}, bf16[2,544,256]{2,1,0:T(8,128)(2,1)S(1)}, u32[]{:S(2)}, u32[]{:S(2)}) %collective-permute-start.7) | collective-permute-done | bytes 557088 | tf_op jit(solution)/shard_map/ppermute | solution.py:474
  26.3 1.2 %shard_map.100 = (bf16[4,256,256]{2,1,0:T(8,128)(2,1)}, f32[96,256]{1,0:T(8,128)S(1)}, f32[96,256]{1,0:T(8,128)S(1)}, bf16[112,256]{1,0:T(8,128)(2,1)S(1)}, bf16...) custom-call(bf16[4,256,256]{2,1,0:T(8,128)(2,1)S(1)} %get-tuple-elem, ...), custom_call_target="tpu_custom_call" | custom-call | flops 452984832 | bytes 1048576 | tf_op jit(solution)/shard_map/pallas_call | solution.py:415
  27.6 0.8 %collective-permute-start.9 = (bf16[112,256]{1,0:T(8,128)(2,1)S(1)}, bf16[112,256]{1,0:T(8,128)(2,1)S(1)}, u32[]{:S(2)}, u32[]{:S(2)}) collective-permute-start(bf16[112,256]{1,0:T(8,128)(2,1)S(1)} %get-tuple-element.56), channel_id=1, source_target_pairs={{0,4},{1,5},{2,6},{3,7},{4,0},{5,1},{6,2},{7,3},{8,12},{9,13},{10,... | collective-permute-start | bytes 172040 | tf_op jit(solution)/shard_map/ppermute | solution.py:574
  28.4 1.3 %collective-permute-start.10 = (bf16[112,256]{1,0:T(8,128)(2,1)S(1)}, bf16[112,256]{1,0:T(8,128)(2,1)S(1)}, u32[]{:S(2)}, u32[]{:S(2)}) collective-permute-start(bf16[112,256]{1,0:T(8,128)(2,1)S(1)} %get-tuple-element.57), channel_id=1, source_target_pairs={{0,6},{1,7},{2,4},{3,5},{4,2},{5,3},{6,0},{7,1},{8,14},{9,15},{10,... | collective-permute-start | bytes 172040 | tf_op jit(solution)/shard_map/ppermute | solution.py:574
  29.7 1.4 %collective-permute-start.8 = (bf16[112,256]{1,0:T(8,128)(2,1)S(1)}, bf16[112,256]{1,0:T(8,128)(2,1)S(1)}, u32[]{:S(2)}, u32[]{:S(2)}) collective-permute-start(bf16[112,256]{1,0:T(8,128)(2,1)S(1)} %get-tuple-element.55.mine_ref), channel_id=1, source_target_pairs={{0,2},{1,3},{2,0},{3,1},{4,6},{5,7},{6,4},{7,5},{8,10},{9,11},{10,... | collective-permute-start | bytes 172040 | tf_op jit(solution)/shard_map/ppermute | solution.py:574
  31.1 3.5 %collective-permute-done.9.refs_1_ = bf16[112,256]{1,0:T(8,128)(2,1)S(1)} collective-permute-done((bf16[112,256]{1,0:T(8,128)(2,1)S(1)}, bf16[112,256]{1,0:T(8,128)(2,1)S(1)}, u32[]{:S(2)}, u32[]{:S(2)}) %collective-permute-start.9) | collective-permute-done | bytes 57376 | tf_op jit(solution)/shard_map/ppermute | solution.py:574
  34.5 0.0 collective-permute-done.10.refs_2_
  34.5 0.9 %collective-permute-done.8.refs_0_ = bf16[112,256]{1,0:T(8,128)(2,1)S(1)} collective-permute-done((bf16[112,256]{1,0:T(8,128)(2,1)S(1)}, bf16[112,256]{1,0:T(8,128)(2,1)S(1)}, u32[]{:S(2)}, u32[]{:S(2)}) %collective-permute-start.8) | collective-permute-done | bytes 57376 | tf_op jit(solution)/shard_map/ppermute | solution.py:574
  35.5 0.8 %collective-permute-start.11 = (bf16[112,256]{1,0:T(8,128)(2,1)S(1)}, bf16[112,256]{1,0:T(8,128)(2,1)S(1)}, u32[]{:S(2)}, u32[]{:S(2)}) collective-permute-start(bf16[112,256]{1,0:T(8,128)(2,1)S(1)} %shard_map.101.a_ref), channel_id=1, source_target_pairs={{0,1},{1,0},{2,3},{3,2},{4,5},{5,4},{6,7},{7,6},{8,9},{9,8},{10,11... | collective-permute-start | bytes 172040 | tf_op jit(solution)/shard_map/ppermute | solution.py:592
  36.3 1.9 %collective-permute-start.16 = (bf16[96,256]{1,0:T(8,128)(2,1)S(1)}, bf16[96,256]{1,0:T(8,128)(2,1)S(1)}, u32[]{:S(2)}, u32[]{:S(2)}) collective-permute-start(bf16[96,256]{1,0:T(8,128)(2,1)S(1)} %get-tuple-element.60), channel_id=1, source_target_pairs={{0,4},{1,5},{2,6},{3,7},{4,0},{5,1},{6,2},{7,3},{8,12},{9,13},{10,... | collective-permute-start | bytes 147464 | tf_op jit(solution)/shard_map/ppermute | solution.py:574
  38.2 1.2 %collective-permute-start.17 = (bf16[96,256]{1,0:T(8,128)(2,1)S(1)}, bf16[96,256]{1,0:T(8,128)(2,1)S(1)}, u32[]{:S(2)}, u32[]{:S(2)}) collective-permute-start(bf16[96,256]{1,0:T(8,128)(2,1)S(1)} %get-tuple-element.61), channel_id=1, source_target_pairs={{0,6},{1,7},{2,4},{3,5},{4,2},{5,3},{6,0},{7,1},{8,14},{9,15},{10,... | collective-permute-start | bytes 147464 | tf_op jit(solution)/shard_map/ppermute | solution.py:574
  39.4 0.4 collective-permute-start.15
  39.8 2.9 %collective-permute-done.16.refs_1_ = bf16[96,256]{1,0:T(8,128)(2,1)S(1)} collective-permute-done((bf16[96,256]{1,0:T(8,128)(2,1)S(1)}, bf16[96,256]{1,0:T(8,128)(2,1)S(1)}, u32[]{:S(2)}, u32[]{:S(2)}) %collective-permute-start.16) | collective-permute-done | bytes 49184 | tf_op jit(solution)/shard_map/ppermute | solution.py:574
  42.7 1.4 %collective-permute-done.17.refs_2_ = bf16[96,256]{1,0:T(8,128)(2,1)S(1)} collective-permute-done((bf16[96,256]{1,0:T(8,128)(2,1)S(1)}, bf16[96,256]{1,0:T(8,128)(2,1)S(1)}, u32[]{:S(2)}, u32[]{:S(2)}) %collective-permute-start.17) | collective-permute-done | bytes 49184 | tf_op jit(solution)/shard_map/ppermute | solution.py:574
  44.1 0.0 collective-permute-done.15.refs_0_
  44.1 1.2 %collective-permute-start.18 = (bf16[96,256]{1,0:T(8,128)(2,1)S(1)}, bf16[96,256]{1,0:T(8,128)(2,1)S(1)}, u32[]{:S(2)}, u32[]{:S(2)}) collective-permute-start(bf16[96,256]{1,0:T(8,128)(2,1)S(1)} %shard_map.103.a_ref), channel_id=1, source_target_pairs={{0,1},{1,0},{2,3},{3,2},{4,5},{5,4},{6,7},{7,6},{8,9},{9,8},{10,11... | collective-permute-start | bytes 147464 | tf_op jit(solution)/shard_map/ppermute | solution.py:592
  45.3 0.0 collective-permute-done.11.b_ref
  45.3 0.0 copy-start
  45.4 2.0 %collective-permute-start.14 = (bf16[96,256]{1,0:T(8,128)(2,1)S(1)}, bf16[96,256]{1,0:T(8,128)(2,1)S(1)}, u32[]{:S(2)}, u32[]{:S(2)}) collective-permute-start(bf16[96,256]{1,0:T(8,128)(2,1)S(1)} %shard_map.102.refs_0_), channel_id=1, source_target_pairs={{0,6},{1,7},{2,4},{3,5},{4,2},{5,3},{6,0},{7,1},{8,14},{9,15},{10,... | collective-permute-start | bytes 147464 | tf_op jit(solution)/shard_map/ppermute | solution.py:574
  47.3 0.0 collective-permute-start.13
  47.3 2.5 %collective-permute-start.12 = (bf16[96,256]{1,0:T(8,128)(2,1)S(1)}, bf16[96,256]{1,0:T(8,128)(2,1)S(1)}, u32[]{:S(2)}, u32[]{:S(2)}) collective-permute-start(bf16[96,256]{1,0:T(8,128)(2,1)S(1)} %shard_map.102.refs_0_), channel_id=1, source_target_pairs={{0,2},{1,3},{2,0},{3,1},{4,6},{5,7},{6,4},{7,5},{8,10},{9,11},{10,... | collective-permute-start | bytes 147464 | tf_op jit(solution)/shard_map/ppermute | solution.py:574
  49.8 0.0 collective-permute-done.18.b_ref
  49.8 2.0 %collective-permute-start.21 = (bf16[96,256]{1,0:T(8,128)(2,1)S(1)}, bf16[96,256]{1,0:T(8,128)(2,1)S(1)}, u32[]{:S(2)}, u32[]{:S(2)}) collective-permute-start(bf16[96,256]{1,0:T(8,128)(2,1)S(1)} %shard_map.104.refs_1_), channel_id=1, source_target_pairs={{0,6},{1,7},{2,4},{3,5},{4,2},{5,3},{6,0},{7,1},{8,14},{9,15},{10,... | collective-permute-start | bytes 147464 | tf_op jit(solution)/shard_map/ppermute | solution.py:574
  51.8 0.0 collective-permute-start.20
  51.8 0.0 collective-permute-done.14.refs_3_
  51.8 2.5 %collective-permute-start.19 = (bf16[96,256]{1,0:T(8,128)(2,1)S(1)}, bf16[96,256]{1,0:T(8,128)(2,1)S(1)}, u32[]{:S(2)}, u32[]{:S(2)}) collective-permute-start(bf16[96,256]{1,0:T(8,128)(2,1)S(1)} %shard_map.104.refs_1_), channel_id=1, source_target_pairs={{0,2},{1,3},{2,0},{3,1},{4,6},{5,7},{6,4},{7,5},{8,10},{9,11},{10,... | collective-permute-start | bytes 147464 | tf_op jit(solution)/shard_map/ppermute | solution.py:574
  54.3 0.0 copy-done
  54.3 1.2 %shard_map.105 = (f32[36,1,256]{2,1,0:T(1,128)}, f32[36,1,256]{2,1,0:T(1,128)}) custom-call(s32[4]{0:T(128)S(1)} %copy-done, bf16[112,256]{1,0:T(8,128)(2,1)S(1)} %shard_map.101.a_ref, bf16[112,256]{1,0:T(8,128)(2,1)S(1)} %collective-permute-done.11.b_ref), custom_call_target="tpu_custom_call" | custom-call | flops 1 | bytes 1048576 | tf_op jit(solution)/shard_map/pallas_call | solution.py:415
  55.5 0.0 collective-permute-done.13.refs_2_
  55.5 0.0 collective-permute-done.12.refs_1_
  55.5 0.8 %spread.2.refs_0_ = f32[768,256]{1,0:T(8,128)} custom-call(bf16[96,256]{1,0:T(8,128)(2,1)S(1)} %shard_map.102.refs_0_, bf16[96,256]{1,0:T(8,128)(2,1)S(1)} %collective-permute-done.12.refs_1_, bf16[96,256]{1,0:T(8,128)(2,1)S(1)} %collective-permute-done.13.refs_2_, bf16[96,256]{1,0:T(8,128)(2,1)S(1)} %collective-permute-done.14.refs_3_), custom_call_target="tpu_custom_call" | custom-call | flops 1 | bytes 1048576 | tf_op jit(solution)/shard_map/spread/pallas_call | solution.py:390
  56.3 0.0 collective-permute-done.21.refs_4_
  56.3 0.6 collective-permute-done.20.refs_3_
  56.9 0.0 collective-permute-done.19.refs_2_
  56.9 0.8 %spread.3 = f32[768,256]{1,0:T(8,128)} custom-call(f32[768,256]{1,0:T(8,128)} %spread.2.refs_0_, bf16[96,256]{1,0:T(8,128)(2,1)S(1)} %shard_map.104.refs_1_, bf16[96,256]{1,0:T(8,128)(2,1)S(1)} %collective-permute-done.19.refs_2_, bf16[96,256]{1,0:T(8,128)(2,1)S(1)} %collective-permute-done.20.refs_3_, ...), custom_call_target="tpu_custom_call", output_to_operand_aliasing={{}: (0, {})} | custom-call | flops 1 | bytes 1048576 | tf_op jit(solution)/shard_map/spread/pallas_call | solution.py:390
  (6 shorter events, 0.1 us)
Async XLA Ops:
  2.9 2.7 %collective-permute-start.2 = (f32[2,256,256]{2,1,0:T(8,128)S(1)}, f32[2,256,256]{2,1,0:T(8,128)S(1)}, u32[]{:S(2)}, u32[]{:S(2)}) collective-permute-start(f32[2,256,256]{2,1,0:T(8,128)S(1)} %get-tuple-element.44), channel_id=1, source_target_pairs={{0,8},{8,0},{16,24},{24,16},{1,9},{9,1},{17,25},{25,17},{2,10},{10... | collective-permute-start | bytes 1572872 | tf_op jit(solution)/shard_map/ppermute | solution.py:474
  3.4 2.1 %collective-permute-start.4 = (bf16[3,256,256]{2,1,0:T(8,128)(2,1)S(1)}, bf16[3,256,256]{2,1,0:T(8,128)(2,1)S(1)}, u32[]{:S(2)}, u32[]{:S(2)}) collective-permute-start(bf16[3,256,256]{2,1,0:T(8,128)(2,1)S(1)} %get-tuple-element.35.w_ref.refs_1_.refs_2_), channel_id=1, source_target_pairs={{0,8},{8,0},{16,24},{24,16},{1,9},{9,1},{17,25},{25,17},{2,10},{10... | collective-permute-start | bytes 1179656 | tf_op jit(solution)/shard_map/ppermute | solution.py:474
  5.5 17.8 %collective-permute-start.5 = (bf16[2,240,256]{2,1,0:T(8,128)(2,1)S(1)}, bf16[2,240,256]{2,1,0:T(8,128)(2,1)S(1)}, u32[]{:S(2)}, u32[]{:S(2)}) collective-permute-start(bf16[2,240,256]{2,1,0:T(8,128)(2,1)S(1)} %shard_map.96), channel_id=1, source_target_pairs={{16,0},{24,8},{0,16},{8,24},{17,1},{25,9},{1,17},{9,25},{18,2},{26... | collective-permute-start | bytes 737288 | tf_op jit(solution)/shard_map/ppermute | solution.py:499
  9.3 5.1 %collective-permute-start = (bf16[6,16,256]{2,1,0:T(8,128)(2,1)S(1)}, bf16[6,16,256]{2,1,0:T(8,128)(2,1)S(1)}, u32[]{:S(2)}, u32[]{:S(2)}) collective-permute-start(bf16[6,16,256]{2,1,0:T(8,128)(2,1)S(1)} %get-tuple-element.39), channel_id=1, source_target_pairs={{0,1},{1,0},{2,3},{3,2},{4,5},{5,4},{6,7},{7,6},{8,9},{9,8},{10,11... | collective-permute-start | bytes 147464 | tf_op jit(solution)/shard_map/ppermute | solution.py:458
  10.9 6.8 %collective-permute-start.1 = (bf16[6,16,256]{2,1,0:T(8,128)(2,1)S(1)}, bf16[6,16,256]{2,1,0:T(8,128)(2,1)S(1)}, u32[]{:S(2)}, u32[]{:S(2)}) collective-permute-start(bf16[6,16,256]{2,1,0:T(8,128)(2,1)S(1)} %get-tuple-element.40), channel_id=1, source_target_pairs={{0,7},{1,2},{2,1},{3,4},{4,3},{5,6},{6,5},{7,0},{8,15},{9,10},{10,... | collective-permute-start | bytes 147464 | tf_op jit(solution)/shard_map/ppermute | solution.py:457
  18.0 1.4 %collective-permute-start.3 = (f32[2,2,32,256]{3,2,1,0:T(8,128)S(1)}, f32[2,2,32,256]{3,2,1,0:T(8,128)S(1)}, u32[]{:S(2)}, u32[]{:S(2)}) collective-permute-start(f32[2,2,32,256]{3,2,1,0:T(8,128)S(1)} %get-tuple-element.45), channel_id=1, source_target_pairs={{0,8},{8,0},{16,24},{24,16},{1,9},{9,1},{17,25},{25,17},{2,10},{10... | collective-permute-start | bytes 393224 | tf_op jit(solution)/shard_map/ppermute | solution.py:474
  19.4 3.9 %collective-permute-start.6 = (bf16[2,2,16,256]{3,2,1,0:T(8,128)(2,1)S(1)}, bf16[2,2,16,256]{3,2,1,0:T(8,128)(2,1)S(1)}, u32[]{:S(2)}, u32[]{:S(2)}) collective-permute-start(bf16[2,2,16,256]{3,2,1,0:T(8,128)(2,1)S(1)} %shard_map.97), channel_id=1, source_target_pairs={{16,0},{24,8},{0,16},{8,24},{17,1},{25,9},{1,17},{9,25},{18,2},{26... | collective-permute-start | bytes 98312 | tf_op jit(solution)/shard_map/ppermute | solution.py:499
  24.3 2.0 %collective-permute-start.7 = (bf16[2,544,256]{2,1,0:T(8,128)(2,1)S(1)}, bf16[2,544,256]{2,1,0:T(8,128)(2,1)S(1)}, u32[]{:S(2)}, u32[]{:S(2)}) collective-permute-start(bf16[2,544,256]{2,1,0:T(8,128)(2,1)S(1)} %get-tuple-element.52), channel_id=1, source_target_pairs={{0,8},{8,0},{16,24},{24,16},{1,9},{9,1},{17,25},{25,17},{2,10},{10... | collective-permute-start | bytes 1671176 | tf_op jit(solution)/shard_map/ppermute | solution.py:474
  27.6 7.0 %collective-permute-start.9 = (bf16[112,256]{1,0:T(8,128)(2,1)S(1)}, bf16[112,256]{1,0:T(8,128)(2,1)S(1)}, u32[]{:S(2)}, u32[]{:S(2)}) collective-permute-start(bf16[112,256]{1,0:T(8,128)(2,1)S(1)} %get-tuple-element.56), channel_id=1, source_target_pairs={{0,4},{1,5},{2,6},{3,7},{4,0},{5,1},{6,2},{7,3},{8,12},{9,13},{10,... | collective-permute-start | bytes 172040 | tf_op jit(solution)/shard_map/ppermute | solution.py:574
  28.4 6.2 %collective-permute-start.10 = (bf16[112,256]{1,0:T(8,128)(2,1)S(1)}, bf16[112,256]{1,0:T(8,128)(2,1)S(1)}, u32[]{:S(2)}, u32[]{:S(2)}) collective-permute-start(bf16[112,256]{1,0:T(8,128)(2,1)S(1)} %get-tuple-element.57), channel_id=1, source_target_pairs={{0,6},{1,7},{2,4},{3,5},{4,2},{5,3},{6,0},{7,1},{8,14},{9,15},{10,... | collective-permute-start | bytes 172040 | tf_op jit(solution)/shard_map/ppermute | solution.py:574
  29.7 5.7 %collective-permute-start.8 = (bf16[112,256]{1,0:T(8,128)(2,1)S(1)}, bf16[112,256]{1,0:T(8,128)(2,1)S(1)}, u32[]{:S(2)}, u32[]{:S(2)}) collective-permute-start(bf16[112,256]{1,0:T(8,128)(2,1)S(1)} %get-tuple-element.55.mine_ref), channel_id=1, source_target_pairs={{0,2},{1,3},{2,0},{3,1},{4,6},{5,7},{6,4},{7,5},{8,10},{9,11},{10,... | collective-permute-start | bytes 172040 | tf_op jit(solution)/shard_map/ppermute | solution.py:574
  35.5 9.9 %collective-permute-start.11 = (bf16[112,256]{1,0:T(8,128)(2,1)S(1)}, bf16[112,256]{1,0:T(8,128)(2,1)S(1)}, u32[]{:S(2)}, u32[]{:S(2)}) collective-permute-start(bf16[112,256]{1,0:T(8,128)(2,1)S(1)} %shard_map.101.a_ref), channel_id=1, source_target_pairs={{0,1},{1,0},{2,3},{3,2},{4,5},{5,4},{6,7},{7,6},{8,9},{9,8},{10,11... | collective-permute-start | bytes 172040 | tf_op jit(solution)/shard_map/ppermute | solution.py:592
  36.3 6.4 %collective-permute-start.16 = (bf16[96,256]{1,0:T(8,128)(2,1)S(1)}, bf16[96,256]{1,0:T(8,128)(2,1)S(1)}, u32[]{:S(2)}, u32[]{:S(2)}) collective-permute-start(bf16[96,256]{1,0:T(8,128)(2,1)S(1)} %get-tuple-element.60), channel_id=1, source_target_pairs={{0,4},{1,5},{2,6},{3,7},{4,0},{5,1},{6,2},{7,3},{8,12},{9,13},{10,... | collective-permute-start | bytes 147464 | tf_op jit(solution)/shard_map/ppermute | solution.py:574
  38.2 5.9 %collective-permute-start.17 = (bf16[96,256]{1,0:T(8,128)(2,1)S(1)}, bf16[96,256]{1,0:T(8,128)(2,1)S(1)}, u32[]{:S(2)}, u32[]{:S(2)}) collective-permute-start(bf16[96,256]{1,0:T(8,128)(2,1)S(1)} %get-tuple-element.61), channel_id=1, source_target_pairs={{0,6},{1,7},{2,4},{3,5},{4,2},{5,3},{6,0},{7,1},{8,14},{9,15},{10,... | collective-permute-start | bytes 147464 | tf_op jit(solution)/shard_map/ppermute | solution.py:574
  39.4 4.7 %collective-permute-start.15 = (bf16[96,256]{1,0:T(8,128)(2,1)S(1)}, bf16[96,256]{1,0:T(8,128)(2,1)S(1)}, u32[]{:S(2)}, u32[]{:S(2)}) collective-permute-start(bf16[96,256]{1,0:T(8,128)(2,1)S(1)} %get-tuple-element.59.mine_ref), channel_id=1, source_target_pairs={{0,2},{1,3},{2,0},{3,1},{4,6},{5,7},{6,4},{7,5},{8,10},{9,11},{10,... | collective-permute-start | bytes 147464 | tf_op jit(solution)/shard_map/ppermute | solution.py:574
  44.1 5.7 %collective-permute-start.18 = (bf16[96,256]{1,0:T(8,128)(2,1)S(1)}, bf16[96,256]{1,0:T(8,128)(2,1)S(1)}, u32[]{:S(2)}, u32[]{:S(2)}) collective-permute-start(bf16[96,256]{1,0:T(8,128)(2,1)S(1)} %shard_map.103.a_ref), channel_id=1, source_target_pairs={{0,1},{1,0},{2,3},{3,2},{4,5},{5,4},{6,7},{7,6},{8,9},{9,8},{10,11... | collective-permute-start | bytes 147464 | tf_op jit(solution)/shard_map/ppermute | solution.py:592
  45.3 8.9 %copy-start = (s32[4]{0:T(128)S(1)}, s32[4]{0:T(128)}, u32[]{:S(2)}) copy-start(s32[4]{0:T(128)} %bins.1) | copy-start | bytes 52
  45.4 6.4 %collective-permute-start.14 = (bf16[96,256]{1,0:T(8,128)(2,1)S(1)}, bf16[96,256]{1,0:T(8,128)(2,1)S(1)}, u32[]{:S(2)}, u32[]{:S(2)}) collective-permute-start(bf16[96,256]{1,0:T(8,128)(2,1)S(1)} %shard_map.102.refs_0_), channel_id=1, source_target_pairs={{0,6},{1,7},{2,4},{3,5},{4,2},{5,3},{6,0},{7,1},{8,14},{9,15},{10,... | collective-permute-start | bytes 147464 | tf_op jit(solution)/shard_map/ppermute | solution.py:574
  47.3 8.2 %collective-permute-start.13 = (bf16[96,256]{1,0:T(8,128)(2,1)S(1)}, bf16[96,256]{1,0:T(8,128)(2,1)S(1)}, u32[]{:S(2)}, u32[]{:S(2)}) collective-permute-start(bf16[96,256]{1,0:T(8,128)(2,1)S(1)} %shard_map.102.refs_0_), channel_id=1, source_target_pairs={{0,4},{1,5},{2,6},{3,7},{4,0},{5,1},{6,2},{7,3},{8,12},{9,13},{10,... | collective-permute-start | bytes 147464 | tf_op jit(solution)/shard_map/ppermute | solution.py:574
  47.3 8.2 %collective-permute-start.12 = (bf16[96,256]{1,0:T(8,128)(2,1)S(1)}, bf16[96,256]{1,0:T(8,128)(2,1)S(1)}, u32[]{:S(2)}, u32[]{:S(2)}) collective-permute-start(bf16[96,256]{1,0:T(8,128)(2,1)S(1)} %shard_map.102.refs_0_), channel_id=1, source_target_pairs={{0,2},{1,3},{2,0},{3,1},{4,6},{5,7},{6,4},{7,5},{8,10},{9,11},{10,... | collective-permute-start | bytes 147464 | tf_op jit(solution)/shard_map/ppermute | solution.py:574
  49.8 6.5 %collective-permute-start.21 = (bf16[96,256]{1,0:T(8,128)(2,1)S(1)}, bf16[96,256]{1,0:T(8,128)(2,1)S(1)}, u32[]{:S(2)}, u32[]{:S(2)}) collective-permute-start(bf16[96,256]{1,0:T(8,128)(2,1)S(1)} %shard_map.104.refs_1_), channel_id=1, source_target_pairs={{0,6},{1,7},{2,4},{3,5},{4,2},{5,3},{6,0},{7,1},{8,14},{9,15},{10,... | collective-permute-start | bytes 147464 | tf_op jit(solution)/shard_map/ppermute | solution.py:574
  51.8 5.1 %collective-permute-start.20 = (bf16[96,256]{1,0:T(8,128)(2,1)S(1)}, bf16[96,256]{1,0:T(8,128)(2,1)S(1)}, u32[]{:S(2)}, u32[]{:S(2)}) collective-permute-start(bf16[96,256]{1,0:T(8,128)(2,1)S(1)} %shard_map.104.refs_1_), channel_id=1, source_target_pairs={{0,4},{1,5},{2,6},{3,7},{4,0},{5,1},{6,2},{7,3},{8,12},{9,13},{10,... | collective-permute-start | bytes 147464 | tf_op jit(solution)/shard_map/ppermute | solution.py:574
  51.8 5.1 %collective-permute-start.19 = (bf16[96,256]{1,0:T(8,128)(2,1)S(1)}, bf16[96,256]{1,0:T(8,128)(2,1)S(1)}, u32[]{:S(2)}, u32[]{:S(2)}) collective-permute-start(bf16[96,256]{1,0:T(8,128)(2,1)S(1)} %shard_map.104.refs_1_), channel_id=1, source_target_pairs={{0,2},{1,3},{2,0},{3,1},{4,6},{5,7},{6,4},{7,5},{8,10},{9,11},{10,... | collective-permute-start | bytes 147464 | tf_op jit(solution)/shard_map/ppermute | solution.py:574

commit v5 on v4

--- a/solution.py
+++ b/solution.py
@@ -276,7 +276,7 @@
     return wide[:half] + wide[half:]
 
 
-def add_terms(place, source, wide, x_ref, pre_ref, pre_rim, gain_ref, total, sums):
+def add_terms(place, source, wide, x_ref, pre_ref, pre_rim, gain_ref, total, sums, start=None):
     micro, rows, channels = x_ref.shape
     pad = (wide - rows) // 2
     inner = slice(pad, pad + rows)
@@ -287,7 +287,11 @@
         for tap, side in enumerate((later, grad_pre, earlier)):
             where = slice(tap * channels, (tap + 1) * channels)
             term = trans_times(x_ref[m], side[inner])
-            total[where] = total[where] + term if place or j else term
+            if j:
+                term = total[where] + term
+            elif start is not None:
+                term = start[where] + term
+            total[where] = term
         film = grad_pre[inner].astype(F32)
         pre = with_rim(pre_ref, pre_rim, m)[inner]
         scale = 1.0 / gain_ref[m]
@@ -302,21 +306,15 @@
 
 
 def last_kernel(outer, *refs):
-    x_ref, pre_ref, pre_rim, gain_ref, total_in, sums_in, d_mine, got_ref, d_ref = refs[:9]
-    own_refs = refs[9 : 9 + PARTS]
-    send_refs = refs[9 + PARTS : -2]
+    x_ref, pre_ref, pre_rim, gain_ref, total_in, sums_in, got_ref = refs[:7]
+    own_refs = refs[7 : 7 + PARTS]
+    send_refs = refs[7 + PARTS : -2]
     total, sums = refs[-2:]
-    micro, rows, _ = x_ref.shape
+    _, rows, _ = x_ref.shape
     wide = got_ref.shape[1] - rows
     mine = lax.axis_index("bulk") // 2
-    half = lax.axis_index("section") % 2
-    total[...] = total_in[...]
     sums[...] = sums_in[...]
-    add_terms(1, got_ref, wide, x_ref, pre_ref, pre_rim, gain_ref, total, sums)
-    for j, m in enumerate(turn(half, micro, 0)):
-        d_ref[m] = d_mine[j]
-    for j, m in enumerate(turn(half, micro, 1)):
-        d_ref[m] = got_ref[j, wide:]
+    add_terms(1, got_ref, wide, x_ref, pre_ref, pre_rim, gain_ref, total, sums, total_in)
     rows_out = split_rows(sums[...])
     extra = rows_out.shape[0]
     chunk = own_refs[0].shape[0]
@@ -358,6 +356,16 @@
     out_ref = refs[-1]
     extra = a_ref.shape[0] - out_ref.shape[0]
     out_ref[...] = (a_ref[extra:].astype(F32) + b_ref[extra:].astype(F32)).astype(BF16)
+
+
+def result_kernel(d_mine, got_ref, out_ref, sems):
+    count, rows = d_mine.shape[:2]
+    half = lax.axis_index("section") % 2
+    away = got_ref.at[:, pl.ds(got_ref.shape[1] - rows, rows), :]
+    pairs = [(d_mine, out_ref.at[pl.ds(half * count, count)])]
+    pairs.append((away, out_ref.at[pl.ds((1 - half) * count, count)]))
+    for copy in copies(pairs, sems):
+        copy.wait()
 
 
 def bins_kernel(micro, bins, a_ref, b_ref, gain_ref, shift_ref):
@@ -555,10 +563,9 @@
     messages = [shape_of((chunk + (0 if part else extra), channels), BF16) for part in range(PARTS)]
     made = call(
         functools.partial(last_kernel, outer),
-        [shape_of(x.shape, BF16)]
-        + [shape_of((chunk, channels), F32)] * PARTS
+        [shape_of((chunk, channels), F32)] * PARTS
         + [messages[part] for part in range(PARTS) for _ in range(outer - 1)],
-        shared + [total_own, sums_own, d_own, got_away],
+        shared + [total_own, sums_own, got_away],
         scratch=[
             pltpu.VMEM((3 * channels, channels), F32),
             pltpu.VMEM((2 * micro, channels), F32),
@@ -566,8 +573,17 @@
         flops=matmul,
         limit=16,
     )
-    d_local = made[0]
-    owns = made[1 : 1 + PARTS]
+    owns = made[:PARTS]
+    d_local = pl.pallas_call(
+        result_kernel,
+        in_specs=[pl.BlockSpec(memory_space=pltpu.VMEM)] * 2,
+        out_specs=pl.BlockSpec(memory_space=pltpu.HBM),
+        out_shape=shape_of(x.shape, BF16),
+        scratch_shapes=[pltpu.SemaphoreType.DMA((2,))],
+        compiler_params=pltpu.CompilerParams(vmem_limit_bytes=4 << 20),
+        cost_estimate=cost(1, 1 << 20),
+        name="results",
+    )(d_own, got_away)
 
     def across(value, k):
         pairs = [(i, i ^ (2 * k)) for i in range(bulk_count)]
@@ -577,7 +593,7 @@
     order = [k for k in range(2, outer)] + [1]
     scattered = []
     for part in range(PARTS):
-        sends = made[1 + PARTS + part * (outer - 1) :][: outer - 1]
+        sends = made[PARTS + part * (outer - 1) :][: outer - 1]
         got = {k: across(sends[k - 1], k) for k in order}
         scattered.append((sends[0], got))
     summed = []

time: 57.8 us -> 57.4 us (level)
  waiting for transfers between devices: 20.5 us -> 19.9 us
    pallas_call x0 -> x1, Pallas kernels: none -> 0.8 us  [step(): pl.pallas_call(result_kernel, in_specs=[pl.BlockSpec(memory_space=pltpu.V...]
    pallas_call x13, Pallas kernels: 6.52 us -> 5.76 us  [call(): pl.pallas_call(kernel, in_specs=[smem] * len(scalars) + [kept] * len(remo...]
    ppermute x12, waiting for transfers between devices: 9.25 us -> 8.67 us  [across(): return lax.ppermute(value, 'bulk', pairs)]
  transfers between devices with their start and end apart: 22 -> 22, of which waited for: 10 -> 9; matrix products, arithmetic and copies ran while one was open for 0% -> 0% of each run, Pallas kernels for 5% -> 6%
where the time goes in v5:
time: 57.4 us; the launch traced here: 57.3 us
  starting transfers between devices  28.4 us (49%)
  waiting for transfers between devices  19.9 us (35%)
  Pallas kernels  8.17 us (14%)
  between operations  0.77 us (1%)
    ppermute x12, starting transfers between devices, across(): return lax.ppermute(value, 'bulk', pairs)  15.9 us
    ppermute x12, waiting for transfers between devices, across(): return lax.ppermute(value, 'bulk', pairs)  8.67 us
    pallas_call x13, Pallas kernels, call(): pl.pallas_call(kernel, in_specs=[smem] * len(scalars) + [kept] * len(remo...  5.76 us
    ppermute x4, waiting for transfers between devices, to_other(): return lax.ppermute(value, 'section', [(i, i ^ 1) for i in range(sections)])  4.86 us
    ppermute x2, starting transfers between devices, down(): lax.ppermute(value, 'section', pairs + [(low, high) for high, low in pairs])  4.55 us
    ppermute x1, starting transfers between devices, step(): far = lax.ppermute(far, 'bulk', opposite)  3.54 us
    ppermute x1, waiting for transfers between devices, step(): far = lax.ppermute(far, 'bulk', opposite)  3.24 us
    ppermute x2, waiting for transfers between devices, down(): lax.ppermute(value, 'section', pairs + [(low, high) for high, low in pairs])  3.15 us
  transfers between devices with their start and end apart: 22, of which 9 were waited for; matrix products, arithmetic and copies ran while one was open for 0% of the time, Pallas kernels for 6%

profile of v5, /device:TPU:0, one launch (start us, length us, event | category | flops | bytes accessed | tf_op | source)
XLA Modules:
  0.0 57.3 jit_solution(8397931294623618510)
XLA Ops:
  0.6 1.3 %shard_map.93 = (bf16[6,16,256]{2,1,0:T(8,128)(2,1)S(1)}, bf16[6,16,256]{2,1,0:T(8,128)(2,1)S(1)}, bf16[4,256,256]{2,1,0:T(8,128)(2,1)S(1)}, bf16[2,256,256]{2,1...) custom-call(s32[4]{0:T(128)} %bins.1, ...), custom_call_target="tpu_custom_call" | custom-call | flops 1 | bytes 1048576 | tf_op jit(solution)/shard_map/pallas_call | solution.py:423
  2.0 0.9 %shard_map.94 = (f32[2,256,256]{2,1,0:T(8,128)S(1)}, f32[2,256,256]{2,1,0:T(8,128)S(1)}, f32[4,256,256]{2,1,0:T(8,128)S(1)}) custom-call(bf16[4,256,256]{2,1,0:T(8,128)(2,1)S(1)} %get-tuple-element.33.x_ref.refs_0_, bf16[3,256,256]{2,1,0:T(8,128)(2,1)S(1)} %get-tuple-element.34.w_ref.refs_1_.refs_2_, f32[4,1,256]{2,1,0:T(1,128)S(1)} %get-tuple-element.35.gain_ref.refs_3_, ...), custom_call_target="tpu_custom_call" | custom-call | flops 452984832 | bytes 1048576 | tf_op jit(solution)/shard_map/pallas_call | solution.py:423
  2.9 0.6 collective-permute-start.2
  3.4 0.1 collective-permute-start.4
  3.5 2.0 %collective-permute-done.4.refs_3_.refs_5_ = bf16[3,256,256]{2,1,0:T(8,128)(2,1)S(1)} collective-permute-done((bf16[3,256,256]{2,1,0:T(8,128)(2,1)S(1)}, bf16[3,256,256]{2,1,0:T(8,128)(2,1)S(1)}, u32[]{:S(2)}, u32[]{:S(2)}) %collective-permute-start.4) | collective-permute-done | bytes 393248 | tf_op jit(solution)/shard_map/ppermute | solution.py:482
  5.5 0.0 collective-permute-done.2.refs_2_.refs_3_
  5.5 3.8 %collective-permute-start.5 = (bf16[2,240,256]{2,1,0:T(8,128)(2,1)S(1)}, bf16[2,240,256]{2,1,0:T(8,128)(2,1)S(1)}, u32[]{:S(2)}, u32[]{:S(2)}) collective-permute-start(bf16[2,240,256]{2,1,0:T(8,128)(2,1)S(1)} %shard_map.96), channel_id=1, source_target_pairs={{16,0},{24,8},{0,16},{8,24},{17,1},{25,9},{1,17},{9,25},{18,2},{26... | collective-permute-start | bytes 737288 | tf_op jit(solution)/shard_map/ppermute | solution.py:507
  9.3 1.5 %collective-permute-start = (bf16[6,16,256]{2,1,0:T(8,128)(2,1)S(1)}, bf16[6,16,256]{2,1,0:T(8,128)(2,1)S(1)}, u32[]{:S(2)}, u32[]{:S(2)}) collective-permute-start(bf16[6,16,256]{2,1,0:T(8,128)(2,1)S(1)} %get-tuple-element.38), channel_id=1, source_target_pairs={{0,1},{1,0},{2,3},{3,2},{4,5},{5,4},{6,7},{7,6},{8,9},{9,8},{10,11... | collective-permute-start | bytes 147464 | tf_op jit(solution)/shard_map/ppermute | solution.py:466
  10.9 3.5 %collective-permute-start.1 = (bf16[6,16,256]{2,1,0:T(8,128)(2,1)S(1)}, bf16[6,16,256]{2,1,0:T(8,128)(2,1)S(1)}, u32[]{:S(2)}, u32[]{:S(2)}) collective-permute-start(bf16[6,16,256]{2,1,0:T(8,128)(2,1)S(1)} %get-tuple-element.39), channel_id=1, source_target_pairs={{0,7},{1,2},{2,1},{3,4},{4,3},{5,6},{6,5},{7,0},{8,15},{9,10},{10,... | collective-permute-start | bytes 147464 | tf_op jit(solution)/shard_map/ppermute | solution.py:465
  14.4 0.0 collective-permute-done.near_ref
  14.4 3.2 %collective-permute-done.1.far_ref = bf16[6,16,256]{2,1,0:T(8,128)(2,1)S(1)} collective-permute-done((bf16[6,16,256]{2,1,0:T(8,128)(2,1)S(1)}, bf16[6,16,256]{2,1,0:T(8,128)(2,1)S(1)}, u32[]{:S(2)}, u32[]{:S(2)}) %collective-permute-start.1) | collective-permute-done | bytes 49184 | tf_op jit(solution)/shard_map/ppermute | solution.py:465
  17.6 0.3 shard_map.95
  18.0 0.1 collective-permute-start.3
  18.1 1.3 %collective-permute-done.3.refs_2_.refs_4_ = f32[2,2,32,256]{3,2,1,0:T(8,128)S(1)} collective-permute-done((f32[2,2,32,256]{3,2,1,0:T(8,128)S(1)}, f32[2,2,32,256]{3,2,1,0:T(8,128)S(1)}, u32[]{:S(2)}, u32[]{:S(2)}) %collective-permute-start.3) | collective-permute-done | bytes 131104 | tf_op jit(solution)/shard_map/ppermute | solution.py:482
  19.4 0.8 %collective-permute-start.6 = (bf16[2,2,16,256]{3,2,1,0:T(8,128)(2,1)S(1)}, bf16[2,2,16,256]{3,2,1,0:T(8,128)(2,1)S(1)}, u32[]{:S(2)}, u32[]{:S(2)}) collective-permute-start(bf16[2,2,16,256]{3,2,1,0:T(8,128)(2,1)S(1)} %shard_map.97), channel_id=1, source_target_pairs={{16,0},{24,8},{0,16},{8,24},{17,1},{25,9},{1,17},{9,25},{18,2},{26... | collective-permute-start | bytes 98312 | tf_op jit(solution)/shard_map/ppermute | solution.py:507
  20.2 3.1 %collective-permute-done.6.refs_9_ = bf16[2,2,16,256]{3,2,1,0:T(8,128)(2,1)S(1)} collective-permute-done((bf16[2,2,16,256]{3,2,1,0:T(8,128)(2,1)S(1)}, bf16[2,2,16,256]{3,2,1,0:T(8,128)(2,1)S(1)}, u32[]{:S(2)}, u32[]{:S(2)}) %collective-permute-start.6) | collective-permute-done | bytes 32800 | tf_op jit(solution)/shard_map/ppermute | solution.py:507
  23.3 0.0 collective-permute-done.5.refs_8_
  23.3 1.0 %shard_map.98 = (bf16[2,288,256]{2,1,0:T(8,128)(2,1)S(1)}, bf16[2,256,256]{2,1,0:T(8,128)(2,1)S(1)}, bf16[2,544,256]{2,1,0:T(8,128)(2,1)S(1)}) custom-call(f32[2,256,256]{2,1,0:T(8,128)S(1)} %get-tuple-element.37.refs_0_, f32[2,2,32,256]{3,2,1,0:T(8,128)S(1)} %get-tuple-element.40.refs_0_.refs_1_, ...), custom_call_target="tpu_custom_call" | custom-call | flops 452984832 | bytes 1048576 | tf_op jit(solution)/shard_map/pallas_call | solution.py:423
  24.3 0.1 collective-permute-start.7
  24.4 0.4 shard_map.99
  24.8 1.5 %collective-permute-done.7.got_ref.refs_6_ = bf16[2,544,256]{2,1,0:T(8,128)(2,1)S(1)} collective-permute-done((bf16[2,544,256]{2,1,0:T(8,128)(2,1)S(1)}, bf16[2,544,256]{2,1,0:T(8,128)(2,1)S(1)}, u32[]{:S(2)}, u32[]{:S(2)}) %collective-permute-start.7) | collective-permute-done | bytes 557088 | tf_op jit(solution)/shard_map/ppermute | solution.py:482
  26.3 0.5 shard_map.100
  26.8 0.9 %collective-permute-start.9 = (bf16[112,256]{1,0:T(8,128)(2,1)S(1)}, bf16[112,256]{1,0:T(8,128)(2,1)S(1)}, u32[]{:S(2)}, u32[]{:S(2)}) collective-permute-start(bf16[112,256]{1,0:T(8,128)(2,1)S(1)} %get-tuple-element.54), channel_id=1, source_target_pairs={{0,4},{1,5},{2,6},{3,7},{4,0},{5,1},{6,2},{7,3},{8,12},{9,13},{10,... | collective-permute-start | bytes 172040 | tf_op jit(solution)/shard_map/ppermute | solution.py:590
  27.7 1.3 %collective-permute-start.10 = (bf16[112,256]{1,0:T(8,128)(2,1)S(1)}, bf16[112,256]{1,0:T(8,128)(2,1)S(1)}, u32[]{:S(2)}, u32[]{:S(2)}) collective-permute-start(bf16[112,256]{1,0:T(8,128)(2,1)S(1)} %get-tuple-element.55), channel_id=1, source_target_pairs={{0,6},{1,7},{2,4},{3,5},{4,2},{5,3},{6,0},{7,1},{8,14},{9,15},{10,... | collective-permute-start | bytes 172040 | tf_op jit(solution)/shard_map/ppermute | solution.py:590
  29.0 1.4 %collective-permute-start.8 = (bf16[112,256]{1,0:T(8,128)(2,1)S(1)}, bf16[112,256]{1,0:T(8,128)(2,1)S(1)}, u32[]{:S(2)}, u32[]{:S(2)}) collective-permute-start(bf16[112,256]{1,0:T(8,128)(2,1)S(1)} %get-tuple-element.53.mine_ref), channel_id=1, source_target_pairs={{0,2},{1,3},{2,0},{3,1},{4,6},{5,7},{6,4},{7,5},{8,10},{9,11},{10,... | collective-permute-start | bytes 172040 | tf_op jit(solution)/shard_map/ppermute | solution.py:590
  30.4 3.5 %collective-permute-done.9.refs_1_ = bf16[112,256]{1,0:T(8,128)(2,1)S(1)} collective-permute-done((bf16[112,256]{1,0:T(8,128)(2,1)S(1)}, bf16[112,256]{1,0:T(8,128)(2,1)S(1)}, u32[]{:S(2)}, u32[]{:S(2)}) %collective-permute-start.9) | collective-permute-done | bytes 57376 | tf_op jit(solution)/shard_map/ppermute | solution.py:590
  33.8 0.0 collective-permute-done.10.refs_2_
  33.8 0.9 %collective-permute-done.8.refs_0_ = bf16[112,256]{1,0:T(8,128)(2,1)S(1)} collective-permute-done((bf16[112,256]{1,0:T(8,128)(2,1)S(1)}, bf16[112,256]{1,0:T(8,128)(2,1)S(1)}, u32[]{:S(2)}, u32[]{:S(2)}) %collective-permute-start.8) | collective-permute-done | bytes 57376 | tf_op jit(solution)/shard_map/ppermute | solution.py:590
  34.8 0.9 %collective-permute-start.11 = (bf16[112,256]{1,0:T(8,128)(2,1)S(1)}, bf16[112,256]{1,0:T(8,128)(2,1)S(1)}, u32[]{:S(2)}, u32[]{:S(2)}) collective-permute-start(bf16[112,256]{1,0:T(8,128)(2,1)S(1)} %shard_map.101.a_ref), channel_id=1, source_target_pairs={{0,1},{1,0},{2,3},{3,2},{4,5},{5,4},{6,7},{7,6},{8,9},{9,8},{10,11... | collective-permute-start | bytes 172040 | tf_op jit(solution)/shard_map/ppermute | solution.py:608
  35.6 1.9 %collective-permute-start.16 = (bf16[96,256]{1,0:T(8,128)(2,1)S(1)}, bf16[96,256]{1,0:T(8,128)(2,1)S(1)}, u32[]{:S(2)}, u32[]{:S(2)}) collective-permute-start(bf16[96,256]{1,0:T(8,128)(2,1)S(1)} %get-tuple-element.58), channel_id=1, source_target_pairs={{0,4},{1,5},{2,6},{3,7},{4,0},{5,1},{6,2},{7,3},{8,12},{9,13},{10,... | collective-permute-start | bytes 147464 | tf_op jit(solution)/shard_map/ppermute | solution.py:590
  37.5 1.2 %collective-permute-start.17 = (bf16[96,256]{1,0:T(8,128)(2,1)S(1)}, bf16[96,256]{1,0:T(8,128)(2,1)S(1)}, u32[]{:S(2)}, u32[]{:S(2)}) collective-permute-start(bf16[96,256]{1,0:T(8,128)(2,1)S(1)} %get-tuple-element.59), channel_id=1, source_target_pairs={{0,6},{1,7},{2,4},{3,5},{4,2},{5,3},{6,0},{7,1},{8,14},{9,15},{10,... | collective-permute-start | bytes 147464 | tf_op jit(solution)/shard_map/ppermute | solution.py:590
  38.7 0.4 collective-permute-start.15
  39.1 3.0 %collective-permute-done.16.refs_1_ = bf16[96,256]{1,0:T(8,128)(2,1)S(1)} collective-permute-done((bf16[96,256]{1,0:T(8,128)(2,1)S(1)}, bf16[96,256]{1,0:T(8,128)(2,1)S(1)}, u32[]{:S(2)}, u32[]{:S(2)}) %collective-permute-start.16) | collective-permute-done | bytes 49184 | tf_op jit(solution)/shard_map/ppermute | solution.py:590
  42.1 1.3 %collective-permute-done.17.refs_2_ = bf16[96,256]{1,0:T(8,128)(2,1)S(1)} collective-permute-done((bf16[96,256]{1,0:T(8,128)(2,1)S(1)}, bf16[96,256]{1,0:T(8,128)(2,1)S(1)}, u32[]{:S(2)}, u32[]{:S(2)}) %collective-permute-start.17) | collective-permute-done | bytes 49184 | tf_op jit(solution)/shard_map/ppermute | solution.py:590
  43.4 0.0 collective-permute-done.15.refs_0_
  43.4 1.2 %collective-permute-start.18 = (bf16[96,256]{1,0:T(8,128)(2,1)S(1)}, bf16[96,256]{1,0:T(8,128)(2,1)S(1)}, u32[]{:S(2)}, u32[]{:S(2)}) collective-permute-start(bf16[96,256]{1,0:T(8,128)(2,1)S(1)} %shard_map.103.a_ref), channel_id=1, source_target_pairs={{0,1},{1,0},{2,3},{3,2},{4,5},{5,4},{6,7},{7,6},{8,9},{9,8},{10,11... | collective-permute-start | bytes 147464 | tf_op jit(solution)/shard_map/ppermute | solution.py:608
  44.6 0.0 collective-permute-done.11.b_ref
  44.6 2.0 %collective-permute-start.14 = (bf16[96,256]{1,0:T(8,128)(2,1)S(1)}, bf16[96,256]{1,0:T(8,128)(2,1)S(1)}, u32[]{:S(2)}, u32[]{:S(2)}) collective-permute-start(bf16[96,256]{1,0:T(8,128)(2,1)S(1)} %shard_map.102.refs_0_), channel_id=1, source_target_pairs={{0,6},{1,7},{2,4},{3,5},{4,2},{5,3},{6,0},{7,1},{8,14},{9,15},{10,... | collective-permute-start | bytes 147464 | tf_op jit(solution)/shard_map/ppermute | solution.py:590
  46.6 0.0 collective-permute-start.13
  46.6 2.5 %collective-permute-start.12 = (bf16[96,256]{1,0:T(8,128)(2,1)S(1)}, bf16[96,256]{1,0:T(8,128)(2,1)S(1)}, u32[]{:S(2)}, u32[]{:S(2)}) collective-permute-start(bf16[96,256]{1,0:T(8,128)(2,1)S(1)} %shard_map.102.refs_0_), channel_id=1, source_target_pairs={{0,2},{1,3},{2,0},{3,1},{4,6},{5,7},{6,4},{7,5},{8,10},{9,11},{10,... | collective-permute-start | bytes 147464 | tf_op jit(solution)/shard_map/ppermute | solution.py:590
  49.1 0.0 collective-permute-done.18.b_ref
  49.1 2.0 %collective-permute-start.21 = (bf16[96,256]{1,0:T(8,128)(2,1)S(1)}, bf16[96,256]{1,0:T(8,128)(2,1)S(1)}, u32[]{:S(2)}, u32[]{:S(2)}) collective-permute-start(bf16[96,256]{1,0:T(8,128)(2,1)S(1)} %shard_map.104.refs_1_), channel_id=1, source_target_pairs={{0,6},{1,7},{2,4},{3,5},{4,2},{5,3},{6,0},{7,1},{8,14},{9,15},{10,... | collective-permute-start | bytes 147464 | tf_op jit(solution)/shard_map/ppermute | solution.py:590
  51.1 0.0 collective-permute-start.20
  51.1 0.0 collective-permute-done.14.refs_3_
  51.1 2.5 %collective-permute-start.19 = (bf16[96,256]{1,0:T(8,128)(2,1)S(1)}, bf16[96,256]{1,0:T(8,128)(2,1)S(1)}, u32[]{:S(2)}, u32[]{:S(2)}) collective-permute-start(bf16[96,256]{1,0:T(8,128)(2,1)S(1)} %shard_map.104.refs_1_), channel_id=1, source_target_pairs={{0,2},{1,3},{2,0},{3,1},{4,6},{5,7},{6,4},{7,5},{8,10},{9,11},{10,... | collective-permute-start | bytes 147464 | tf_op jit(solution)/shard_map/ppermute | solution.py:590
  53.6 0.0 copy-start
  53.6 0.8 %results.1 = bf16[4,256,256]{2,1,0:T(8,128)(2,1)} custom-call(bf16[2,256,256]{2,1,0:T(8,128)(2,1)S(1)} %get-tuple-element.45.d_mine, bf16[2,544,256]{2,1,0:T(8,128)(2,1)S(1)} %collective-permute-done.7.got_ref.refs_6_), custom_call_target="tpu_custom_call" | custom-call | flops 1 | bytes 1048576 | tf_op jit(solution)/shard_map/results/pallas_call | solution.py:577
  54.4 0.0 copy-done
  54.4 1.2 %shard_map.105 = (f32[36,1,256]{2,1,0:T(1,128)}, f32[36,1,256]{2,1,0:T(1,128)}) custom-call(s32[4]{0:T(128)S(1)} %copy-done, bf16[112,256]{1,0:T(8,128)(2,1)S(1)} %shard_map.101.a_ref, bf16[112,256]{1,0:T(8,128)(2,1)S(1)} %collective-permute-done.11.b_ref), custom_call_target="tpu_custom_call" | custom-call | flops 1 | bytes 1048576 | tf_op jit(solution)/shard_map/pallas_call | solution.py:423
  55.6 0.0 collective-permute-done.13.refs_2_
  55.6 0.0 collective-permute-done.12.refs_1_
  55.6 0.8 %spread.2.refs_0_ = f32[768,256]{1,0:T(8,128)} custom-call(bf16[96,256]{1,0:T(8,128)(2,1)S(1)} %shard_map.102.refs_0_, bf16[96,256]{1,0:T(8,128)(2,1)S(1)} %collective-permute-done.12.refs_1_, bf16[96,256]{1,0:T(8,128)(2,1)S(1)} %collective-permute-done.13.refs_2_, bf16[96,256]{1,0:T(8,128)(2,1)S(1)} %collective-permute-done.14.refs_3_), custom_call_target="tpu_custom_call" | custom-call | flops 1 | bytes 1048576 | tf_op jit(solution)/shard_map/spread/pallas_call | solution.py:398
  56.4 0.0 collective-permute-done.21.refs_4_
  56.4 0.0 collective-permute-done.20.refs_3_
  56.4 0.0 collective-permute-done.19.refs_2_
  56.5 0.8 %spread.3 = f32[768,256]{1,0:T(8,128)} custom-call(f32[768,256]{1,0:T(8,128)} %spread.2.refs_0_, bf16[96,256]{1,0:T(8,128)(2,1)S(1)} %shard_map.104.refs_1_, bf16[96,256]{1,0:T(8,128)(2,1)S(1)} %collective-permute-done.19.refs_2_, bf16[96,256]{1,0:T(8,128)(2,1)S(1)} %collective-permute-done.20.refs_3_, ...), custom_call_target="tpu_custom_call", output_to_operand_aliasing={{}: (0, {})} | custom-call | flops 1 | bytes 1048576 | tf_op jit(solution)/shard_map/spread/pallas_call | solution.py:398
  (6 shorter events, 0.1 us)
Async XLA Ops:
  2.9 2.7 %collective-permute-start.2 = (f32[2,256,256]{2,1,0:T(8,128)S(1)}, f32[2,256,256]{2,1,0:T(8,128)S(1)}, u32[]{:S(2)}, u32[]{:S(2)}) collective-permute-start(f32[2,256,256]{2,1,0:T(8,128)S(1)} %get-tuple-element.41), channel_id=1, source_target_pairs={{0,8},{8,0},{16,24},{24,16},{1,9},{9,1},{17,25},{25,17},{2,10},{10... | collective-permute-start | bytes 1572872 | tf_op jit(solution)/shard_map/ppermute | solution.py:482
  3.4 2.1 %collective-permute-start.4 = (bf16[3,256,256]{2,1,0:T(8,128)(2,1)S(1)}, bf16[3,256,256]{2,1,0:T(8,128)(2,1)S(1)}, u32[]{:S(2)}, u32[]{:S(2)}) collective-permute-start(bf16[3,256,256]{2,1,0:T(8,128)(2,1)S(1)} %get-tuple-element.34.w_ref.refs_1_.refs_2_), channel_id=1, source_target_pairs={{0,8},{8,0},{16,24},{24,16},{1,9},{9,1},{17,25},{25,17},{2,10},{10... | collective-permute-start | bytes 1179656 | tf_op jit(solution)/shard_map/ppermute | solution.py:482
  5.5 17.8 %collective-permute-start.5 = (bf16[2,240,256]{2,1,0:T(8,128)(2,1)S(1)}, bf16[2,240,256]{2,1,0:T(8,128)(2,1)S(1)}, u32[]{:S(2)}, u32[]{:S(2)}) collective-permute-start(bf16[2,240,256]{2,1,0:T(8,128)(2,1)S(1)} %shard_map.96), channel_id=1, source_target_pairs={{16,0},{24,8},{0,16},{8,24},{17,1},{25,9},{1,17},{9,25},{18,2},{26... | collective-permute-start | bytes 737288 | tf_op jit(solution)/shard_map/ppermute | solution.py:507
  9.3 5.1 %collective-permute-start = (bf16[6,16,256]{2,1,0:T(8,128)(2,1)S(1)}, bf16[6,16,256]{2,1,0:T(8,128)(2,1)S(1)}, u32[]{:S(2)}, u32[]{:S(2)}) collective-permute-start(bf16[6,16,256]{2,1,0:T(8,128)(2,1)S(1)} %get-tuple-element.38), channel_id=1, source_target_pairs={{0,1},{1,0},{2,3},{3,2},{4,5},{5,4},{6,7},{7,6},{8,9},{9,8},{10,11... | collective-permute-start | bytes 147464 | tf_op jit(solution)/shard_map/ppermute | solution.py:466
  10.9 6.8 %collective-permute-start.1 = (bf16[6,16,256]{2,1,0:T(8,128)(2,1)S(1)}, bf16[6,16,256]{2,1,0:T(8,128)(2,1)S(1)}, u32[]{:S(2)}, u32[]{:S(2)}) collective-permute-start(bf16[6,16,256]{2,1,0:T(8,128)(2,1)S(1)} %get-tuple-element.39), channel_id=1, source_target_pairs={{0,7},{1,2},{2,1},{3,4},{4,3},{5,6},{6,5},{7,0},{8,15},{9,10},{10,... | collective-permute-start | bytes 147464 | tf_op jit(solution)/shard_map/ppermute | solution.py:465
  18.0 1.4 %collective-permute-start.3 = (f32[2,2,32,256]{3,2,1,0:T(8,128)S(1)}, f32[2,2,32,256]{3,2,1,0:T(8,128)S(1)}, u32[]{:S(2)}, u32[]{:S(2)}) collective-permute-start(f32[2,2,32,256]{3,2,1,0:T(8,128)S(1)} %get-tuple-element.42), channel_id=1, source_target_pairs={{0,8},{8,0},{16,24},{24,16},{1,9},{9,1},{17,25},{25,17},{2,10},{10... | collective-permute-start | bytes 393224 | tf_op jit(solution)/shard_map/ppermute | solution.py:482
  19.4 3.9 %collective-permute-start.6 = (bf16[2,2,16,256]{3,2,1,0:T(8,128)(2,1)S(1)}, bf16[2,2,16,256]{3,2,1,0:T(8,128)(2,1)S(1)}, u32[]{:S(2)}, u32[]{:S(2)}) collective-permute-start(bf16[2,2,16,256]{3,2,1,0:T(8,128)(2,1)S(1)} %shard_map.97), channel_id=1, source_target_pairs={{16,0},{24,8},{0,16},{8,24},{17,1},{25,9},{1,17},{9,25},{18,2},{26... | collective-permute-start | bytes 98312 | tf_op jit(solution)/shard_map/ppermute | solution.py:507
  24.3 2.0 %collective-permute-start.7 = (bf16[2,544,256]{2,1,0:T(8,128)(2,1)S(1)}, bf16[2,544,256]{2,1,0:T(8,128)(2,1)S(1)}, u32[]{:S(2)}, u32[]{:S(2)}) collective-permute-start(bf16[2,544,256]{2,1,0:T(8,128)(2,1)S(1)} %get-tuple-element.46), channel_id=1, source_target_pairs={{0,8},{8,0},{16,24},{24,16},{1,9},{9,1},{17,25},{25,17},{2,10},{10... | collective-permute-start | bytes 1671176 | tf_op jit(solution)/shard_map/ppermute | solution.py:482
  26.8 7.0 %collective-permute-start.9 = (bf16[112,256]{1,0:T(8,128)(2,1)S(1)}, bf16[112,256]{1,0:T(8,128)(2,1)S(1)}, u32[]{:S(2)}, u32[]{:S(2)}) collective-permute-start(bf16[112,256]{1,0:T(8,128)(2,1)S(1)} %get-tuple-element.54), channel_id=1, source_target_pairs={{0,4},{1,5},{2,6},{3,7},{4,0},{5,1},{6,2},{7,3},{8,12},{9,13},{10,... | collective-permute-start | bytes 172040 | tf_op jit(solution)/shard_map/ppermute | solution.py:590
  27.7 6.2 %collective-permute-start.10 = (bf16[112,256]{1,0:T(8,128)(2,1)S(1)}, bf16[112,256]{1,0:T(8,128)(2,1)S(1)}, u32[]{:S(2)}, u32[]{:S(2)}) collective-permute-start(bf16[112,256]{1,0:T(8,128)(2,1)S(1)} %get-tuple-element.55), channel_id=1, source_target_pairs={{0,6},{1,7},{2,4},{3,5},{4,2},{5,3},{6,0},{7,1},{8,14},{9,15},{10,... | collective-permute-start | bytes 172040 | tf_op jit(solution)/shard_map/ppermute | solution.py:590
  29.0 5.7 %collective-permute-start.8 = (bf16[112,256]{1,0:T(8,128)(2,1)S(1)}, bf16[112,256]{1,0:T(8,128)(2,1)S(1)}, u32[]{:S(2)}, u32[]{:S(2)}) collective-permute-start(bf16[112,256]{1,0:T(8,128)(2,1)S(1)} %get-tuple-element.53.mine_ref), channel_id=1, source_target_pairs={{0,2},{1,3},{2,0},{3,1},{4,6},{5,7},{6,4},{7,5},{8,10},{9,11},{10,... | collective-permute-start | bytes 172040 | tf_op jit(solution)/shard_map/ppermute | solution.py:590
  34.8 9.8 %collective-permute-start.11 = (bf16[112,256]{1,0:T(8,128)(2,1)S(1)}, bf16[112,256]{1,0:T(8,128)(2,1)S(1)}, u32[]{:S(2)}, u32[]{:S(2)}) collective-permute-start(bf16[112,256]{1,0:T(8,128)(2,1)S(1)} %shard_map.101.a_ref), channel_id=1, source_target_pairs={{0,1},{1,0},{2,3},{3,2},{4,5},{5,4},{6,7},{7,6},{8,9},{9,8},{10,11... | collective-permute-start | bytes 172040 | tf_op jit(solution)/shard_map/ppermute | solution.py:608
  35.6 6.5 %collective-permute-start.16 = (bf16[96,256]{1,0:T(8,128)(2,1)S(1)}, bf16[96,256]{1,0:T(8,128)(2,1)S(1)}, u32[]{:S(2)}, u32[]{:S(2)}) collective-permute-start(bf16[96,256]{1,0:T(8,128)(2,1)S(1)} %get-tuple-element.58), channel_id=1, source_target_pairs={{0,4},{1,5},{2,6},{3,7},{4,0},{5,1},{6,2},{7,3},{8,12},{9,13},{10,... | collective-permute-start | bytes 147464 | tf_op jit(solution)/shard_map/ppermute | solution.py:590
  37.5 5.9 %collective-permute-start.17 = (bf16[96,256]{1,0:T(8,128)(2,1)S(1)}, bf16[96,256]{1,0:T(8,128)(2,1)S(1)}, u32[]{:S(2)}, u32[]{:S(2)}) collective-permute-start(bf16[96,256]{1,0:T(8,128)(2,1)S(1)} %get-tuple-element.59), channel_id=1, source_target_pairs={{0,6},{1,7},{2,4},{3,5},{4,2},{5,3},{6,0},{7,1},{8,14},{9,15},{10,... | collective-permute-start | bytes 147464 | tf_op jit(solution)/shard_map/ppermute | solution.py:590
  38.7 4.7 %collective-permute-start.15 = (bf16[96,256]{1,0:T(8,128)(2,1)S(1)}, bf16[96,256]{1,0:T(8,128)(2,1)S(1)}, u32[]{:S(2)}, u32[]{:S(2)}) collective-permute-start(bf16[96,256]{1,0:T(8,128)(2,1)S(1)} %get-tuple-element.57.mine_ref), channel_id=1, source_target_pairs={{0,2},{1,3},{2,0},{3,1},{4,6},{5,7},{6,4},{7,5},{8,10},{9,11},{10,... | collective-permute-start | bytes 147464 | tf_op jit(solution)/shard_map/ppermute | solution.py:590
  43.4 5.7 %collective-permute-start.18 = (bf16[96,256]{1,0:T(8,128)(2,1)S(1)}, bf16[96,256]{1,0:T(8,128)(2,1)S(1)}, u32[]{:S(2)}, u32[]{:S(2)}) collective-permute-start(bf16[96,256]{1,0:T(8,128)(2,1)S(1)} %shard_map.103.a_ref), channel_id=1, source_target_pairs={{0,1},{1,0},{2,3},{3,2},{4,5},{5,4},{6,7},{7,6},{8,9},{9,8},{10,11... | collective-permute-start | bytes 147464 | tf_op jit(solution)/shard_map/ppermute | solution.py:608
  44.6 6.4 %collective-permute-start.14 = (bf16[96,256]{1,0:T(8,128)(2,1)S(1)}, bf16[96,256]{1,0:T(8,128)(2,1)S(1)}, u32[]{:S(2)}, u32[]{:S(2)}) collective-permute-start(bf16[96,256]{1,0:T(8,128)(2,1)S(1)} %shard_map.102.refs_0_), channel_id=1, source_target_pairs={{0,6},{1,7},{2,4},{3,5},{4,2},{5,3},{6,0},{7,1},{8,14},{9,15},{10,... | collective-permute-start | bytes 147464 | tf_op jit(solution)/shard_map/ppermute | solution.py:590
  46.6 9.0 %collective-permute-start.13 = (bf16[96,256]{1,0:T(8,128)(2,1)S(1)}, bf16[96,256]{1,0:T(8,128)(2,1)S(1)}, u32[]{:S(2)}, u32[]{:S(2)}) collective-permute-start(bf16[96,256]{1,0:T(8,128)(2,1)S(1)} %shard_map.102.refs_0_), channel_id=1, source_target_pairs={{0,4},{1,5},{2,6},{3,7},{4,0},{5,1},{6,2},{7,3},{8,12},{9,13},{10,... | collective-permute-start | bytes 147464 | tf_op jit(solution)/shard_map/ppermute | solution.py:590
  46.6 9.0 %collective-permute-start.12 = (bf16[96,256]{1,0:T(8,128)(2,1)S(1)}, bf16[96,256]{1,0:T(8,128)(2,1)S(1)}, u32[]{:S(2)}, u32[]{:S(2)}) collective-permute-start(bf16[96,256]{1,0:T(8,128)(2,1)S(1)} %shard_map.102.refs_0_), channel_id=1, source_target_pairs={{0,2},{1,3},{2,0},{3,1},{4,6},{5,7},{6,4},{7,5},{8,10},{9,11},{10,... | collective-permute-start | bytes 147464 | tf_op jit(solution)/shard_map/ppermute | solution.py:590
  49.1 7.3 %collective-permute-start.21 = (bf16[96,256]{1,0:T(8,128)(2,1)S(1)}, bf16[96,256]{1,0:T(8,128)(2,1)S(1)}, u32[]{:S(2)}, u32[]{:S(2)}) collective-permute-start(bf16[96,256]{1,0:T(8,128)(2,1)S(1)} %shard_map.104.refs_1_), channel_id=1, source_target_pairs={{0,6},{1,7},{2,4},{3,5},{4,2},{5,3},{6,0},{7,1},{8,14},{9,15},{10,... | collective-permute-start | bytes 147464 | tf_op jit(solution)/shard_map/ppermute | solution.py:590
  51.1 5.3 %collective-permute-start.20 = (bf16[96,256]{1,0:T(8,128)(2,1)S(1)}, bf16[96,256]{1,0:T(8,128)(2,1)S(1)}, u32[]{:S(2)}, u32[]{:S(2)}) collective-permute-start(bf16[96,256]{1,0:T(8,128)(2,1)S(1)} %shard_map.104.refs_1_), channel_id=1, source_target_pairs={{0,4},{1,5},{2,6},{3,7},{4,0},{5,1},{6,2},{7,3},{8,12},{9,13},{10,... | collective-permute-start | bytes 147464 | tf_op jit(solution)/shard_map/ppermute | solution.py:590
  51.1 5.4 %collective-permute-start.19 = (bf16[96,256]{1,0:T(8,128)(2,1)S(1)}, bf16[96,256]{1,0:T(8,128)(2,1)S(1)}, u32[]{:S(2)}, u32[]{:S(2)}) collective-permute-start(bf16[96,256]{1,0:T(8,128)(2,1)S(1)} %shard_map.104.refs_1_), channel_id=1, source_target_pairs={{0,2},{1,3},{2,0},{3,1},{4,6},{5,7},{6,4},{7,5},{8,10},{9,11},{10,... | collective-permute-start | bytes 147464 | tf_op jit(solution)/shard_map/ppermute | solution.py:590
  53.6 0.8 %copy-start = (s32[4]{0:T(128)S(1)}, s32[4]{0:T(128)}, u32[]{:S(2)}) copy-start(s32[4]{0:T(128)} %bins.1) | copy-start | bytes 52

commit v6 on v5

--- a/solution.py
+++ b/solution.py
@@ -233,7 +233,7 @@
 def chain_kernel(hops, *refs):
     own, other, top_refs = refs[:3], refs[3:6], refs[6:8]
     got_refs = refs[8 : 8 + 2 * hops]
-    grad_ref, d_ref, send_ref, g_now = refs[8 + 2 * hops :]
+    grad_ref, d_ref, send_ref, send_d, g_now = refs[8 + 2 * hops :]
     rows, wide = d_ref.shape[1], grad_ref.shape[1]
     pad = (wide - rows) // 2
     inner = slice(pad, pad + rows)
@@ -258,8 +258,8 @@
             mine, away = (first, second) if half else (second, first)
             grad_ref[j] = mine[0]
             d_ref[j] = mine[1][inner]
-            send_ref[j, :wide] = away[0]
-            send_ref[j, wide:] = away[1][inner]
+            send_ref[j] = away[0]
+            send_d[j] = away[1][inner]
 
     by_half(None, own, other, run)
 
@@ -310,8 +310,7 @@
     own_refs = refs[7 : 7 + PARTS]
     send_refs = refs[7 + PARTS : -2]
     total, sums = refs[-2:]
-    _, rows, _ = x_ref.shape
-    wide = got_ref.shape[1] - rows
+    wide = got_ref.shape[1]
     mine = lax.axis_index("bulk") // 2
     sums[...] = sums_in[...]
     add_terms(1, got_ref, wide, x_ref, pre_ref, pre_rim, gain_ref, total, sums, total_in)
@@ -359,11 +358,10 @@
 
 
 def result_kernel(d_mine, got_ref, out_ref, sems):
-    count, rows = d_mine.shape[:2]
+    count = d_mine.shape[0]
     half = lax.axis_index("section") % 2
-    away = got_ref.at[:, pl.ds(got_ref.shape[1] - rows, rows), :]
     pairs = [(d_mine, out_ref.at[pl.ds(half * count, count)])]
-    pairs.append((away, out_ref.at[pl.ds((1 - half) * count, count)]))
+    pairs.append((got_ref, out_ref.at[pl.ds((1 - half) * count, count)]))
     for copy in copies(pairs, sems):
         copy.wait()
 
@@ -536,12 +534,13 @@
         )
         outer_rows = down(outer_rows, pair)
         sources += [inner, outer_rows]
-    grad_own, d_own, away = call(
+    grad_own, d_own, away, away_d = call(
         functools.partial(chain_kernel, hops),
         [
             half_wide,
             shape_of((count, rows, channels), BF16),
-            shape_of((count, wide + rows, channels), BF16),
+            half_wide,
+            shape_of((count, rows, channels), BF16),
         ],
         tables + [cot, g_rim] + sources,
         scratch=[pltpu.VMEM(half_wide.shape, F32)],
@@ -549,6 +548,7 @@
         limit=12,
     )
     got_away = to_other(away)
+    got_d = to_other(away_d)
     shared = [x, pre, pre_rim, gain_rows]
     total_own, sums_own = call(
         own_kernel,
@@ -583,7 +583,7 @@
         compiler_params=pltpu.CompilerParams(vmem_limit_bytes=4 << 20),
         cost_estimate=cost(1, 1 << 20),
         name="results",
-    )(d_own, got_away)
+    )(d_own, got_d)
 
     def across(value, k):
         pairs = [(i, i ^ (2 * k)) for i in range(bulk_count)]

time: 57.4 us -> 57 us (level)
  waiting for transfers between devices: 19.9 us -> 19.1 us
    ppermute x4 -> x5, waiting for transfers between devices: 4.86 us -> 3.99 us  [to_other(): return lax.ppermute(value, 'section', [(i, i ^ 1) for i in range(sections)])]
    ppermute x4 -> x5, starting transfers between devices: 0.78 us -> 1.28 us  [to_other(): return lax.ppermute(value, 'section', [(i, i ^ 1) for i in range(sections)])]
  transfers between devices with their start and end apart: 22 -> 23, of which waited for: 9 -> 9; matrix products, arithmetic and copies ran while one was open for 0% -> 0% of each run, Pallas kernels for 6% -> 7%
where the time goes in v6:
time: 57 us; the launch traced here: 56.9 us
  starting transfers between devices  28.9 us (51%)
  waiting for transfers between devices  19.1 us (34%)
  Pallas kernels  8.17 us (14%)
  between operations  0.78 us (1%)
    ppermute x12, starting transfers between devices, across(): return lax.ppermute(value, 'bulk', pairs)  15.9 us
    ppermute x12, waiting for transfers between devices, across(): return lax.ppermute(value, 'bulk', pairs)  8.66 us
    pallas_call x13, Pallas kernels, call(): pl.pallas_call(kernel, in_specs=[smem] * len(scalars) + [kept] * len(remo...  5.76 us
    ppermute x2, starting transfers between devices, down(): lax.ppermute(value, 'section', pairs + [(low, high) for high, low in pairs])  4.55 us
    ppermute x5, waiting for transfers between devices, to_other(): return lax.ppermute(value, 'section', [(i, i ^ 1) for i in range(sections)])  3.99 us
    ppermute x1, starting transfers between devices, step(): far = lax.ppermute(far, 'bulk', opposite)  3.54 us
    ppermute x1, waiting for transfers between devices, step(): far = lax.ppermute(far, 'bulk', opposite)  3.24 us
    ppermute x2, waiting for transfers between devices, down(): lax.ppermute(value, 'section', pairs + [(low, high) for high, low in pairs])  3.15 us
  transfers between devices with their start and end apart: 23, of which 9 were waited for; matrix products, arithmetic and copies ran while one was open for 0% of the time, Pallas kernels for 7%

profile of v6, /device:TPU:0, one launch (start us, length us, event | category | flops | bytes accessed | tf_op | source)
XLA Modules:
  0.0 56.9 jit_solution(9132475845155833585)
XLA Ops:
  0.6 1.3 %shard_map.93 = (bf16[6,16,256]{2,1,0:T(8,128)(2,1)S(1)}, bf16[6,16,256]{2,1,0:T(8,128)(2,1)S(1)}, bf16[4,256,256]{2,1,0:T(8,128)(2,1)S(1)}, bf16[2,256,256]{2,1...) custom-call(s32[4]{0:T(128)} %bins.1, ...), custom_call_target="tpu_custom_call" | custom-call | flops 1 | bytes 1048576 | tf_op jit(solution)/shard_map/pallas_call | solution.py:421
  2.0 0.9 %shard_map.94 = (f32[2,256,256]{2,1,0:T(8,128)S(1)}, f32[2,256,256]{2,1,0:T(8,128)S(1)}, f32[4,256,256]{2,1,0:T(8,128)S(1)}) custom-call(bf16[4,256,256]{2,1,0:T(8,128)(2,1)S(1)} %get-tuple-element.34.x_ref.refs_0_, bf16[3,256,256]{2,1,0:T(8,128)(2,1)S(1)} %get-tuple-element.35.w_ref.refs_1_.refs_2_, f32[4,1,256]{2,1,0:T(1,128)S(1)} %get-tuple-element.36.gain_ref.refs_3_, ...), custom_call_target="tpu_custom_call" | custom-call | flops 452984832 | bytes 1048576 | tf_op jit(solution)/shard_map/pallas_call | solution.py:421
  2.9 0.6 collective-permute-start.2
  3.4 0.1 collective-permute-start.4
  3.5 2.0 %collective-permute-done.4.refs_3_.refs_5_ = bf16[3,256,256]{2,1,0:T(8,128)(2,1)S(1)} collective-permute-done((bf16[3,256,256]{2,1,0:T(8,128)(2,1)S(1)}, bf16[3,256,256]{2,1,0:T(8,128)(2,1)S(1)}, u32[]{:S(2)}, u32[]{:S(2)}) %collective-permute-start.4) | collective-permute-done | bytes 393248 | tf_op jit(solution)/shard_map/ppermute | solution.py:480
  5.5 0.0 collective-permute-done.2.refs_2_.refs_3_
  5.5 3.8 %collective-permute-start.5 = (bf16[2,240,256]{2,1,0:T(8,128)(2,1)S(1)}, bf16[2,240,256]{2,1,0:T(8,128)(2,1)S(1)}, u32[]{:S(2)}, u32[]{:S(2)}) collective-permute-start(bf16[2,240,256]{2,1,0:T(8,128)(2,1)S(1)} %shard_map.96), channel_id=1, source_target_pairs={{16,0},{24,8},{0,16},{8,24},{17,1},{25,9},{1,17},{9,25},{18,2},{26... | collective-permute-start | bytes 737288 | tf_op jit(solution)/shard_map/ppermute | solution.py:505
  9.3 1.5 %collective-permute-start = (bf16[6,16,256]{2,1,0:T(8,128)(2,1)S(1)}, bf16[6,16,256]{2,1,0:T(8,128)(2,1)S(1)}, u32[]{:S(2)}, u32[]{:S(2)}) collective-permute-start(bf16[6,16,256]{2,1,0:T(8,128)(2,1)S(1)} %get-tuple-element.39), channel_id=1, source_target_pairs={{0,1},{1,0},{2,3},{3,2},{4,5},{5,4},{6,7},{7,6},{8,9},{9,8},{10,11... | collective-permute-start | bytes 147464 | tf_op jit(solution)/shard_map/ppermute | solution.py:464
  10.9 3.5 %collective-permute-start.1 = (bf16[6,16,256]{2,1,0:T(8,128)(2,1)S(1)}, bf16[6,16,256]{2,1,0:T(8,128)(2,1)S(1)}, u32[]{:S(2)}, u32[]{:S(2)}) collective-permute-start(bf16[6,16,256]{2,1,0:T(8,128)(2,1)S(1)} %get-tuple-element.40), channel_id=1, source_target_pairs={{0,7},{1,2},{2,1},{3,4},{4,3},{5,6},{6,5},{7,0},{8,15},{9,10},{10,... | collective-permute-start | bytes 147464 | tf_op jit(solution)/shard_map/ppermute | solution.py:463
  14.4 0.0 collective-permute-done.near_ref
  14.4 3.2 %collective-permute-done.1.far_ref = bf16[6,16,256]{2,1,0:T(8,128)(2,1)S(1)} collective-permute-done((bf16[6,16,256]{2,1,0:T(8,128)(2,1)S(1)}, bf16[6,16,256]{2,1,0:T(8,128)(2,1)S(1)}, u32[]{:S(2)}, u32[]{:S(2)}) %collective-permute-start.1) | collective-permute-done | bytes 49184 | tf_op jit(solution)/shard_map/ppermute | solution.py:463
  17.6 0.3 shard_map.95
  18.0 0.1 collective-permute-start.3
  18.1 1.3 %collective-permute-done.3.refs_2_.refs_4_ = f32[2,2,32,256]{3,2,1,0:T(8,128)S(1)} collective-permute-done((f32[2,2,32,256]{3,2,1,0:T(8,128)S(1)}, f32[2,2,32,256]{3,2,1,0:T(8,128)S(1)}, u32[]{:S(2)}, u32[]{:S(2)}) %collective-permute-start.3) | collective-permute-done | bytes 131104 | tf_op jit(solution)/shard_map/ppermute | solution.py:480
  19.4 0.8 %collective-permute-start.6 = (bf16[2,2,16,256]{3,2,1,0:T(8,128)(2,1)S(1)}, bf16[2,2,16,256]{3,2,1,0:T(8,128)(2,1)S(1)}, u32[]{:S(2)}, u32[]{:S(2)}) collective-permute-start(bf16[2,2,16,256]{3,2,1,0:T(8,128)(2,1)S(1)} %shard_map.97), channel_id=1, source_target_pairs={{16,0},{24,8},{0,16},{8,24},{17,1},{25,9},{1,17},{9,25},{18,2},{26... | collective-permute-start | bytes 98312 | tf_op jit(solution)/shard_map/ppermute | solution.py:505
  20.2 3.1 %collective-permute-done.6.refs_9_ = bf16[2,2,16,256]{3,2,1,0:T(8,128)(2,1)S(1)} collective-permute-done((bf16[2,2,16,256]{3,2,1,0:T(8,128)(2,1)S(1)}, bf16[2,2,16,256]{3,2,1,0:T(8,128)(2,1)S(1)}, u32[]{:S(2)}, u32[]{:S(2)}) %collective-permute-start.6) | collective-permute-done | bytes 32800 | tf_op jit(solution)/shard_map/ppermute | solution.py:505
  23.3 0.0 collective-permute-done.5.refs_8_
  23.3 1.0 %shard_map.98 = (bf16[2,288,256]{2,1,0:T(8,128)(2,1)S(1)}, bf16[2,256,256]{2,1,0:T(8,128)(2,1)S(1)}, bf16[2,288,256]{2,1,0:T(8,128)(2,1)S(1)}, bf16[2,256,256]{2,1,0:T(8,128)(2,1)S(1)}) custom-call(f32[2,256,256]{2,1,0:T(8,128)S(1)} %get-tuple-element.38.refs_0_, f32[2,2,32,256]{3,2,1,0:T(8,128)S(1)} %get-tuple-element.41.refs_0_.refs_1_, ...), custom_call_target="tpu_custom_call" | custom-call | flops 452984832 | bytes 1048576 | tf_op jit(solution)/shard_map/pallas_call | solution.py:421
  24.3 0.1 collective-permute-start.8
  24.4 0.5 collective-permute-start.7
  24.9 0.4 shard_map.99
  25.3 0.6 %collective-permute-done.8.refs_6_ = bf16[2,288,256]{2,1,0:T(8,128)(2,1)S(1)} collective-permute-done((bf16[2,288,256]{2,1,0:T(8,128)(2,1)S(1)}, bf16[2,288,256]{2,1,0:T(8,128)(2,1)S(1)}, u32[]{:S(2)}, u32[]{:S(2)}) %collective-permute-start.8) | collective-permute-done | bytes 294944 | tf_op jit(solution)/shard_map/ppermute | solution.py:480
  25.9 0.5 shard_map.100
  26.4 0.9 %collective-permute-start.10 = (bf16[112,256]{1,0:T(8,128)(2,1)S(1)}, bf16[112,256]{1,0:T(8,128)(2,1)S(1)}, u32[]{:S(2)}, u32[]{:S(2)}) collective-permute-start(bf16[112,256]{1,0:T(8,128)(2,1)S(1)} %get-tuple-element.56), channel_id=1, source_target_pairs={{0,4},{1,5},{2,6},{3,7},{4,0},{5,1},{6,2},{7,3},{8,12},{9,13},{10,... | collective-permute-start | bytes 172040 | tf_op jit(solution)/shard_map/ppermute | solution.py:590
  27.3 1.3 %collective-permute-start.11 = (bf16[112,256]{1,0:T(8,128)(2,1)S(1)}, bf16[112,256]{1,0:T(8,128)(2,1)S(1)}, u32[]{:S(2)}, u32[]{:S(2)}) collective-permute-start(bf16[112,256]{1,0:T(8,128)(2,1)S(1)} %get-tuple-element.57), channel_id=1, source_target_pairs={{0,6},{1,7},{2,4},{3,5},{4,2},{5,3},{6,0},{7,1},{8,14},{9,15},{10,... | collective-permute-start | bytes 172040 | tf_op jit(solution)/shard_map/ppermute | solution.py:590
  28.6 1.4 %collective-permute-start.9 = (bf16[112,256]{1,0:T(8,128)(2,1)S(1)}, bf16[112,256]{1,0:T(8,128)(2,1)S(1)}, u32[]{:S(2)}, u32[]{:S(2)}) collective-permute-start(bf16[112,256]{1,0:T(8,128)(2,1)S(1)} %get-tuple-element.55.mine_ref), channel_id=1, source_target_pairs={{0,2},{1,3},{2,0},{3,1},{4,6},{5,7},{6,4},{7,5},{8,10},{9,11},{10,... | collective-permute-start | bytes 172040 | tf_op jit(solution)/shard_map/ppermute | solution.py:590
  30.0 3.5 %collective-permute-done.10.refs_1_ = bf16[112,256]{1,0:T(8,128)(2,1)S(1)} collective-permute-done((bf16[112,256]{1,0:T(8,128)(2,1)S(1)}, bf16[112,256]{1,0:T(8,128)(2,1)S(1)}, u32[]{:S(2)}, u32[]{:S(2)}) %collective-permute-start.10) | collective-permute-done | bytes 57376 | tf_op jit(solution)/shard_map/ppermute | solution.py:590
  33.5 0.0 collective-permute-done.11.refs_2_
  33.5 0.9 %collective-permute-done.9.refs_0_ = bf16[112,256]{1,0:T(8,128)(2,1)S(1)} collective-permute-done((bf16[112,256]{1,0:T(8,128)(2,1)S(1)}, bf16[112,256]{1,0:T(8,128)(2,1)S(1)}, u32[]{:S(2)}, u32[]{:S(2)}) %collective-permute-start.9) | collective-permute-done | bytes 57376 | tf_op jit(solution)/shard_map/ppermute | solution.py:590
  34.4 0.9 %collective-permute-start.12 = (bf16[112,256]{1,0:T(8,128)(2,1)S(1)}, bf16[112,256]{1,0:T(8,128)(2,1)S(1)}, u32[]{:S(2)}, u32[]{:S(2)}) collective-permute-start(bf16[112,256]{1,0:T(8,128)(2,1)S(1)} %shard_map.101.a_ref), channel_id=1, source_target_pairs={{0,1},{1,0},{2,3},{3,2},{4,5},{5,4},{6,7},{7,6},{8,9},{9,8},{10,11... | collective-permute-start | bytes 172040 | tf_op jit(solution)/shard_map/ppermute | solution.py:608
  35.3 1.9 %collective-permute-start.17 = (bf16[96,256]{1,0:T(8,128)(2,1)S(1)}, bf16[96,256]{1,0:T(8,128)(2,1)S(1)}, u32[]{:S(2)}, u32[]{:S(2)}) collective-permute-start(bf16[96,256]{1,0:T(8,128)(2,1)S(1)} %get-tuple-element.60), channel_id=1, source_target_pairs={{0,4},{1,5},{2,6},{3,7},{4,0},{5,1},{6,2},{7,3},{8,12},{9,13},{10,... | collective-permute-start | bytes 147464 | tf_op jit(solution)/shard_map/ppermute | solution.py:590
  37.1 1.2 %collective-permute-start.18 = (bf16[96,256]{1,0:T(8,128)(2,1)S(1)}, bf16[96,256]{1,0:T(8,128)(2,1)S(1)}, u32[]{:S(2)}, u32[]{:S(2)}) collective-permute-start(bf16[96,256]{1,0:T(8,128)(2,1)S(1)} %get-tuple-element.61), channel_id=1, source_target_pairs={{0,6},{1,7},{2,4},{3,5},{4,2},{5,3},{6,0},{7,1},{8,14},{9,15},{10,... | collective-permute-start | bytes 147464 | tf_op jit(solution)/shard_map/ppermute | solution.py:590
  38.3 0.4 collective-permute-start.16
  38.8 3.0 %collective-permute-done.17.refs_1_ = bf16[96,256]{1,0:T(8,128)(2,1)S(1)} collective-permute-done((bf16[96,256]{1,0:T(8,128)(2,1)S(1)}, bf16[96,256]{1,0:T(8,128)(2,1)S(1)}, u32[]{:S(2)}, u32[]{:S(2)}) %collective-permute-start.17) | collective-permute-done | bytes 49184 | tf_op jit(solution)/shard_map/ppermute | solution.py:590
  41.7 1.3 %collective-permute-done.18.refs_2_ = bf16[96,256]{1,0:T(8,128)(2,1)S(1)} collective-permute-done((bf16[96,256]{1,0:T(8,128)(2,1)S(1)}, bf16[96,256]{1,0:T(8,128)(2,1)S(1)}, u32[]{:S(2)}, u32[]{:S(2)}) %collective-permute-start.18) | collective-permute-done | bytes 49184 | tf_op jit(solution)/shard_map/ppermute | solution.py:590
  43.0 0.0 collective-permute-done.16.refs_0_
  43.1 1.2 %collective-permute-start.19 = (bf16[96,256]{1,0:T(8,128)(2,1)S(1)}, bf16[96,256]{1,0:T(8,128)(2,1)S(1)}, u32[]{:S(2)}, u32[]{:S(2)}) collective-permute-start(bf16[96,256]{1,0:T(8,128)(2,1)S(1)} %shard_map.103.a_ref), channel_id=1, source_target_pairs={{0,1},{1,0},{2,3},{3,2},{4,5},{5,4},{6,7},{7,6},{8,9},{9,8},{10,11... | collective-permute-start | bytes 147464 | tf_op jit(solution)/shard_map/ppermute | solution.py:608
  44.2 0.0 collective-permute-done.12.b_ref
  44.3 2.0 %collective-permute-start.15 = (bf16[96,256]{1,0:T(8,128)(2,1)S(1)}, bf16[96,256]{1,0:T(8,128)(2,1)S(1)}, u32[]{:S(2)}, u32[]{:S(2)}) collective-permute-start(bf16[96,256]{1,0:T(8,128)(2,1)S(1)} %shard_map.102.refs_0_), channel_id=1, source_target_pairs={{0,6},{1,7},{2,4},{3,5},{4,2},{5,3},{6,0},{7,1},{8,14},{9,15},{10,... | collective-permute-start | bytes 147464 | tf_op jit(solution)/shard_map/ppermute | solution.py:590
  46.2 0.0 collective-permute-start.14
  46.2 2.5 %collective-permute-start.13 = (bf16[96,256]{1,0:T(8,128)(2,1)S(1)}, bf16[96,256]{1,0:T(8,128)(2,1)S(1)}, u32[]{:S(2)}, u32[]{:S(2)}) collective-permute-start(bf16[96,256]{1,0:T(8,128)(2,1)S(1)} %shard_map.102.refs_0_), channel_id=1, source_target_pairs={{0,2},{1,3},{2,0},{3,1},{4,6},{5,7},{6,4},{7,5},{8,10},{9,11},{10,... | collective-permute-start | bytes 147464 | tf_op jit(solution)/shard_map/ppermute | solution.py:590
  48.7 0.0 collective-permute-done.19.b_ref
  48.7 2.0 %collective-permute-start.22 = (bf16[96,256]{1,0:T(8,128)(2,1)S(1)}, bf16[96,256]{1,0:T(8,128)(2,1)S(1)}, u32[]{:S(2)}, u32[]{:S(2)}) collective-permute-start(bf16[96,256]{1,0:T(8,128)(2,1)S(1)} %shard_map.104.refs_1_), channel_id=1, source_target_pairs={{0,6},{1,7},{2,4},{3,5},{4,2},{5,3},{6,0},{7,1},{8,14},{9,15},{10,... | collective-permute-start | bytes 147464 | tf_op jit(solution)/shard_map/ppermute | solution.py:590
  50.7 0.0 collective-permute-done.7.got_ref
  50.7 0.0 collective-permute-start.21
  50.7 0.0 collective-permute-done.15.refs_3_
  50.7 2.5 %collective-permute-start.20 = (bf16[96,256]{1,0:T(8,128)(2,1)S(1)}, bf16[96,256]{1,0:T(8,128)(2,1)S(1)}, u32[]{:S(2)}, u32[]{:S(2)}) collective-permute-start(bf16[96,256]{1,0:T(8,128)(2,1)S(1)} %shard_map.104.refs_1_), channel_id=1, source_target_pairs={{0,2},{1,3},{2,0},{3,1},{4,6},{5,7},{6,4},{7,5},{8,10},{9,11},{10,... | collective-permute-start | bytes 147464 | tf_op jit(solution)/shard_map/ppermute | solution.py:590
  53.2 0.0 copy-start
  53.2 0.8 %results.1 = bf16[4,256,256]{2,1,0:T(8,128)(2,1)} custom-call(bf16[2,256,256]{2,1,0:T(8,128)(2,1)S(1)} %get-tuple-element.46.d_mine, bf16[2,256,256]{2,1,0:T(8,128)(2,1)S(1)} %collective-permute-done.7.got_ref), custom_call_target="tpu_custom_call" | custom-call | flops 1 | bytes 1048576 | tf_op jit(solution)/shard_map/results/pallas_call | solution.py:577
  54.0 0.0 copy-done
  54.0 1.2 %shard_map.105 = (f32[36,1,256]{2,1,0:T(1,128)}, f32[36,1,256]{2,1,0:T(1,128)}) custom-call(s32[4]{0:T(128)S(1)} %copy-done, bf16[112,256]{1,0:T(8,128)(2,1)S(1)} %shard_map.101.a_ref, bf16[112,256]{1,0:T(8,128)(2,1)S(1)} %collective-permute-done.12.b_ref), custom_call_target="tpu_custom_call" | custom-call | flops 1 | bytes 1048576 | tf_op jit(solution)/shard_map/pallas_call | solution.py:421
  55.2 0.0 collective-permute-done.14.refs_2_
  55.2 0.0 collective-permute-done.13.refs_1_
  55.2 0.8 %spread.2.refs_0_ = f32[768,256]{1,0:T(8,128)} custom-call(bf16[96,256]{1,0:T(8,128)(2,1)S(1)} %shard_map.102.refs_0_, bf16[96,256]{1,0:T(8,128)(2,1)S(1)} %collective-permute-done.13.refs_1_, bf16[96,256]{1,0:T(8,128)(2,1)S(1)} %collective-permute-done.14.refs_2_, bf16[96,256]{1,0:T(8,128)(2,1)S(1)} %collective-permute-done.15.refs_3_), custom_call_target="tpu_custom_call" | custom-call | flops 1 | bytes 1048576 | tf_op jit(solution)/shard_map/spread/pallas_call | solution.py:396
  56.0 0.0 collective-permute-done.22.refs_4_
  56.1 0.0 collective-permute-done.21.refs_3_
  56.1 0.0 collective-permute-done.20.refs_2_
  56.1 0.8 %spread.3 = f32[768,256]{1,0:T(8,128)} custom-call(f32[768,256]{1,0:T(8,128)} %spread.2.refs_0_, bf16[96,256]{1,0:T(8,128)(2,1)S(1)} %shard_map.104.refs_1_, bf16[96,256]{1,0:T(8,128)(2,1)S(1)} %collective-permute-done.20.refs_2_, bf16[96,256]{1,0:T(8,128)(2,1)S(1)} %collective-permute-done.21.refs_3_, ...), custom_call_target="tpu_custom_call", output_to_operand_aliasing={{}: (0, {})} | custom-call | flops 1 | bytes 1048576 | tf_op jit(solution)/shard_map/spread/pallas_call | solution.py:396
  (6 shorter events, 0.1 us)
Async XLA Ops:
  2.9 2.7 %collective-permute-start.2 = (f32[2,256,256]{2,1,0:T(8,128)S(1)}, f32[2,256,256]{2,1,0:T(8,128)S(1)}, u32[]{:S(2)}, u32[]{:S(2)}) collective-permute-start(f32[2,256,256]{2,1,0:T(8,128)S(1)} %get-tuple-element.42), channel_id=1, source_target_pairs={{0,8},{8,0},{16,24},{24,16},{1,9},{9,1},{17,25},{25,17},{2,10},{10... | collective-permute-start | bytes 1572872 | tf_op jit(solution)/shard_map/ppermute | solution.py:480
  3.4 2.1 %collective-permute-start.4 = (bf16[3,256,256]{2,1,0:T(8,128)(2,1)S(1)}, bf16[3,256,256]{2,1,0:T(8,128)(2,1)S(1)}, u32[]{:S(2)}, u32[]{:S(2)}) collective-permute-start(bf16[3,256,256]{2,1,0:T(8,128)(2,1)S(1)} %get-tuple-element.35.w_ref.refs_1_.refs_2_), channel_id=1, source_target_pairs={{0,8},{8,0},{16,24},{24,16},{1,9},{9,1},{17,25},{25,17},{2,10},{10... | collective-permute-start | bytes 1179656 | tf_op jit(solution)/shard_map/ppermute | solution.py:480
  5.5 17.8 %collective-permute-start.5 = (bf16[2,240,256]{2,1,0:T(8,128)(2,1)S(1)}, bf16[2,240,256]{2,1,0:T(8,128)(2,1)S(1)}, u32[]{:S(2)}, u32[]{:S(2)}) collective-permute-start(bf16[2,240,256]{2,1,0:T(8,128)(2,1)S(1)} %shard_map.96), channel_id=1, source_target_pairs={{16,0},{24,8},{0,16},{8,24},{17,1},{25,9},{1,17},{9,25},{18,2},{26... | collective-permute-start | bytes 737288 | tf_op jit(solution)/shard_map/ppermute | solution.py:505
  9.3 5.1 %collective-permute-start = (bf16[6,16,256]{2,1,0:T(8,128)(2,1)S(1)}, bf16[6,16,256]{2,1,0:T(8,128)(2,1)S(1)}, u32[]{:S(2)}, u32[]{:S(2)}) collective-permute-start(bf16[6,16,256]{2,1,0:T(8,128)(2,1)S(1)} %get-tuple-element.39), channel_id=1, source_target_pairs={{0,1},{1,0},{2,3},{3,2},{4,5},{5,4},{6,7},{7,6},{8,9},{9,8},{10,11... | collective-permute-start | bytes 147464 | tf_op jit(solution)/shard_map/ppermute | solution.py:464
  10.9 6.8 %collective-permute-start.1 = (bf16[6,16,256]{2,1,0:T(8,128)(2,1)S(1)}, bf16[6,16,256]{2,1,0:T(8,128)(2,1)S(1)}, u32[]{:S(2)}, u32[]{:S(2)}) collective-permute-start(bf16[6,16,256]{2,1,0:T(8,128)(2,1)S(1)} %get-tuple-element.40), channel_id=1, source_target_pairs={{0,7},{1,2},{2,1},{3,4},{4,3},{5,6},{6,5},{7,0},{8,15},{9,10},{10,... | collective-permute-start | bytes 147464 | tf_op jit(solution)/shard_map/ppermute | solution.py:463
  18.0 1.4 %collective-permute-start.3 = (f32[2,2,32,256]{3,2,1,0:T(8,128)S(1)}, f32[2,2,32,256]{3,2,1,0:T(8,128)S(1)}, u32[]{:S(2)}, u32[]{:S(2)}) collective-permute-start(f32[2,2,32,256]{3,2,1,0:T(8,128)S(1)} %get-tuple-element.43), channel_id=1, source_target_pairs={{0,8},{8,0},{16,24},{24,16},{1,9},{9,1},{17,25},{25,17},{2,10},{10... | collective-permute-start | bytes 393224 | tf_op jit(solution)/shard_map/ppermute | solution.py:480
  19.4 3.9 %collective-permute-start.6 = (bf16[2,2,16,256]{3,2,1,0:T(8,128)(2,1)S(1)}, bf16[2,2,16,256]{3,2,1,0:T(8,128)(2,1)S(1)}, u32[]{:S(2)}, u32[]{:S(2)}) collective-permute-start(bf16[2,2,16,256]{3,2,1,0:T(8,128)(2,1)S(1)} %shard_map.97), channel_id=1, source_target_pairs={{16,0},{24,8},{0,16},{8,24},{17,1},{25,9},{1,17},{9,25},{18,2},{26... | collective-permute-start | bytes 98312 | tf_op jit(solution)/shard_map/ppermute | solution.py:505
  24.3 1.6 %collective-permute-start.8 = (bf16[2,288,256]{2,1,0:T(8,128)(2,1)S(1)}, bf16[2,288,256]{2,1,0:T(8,128)(2,1)S(1)}, u32[]{:S(2)}, u32[]{:S(2)}) collective-permute-start(bf16[2,288,256]{2,1,0:T(8,128)(2,1)S(1)} %get-tuple-element.53), channel_id=1, source_target_pairs={{0,8},{8,0},{16,24},{24,16},{1,9},{9,1},{17,25},{25,17},{2,10},{10... | collective-permute-start | bytes 884744 | tf_op jit(solution)/shard_map/ppermute | solution.py:480
  24.4 26.3 %collective-permute-start.7 = (bf16[2,256,256]{2,1,0:T(8,128)(2,1)S(1)}, bf16[2,256,256]{2,1,0:T(8,128)(2,1)S(1)}, u32[]{:S(2)}, u32[]{:S(2)}) collective-permute-start(bf16[2,256,256]{2,1,0:T(8,128)(2,1)S(1)} %get-tuple-element.47), channel_id=1, source_target_pairs={{0,8},{8,0},{16,24},{24,16},{1,9},{9,1},{17,25},{25,17},{2,10},{10... | collective-permute-start | bytes 786440 | tf_op jit(solution)/shard_map/ppermute | solution.py:480
  26.4 7.0 %collective-permute-start.10 = (bf16[112,256]{1,0:T(8,128)(2,1)S(1)}, bf16[112,256]{1,0:T(8,128)(2,1)S(1)}, u32[]{:S(2)}, u32[]{:S(2)}) collective-permute-start(bf16[112,256]{1,0:T(8,128)(2,1)S(1)} %get-tuple-element.56), channel_id=1, source_target_pairs={{0,4},{1,5},{2,6},{3,7},{4,0},{5,1},{6,2},{7,3},{8,12},{9,13},{10,... | collective-permute-start | bytes 172040 | tf_op jit(solution)/shard_map/ppermute | solution.py:590
  27.3 6.2 %collective-permute-start.11 = (bf16[112,256]{1,0:T(8,128)(2,1)S(1)}, bf16[112,256]{1,0:T(8,128)(2,1)S(1)}, u32[]{:S(2)}, u32[]{:S(2)}) collective-permute-start(bf16[112,256]{1,0:T(8,128)(2,1)S(1)} %get-tuple-element.57), channel_id=1, source_target_pairs={{0,6},{1,7},{2,4},{3,5},{4,2},{5,3},{6,0},{7,1},{8,14},{9,15},{10,... | collective-permute-start | bytes 172040 | tf_op jit(solution)/shard_map/ppermute | solution.py:590
  28.6 5.7 %collective-permute-start.9 = (bf16[112,256]{1,0:T(8,128)(2,1)S(1)}, bf16[112,256]{1,0:T(8,128)(2,1)S(1)}, u32[]{:S(2)}, u32[]{:S(2)}) collective-permute-start(bf16[112,256]{1,0:T(8,128)(2,1)S(1)} %get-tuple-element.55.mine_ref), channel_id=1, source_target_pairs={{0,2},{1,3},{2,0},{3,1},{4,6},{5,7},{6,4},{7,5},{8,10},{9,11},{10,... | collective-permute-start | bytes 172040 | tf_op jit(solution)/shard_map/ppermute | solution.py:590
  34.4 9.8 %collective-permute-start.12 = (bf16[112,256]{1,0:T(8,128)(2,1)S(1)}, bf16[112,256]{1,0:T(8,128)(2,1)S(1)}, u32[]{:S(2)}, u32[]{:S(2)}) collective-permute-start(bf16[112,256]{1,0:T(8,128)(2,1)S(1)} %shard_map.101.a_ref), channel_id=1, source_target_pairs={{0,1},{1,0},{2,3},{3,2},{4,5},{5,4},{6,7},{7,6},{8,9},{9,8},{10,11... | collective-permute-start | bytes 172040 | tf_op jit(solution)/shard_map/ppermute | solution.py:608
  35.3 6.5 %collective-permute-start.17 = (bf16[96,256]{1,0:T(8,128)(2,1)S(1)}, bf16[96,256]{1,0:T(8,128)(2,1)S(1)}, u32[]{:S(2)}, u32[]{:S(2)}) collective-permute-start(bf16[96,256]{1,0:T(8,128)(2,1)S(1)} %get-tuple-element.60), channel_id=1, source_target_pairs={{0,4},{1,5},{2,6},{3,7},{4,0},{5,1},{6,2},{7,3},{8,12},{9,13},{10,... | collective-permute-start | bytes 147464 | tf_op jit(solution)/shard_map/ppermute | solution.py:590
  37.1 5.9 %collective-permute-start.18 = (bf16[96,256]{1,0:T(8,128)(2,1)S(1)}, bf16[96,256]{1,0:T(8,128)(2,1)S(1)}, u32[]{:S(2)}, u32[]{:S(2)}) collective-permute-start(bf16[96,256]{1,0:T(8,128)(2,1)S(1)} %get-tuple-element.61), channel_id=1, source_target_pairs={{0,6},{1,7},{2,4},{3,5},{4,2},{5,3},{6,0},{7,1},{8,14},{9,15},{10,... | collective-permute-start | bytes 147464 | tf_op jit(solution)/shard_map/ppermute | solution.py:590
  38.3 4.7 %collective-permute-start.16 = (bf16[96,256]{1,0:T(8,128)(2,1)S(1)}, bf16[96,256]{1,0:T(8,128)(2,1)S(1)}, u32[]{:S(2)}, u32[]{:S(2)}) collective-permute-start(bf16[96,256]{1,0:T(8,128)(2,1)S(1)} %get-tuple-element.59.mine_ref), channel_id=1, source_target_pairs={{0,2},{1,3},{2,0},{3,1},{4,6},{5,7},{6,4},{7,5},{8,10},{9,11},{10,... | collective-permute-start | bytes 147464 | tf_op jit(solution)/shard_map/ppermute | solution.py:590
  43.1 5.7 %collective-permute-start.19 = (bf16[96,256]{1,0:T(8,128)(2,1)S(1)}, bf16[96,256]{1,0:T(8,128)(2,1)S(1)}, u32[]{:S(2)}, u32[]{:S(2)}) collective-permute-start(bf16[96,256]{1,0:T(8,128)(2,1)S(1)} %shard_map.103.a_ref), channel_id=1, source_target_pairs={{0,1},{1,0},{2,3},{3,2},{4,5},{5,4},{6,7},{7,6},{8,9},{9,8},{10,11... | collective-permute-start | bytes 147464 | tf_op jit(solution)/shard_map/ppermute | solution.py:608
  44.3 6.4 %collective-permute-start.15 = (bf16[96,256]{1,0:T(8,128)(2,1)S(1)}, bf16[96,256]{1,0:T(8,128)(2,1)S(1)}, u32[]{:S(2)}, u32[]{:S(2)}) collective-permute-start(bf16[96,256]{1,0:T(8,128)(2,1)S(1)} %shard_map.102.refs_0_), channel_id=1, source_target_pairs={{0,6},{1,7},{2,4},{3,5},{4,2},{5,3},{6,0},{7,1},{8,14},{9,15},{10,... | collective-permute-start | bytes 147464 | tf_op jit(solution)/shard_map/ppermute | solution.py:590
  46.2 9.0 %collective-permute-start.14 = (bf16[96,256]{1,0:T(8,128)(2,1)S(1)}, bf16[96,256]{1,0:T(8,128)(2,1)S(1)}, u32[]{:S(2)}, u32[]{:S(2)}) collective-permute-start(bf16[96,256]{1,0:T(8,128)(2,1)S(1)} %shard_map.102.refs_0_), channel_id=1, source_target_pairs={{0,4},{1,5},{2,6},{3,7},{4,0},{5,1},{6,2},{7,3},{8,12},{9,13},{10,... | collective-permute-start | bytes 147464 | tf_op jit(solution)/shard_map/ppermute | solution.py:590
  46.2 9.0 %collective-permute-start.13 = (bf16[96,256]{1,0:T(8,128)(2,1)S(1)}, bf16[96,256]{1,0:T(8,128)(2,1)S(1)}, u32[]{:S(2)}, u32[]{:S(2)}) collective-permute-start(bf16[96,256]{1,0:T(8,128)(2,1)S(1)} %shard_map.102.refs_0_), channel_id=1, source_target_pairs={{0,2},{1,3},{2,0},{3,1},{4,6},{5,7},{6,4},{7,5},{8,10},{9,11},{10,... | collective-permute-start | bytes 147464 | tf_op jit(solution)/shard_map/ppermute | solution.py:590
  48.7 7.3 %collective-permute-start.22 = (bf16[96,256]{1,0:T(8,128)(2,1)S(1)}, bf16[96,256]{1,0:T(8,128)(2,1)S(1)}, u32[]{:S(2)}, u32[]{:S(2)}) collective-permute-start(bf16[96,256]{1,0:T(8,128)(2,1)S(1)} %shard_map.104.refs_1_), channel_id=1, source_target_pairs={{0,6},{1,7},{2,4},{3,5},{4,2},{5,3},{6,0},{7,1},{8,14},{9,15},{10,... | collective-permute-start | bytes 147464 | tf_op jit(solution)/shard_map/ppermute | solution.py:590
  50.7 5.3 %collective-permute-start.21 = (bf16[96,256]{1,0:T(8,128)(2,1)S(1)}, bf16[96,256]{1,0:T(8,128)(2,1)S(1)}, u32[]{:S(2)}, u32[]{:S(2)}) collective-permute-start(bf16[96,256]{1,0:T(8,128)(2,1)S(1)} %shard_map.104.refs_1_), channel_id=1, source_target_pairs={{0,4},{1,5},{2,6},{3,7},{4,0},{5,1},{6,2},{7,3},{8,12},{9,13},{10,... | collective-permute-start | bytes 147464 | tf_op jit(solution)/shard_map/ppermute | solution.py:590
  50.7 5.3 %collective-permute-start.20 = (bf16[96,256]{1,0:T(8,128)(2,1)S(1)}, bf16[96,256]{1,0:T(8,128)(2,1)S(1)}, u32[]{:S(2)}, u32[]{:S(2)}) collective-permute-start(bf16[96,256]{1,0:T(8,128)(2,1)S(1)} %shard_map.104.refs_1_), channel_id=1, source_target_pairs={{0,2},{1,3},{2,0},{3,1},{4,6},{5,7},{6,4},{7,5},{8,10},{9,11},{10,... | collective-permute-start | bytes 147464 | tf_op jit(solution)/shard_map/ppermute | solution.py:590
  53.2 0.8 %copy-start = (s32[4]{0:T(128)S(1)}, s32[4]{0:T(128)}, u32[]{:S(2)}) copy-start(s32[4]{0:T(128)} %bins.1) | copy-start | bytes 52
